TPU v7x, 32 devices: a whole 2x2x4 slice. The times are simulated.
32 devices in a mesh: rep: 4 (over y, x), shard: 8 (over z, core).
Axes of the slice: x: 2, y: 2, z: 4, core: 2. Of those that a mesh axis runs over, the one named last changes fastest.
Arguments:
- tokens: bfloat16 [32768, 768], P(('rep', 'shard')), may hold values from -6 to 6
- cotangent: bfloat16 [32768, 768], P(('rep', 'shard')), may hold values from -6 to 6
- qkv_weight: bfloat16 [768, 2304], P('shard'), may hold values from -0.21875 to 0.21875
- query_value_bias: bfloat16 [2, 768], P(None, 'shard'), may hold values from -3 to 3
- out_weight: bfloat16 [768, 768], P('shard'), may hold values from -0.875 to 0.875
- out_bias: bfloat16 [768], P('shard'), may hold values from -2 to 2
- norm_one_gain: bfloat16 [768], P('shard'), may hold values from 0.099609375 to 1.8984375
- norm_one_shift: bfloat16 [768], P('shard'), may hold values from -2 to 2
- up_weight: bfloat16 [768, 3072], P('shard'), may hold values from -0.21875 to 0.21875
- up_bias: bfloat16 [3072], P('shard'), may hold values from -3 to 3
- down_weight: bfloat16 [3072, 768], P('shard'), may hold values from -0.109375 to 0.109375
- down_bias: bfloat16 [768], P('shard'), may hold values from -2 to 2
- norm_two_gain: bfloat16 [768], P('shard'), may hold values from 0.099609375 to 1.8984375
- norm_two_shift: bfloat16 [768], P('shard'), may hold values from -2 to 2
- segment_ids: int32 [64, 512], P(('rep', 'shard')), may hold values from 0 to 7, never falling along the last dimension, each value on 1 to 256 neighbouring positions
- valid: int32 [64, 512], P(('rep', 'shard')), may hold values from 0 to 1, as said below
Outputs:
- layer_output: bfloat16 [32768, 768], P(('rep', 'shard'))
- input_grad: bfloat16 [32768, 768], P(('rep', 'shard'))
- grad_qkv_weight: float32 [768, 2304], P('shard')
- grad_query_value_bias: float32 [2, 768], P(None, 'shard')
- grad_out_weight: float32 [768, 768], P('shard')
- grad_out_bias: float32 [768], P('shard')
- grad_norm_one_gain: float32 [768], P('shard')
- grad_norm_one_shift: float32 [768], P('shard')
- grad_up_weight: float32 [768, 3072], P('shard')
- grad_up_bias: float32 [3072], P('shard')
- grad_down_weight: float32 [3072, 768], P('shard')
- grad_down_bias: float32 [768], P('shard')
- grad_norm_two_gain: float32 [768], P('shard')
- grad_norm_two_shift: float32 [768], P('shard')
Inputs may be any that keep to these rules, and one draw needn't show every extreme that they name: `segment_ids`: within each sequence of 512 positions the numbers never fall; a document covers 1 to 256 positions, and one covers exactly 256. `valid`: in each sequence of 512 positions the tokens come first, followed by 0 to 64 padding positions.
All inputs are finite; a program needn't handle non-finite values.
Results may differ from a plain program's by a relative error of at most 0.015.
Values may be sent and summed in bfloat16 or wider, within the bound.
No kernel may reach another device: no remote copies, remote signals or barrier semaphores. Data moves between devices by JAX's collectives and lax.ppermute only.
A program may use at most 192 MiB of HBM per device.

v0:
```python
import functools

import jax
import jax.numpy as jnp
from jax import lax
from jax.experimental import pallas as pl
from jax.experimental.pallas import tpu as pltpu
from jax.sharding import PartitionSpec as P

HD = 64
GW = 256
SCALE = 0.125 * 1.4426950408889634
BIG = 1e30
VMEM_LIMIT = 60 * 1024 * 1024
bf16 = jnp.bfloat16
f32 = jnp.float32
SMEM = pl.BlockSpec(memory_space=pltpu.SMEM)
VMEM = pl.BlockSpec(memory_space=pltpu.VMEM)


def nn(a, b):
    return lax.dot_general(a, b, (((1,), (0,)), ((), ())), preferred_element_type=f32)


def nt(a, b):
    return lax.dot_general(a, b, (((1,), (1,)), ((), ())), preferred_element_type=f32)


def tn(a, b):
    return lax.dot_general(a, b, (((0,), (0,)), ((), ())), preferred_element_type=f32)


def params(**more):
    return pltpu.CompilerParams(vmem_limit_bytes=VMEM_LIMIT, **more)


def cost(flops, moved):
    return pl.CostEstimate(flops=flops, bytes_accessed=moved, transcendentals=0)


def attend_kernel(tok, wq, wk, wv, vecs, aq, ak, q_o, k_o, v_o, ctx_o, lse_o):
    x = tok[...]
    q = (nn(x, wq[...]) + vecs[0:1, :].astype(f32)).astype(bf16)
    k = nn(x, wk[...]).astype(bf16)
    v = (nn(x, wv[...]) + vecs[1:2, :].astype(f32)).astype(bf16)
    q_o[...] = q
    k_o[...] = k
    v_o[...] = v
    length, width = q.shape
    lane = lax.broadcasted_iota(jnp.int32, (length, width), 1) // HD
    slot = lax.broadcasted_iota(jnp.int32, (length, 128), 1)
    acc = None
    scale = jnp.zeros((length, width), f32)
    stat = jnp.zeros((length, 128), f32)
    for h in range(width // HD):
        mine = lane == h
        qa = jnp.where(mine, q, aq[...])
        ka = jnp.where(mine, k, ak[...])
        va = jnp.where(mine, v, jnp.zeros_like(v))
        t = nt(qa, ka) * SCALE
        m = jnp.max(t, axis=1, keepdims=True)
        p = jnp.exp2(t - m)
        total = jnp.sum(p, axis=1, keepdims=True)
        part = nn(p.astype(bf16), va)
        acc = part if acc is None else acc + part
        scale = jnp.where(mine, 1.0 / total, scale)
        stat = jnp.where(slot == h, m + jnp.log2(total), stat)
    ctx_o[...] = (acc * scale).astype(bf16)
    lse_o[0] = stat.T[:8]


def attend(g, tokens, w, vecs, aq, ak, length):
    rows, width = tokens.shape
    groups = width // GW
    seqs = rows // length
    col = lambda o: pl.BlockSpec((width, GW), lambda b: (0, o * groups + g))
    seq = pl.BlockSpec((length, width), lambda b: (b, 0))
    blk = pl.BlockSpec((length, GW), lambda b: (b, 0))
    act = jax.ShapeDtypeStruct((rows, GW), bf16)
    return pl.pallas_call(
        attend_kernel,
        grid=(seqs,),
        in_specs=[seq, col(0), col(1), col(2), pl.BlockSpec((16, GW), lambda b: (0, g)), blk, blk],
        out_specs=[blk, blk, blk, blk, pl.BlockSpec((1, 8, length), lambda b: (b, 0, 0))],
        out_shape=[act, act, act, act, jax.ShapeDtypeStruct((seqs, 8, length), f32)],
        compiler_params=params(),
        cost_estimate=cost(4_000_000_000, 5_000_000),
        name="attend",
    )(tokens, w, w, w, vecs, aq, ak)


def owner_of(s, at_r):
    return lax.rem(s // 2 - at_r[2] + 4, 4), at_r[3] != s % 2


def select_lanes(s, piece, width):
    i = lax.broadcasted_iota(jnp.int32, (128, width), 0)
    j = lax.broadcasted_iota(jnp.int32, (128, width), 1)
    return ((j == s * piece + i) & (i < piece)).astype(f32).astype(bf16)


def attend_back_kernel(mode, at_r, q_r, k_r, v_r, do_r, ctx_r, lse_r, aq, ak, tok, wq, wk, wv, dx_i, *rest):
    b = pl.program_id(0)
    last = b == pl.num_programs(0) - 1
    if mode == "plain":
        dw_o, dx_o, db_o, dw_s = rest
    elif mode == "first":
        own_o, other_o, dx_o, db_o, dw_s = rest
    elif mode == "second":
        _, _, own_o, other_o, dx_o, db_o, dw_s = rest
    else:
        db0, db1, tbl, own_o, other_o, dx_o, db_o, dw_s = rest
    q, k, v, do = q_r[...], k_r[...], v_r[...], do_r[...]
    length, width = q.shape
    lane = lax.broadcasted_iota(jnp.int32, (length, width), 1) // HD
    sel = lax.broadcasted_iota(jnp.int32, (8, width), 1) // HD == lax.broadcasted_iota(jnp.int32, (8, width), 0)
    sel = sel.astype(f32).astype(bf16)
    prod = do.astype(f32) * ctx_r[...].astype(f32)
    hi = prod.astype(bf16)
    lo = (prod - hi.astype(f32)).astype(bf16)
    delta = nt(sel, hi) + nt(sel, lo)
    dq = dk = dv = None
    zero = jnp.zeros_like(q)
    for h in range(width // HD):
        mine = lane == h
        qa = jnp.where(mine, q, aq[...])
        ka = jnp.where(mine, k, ak[...])
        va = jnp.where(mine, v, zero)
        p = jnp.exp2(nt(ka, qa) * SCALE - lse_r[0, h : h + 1, :])
        dp = nt(va, do)
        ds = (p * (dp - delta[h : h + 1, :])).astype(bf16)
        dv_h = nn(p.astype(bf16), jnp.where(mine, do, zero))
        dk_h = nn(ds, jnp.where(mine, q, zero))
        dq_h = tn(ds, jnp.where(mine, k, zero))
        dv = dv_h if dv is None else dv + dv_h
        dk = dk_h if dk is None else dk + dk_h
        dq = dq_h if dq is None else dq + dq_h
    dq = (dq * 0.125).astype(bf16)
    dk = (dk * 0.125).astype(bf16)
    dv = dv.astype(bf16)
    back = jnp.concatenate([dq, dk, dv], axis=1)
    dw = tn(tok[...], back)
    dx = nt(dq, wq[...]) + nt(dk, wk[...]) + nt(dv, wv[...])
    dx_o[...] = (dx_i[...].astype(f32) + dx).astype(dx_o.dtype)
    sums = jnp.sum(back.astype(f32), axis=0, keepdims=True)

    @pl.when(b == 0)
    def _():
        dw_s[...] = dw
        db_o[...] = sums

    @pl.when(b > 0)
    def _():
        dw_s[...] += dw
        db_o[...] += sums

    @pl.when(last)
    def _():
        if mode == "plain":
            for i in range(3):
                dw_o[i] = dw_s[:, i * width : (i + 1) * width].astype(bf16)
            return
        res = dw_s[...].astype(bf16)
        piece = res.shape[0] // 8
        half, wide = piece // 2, res.shape[1] // 2
        for s in range(8):
            kk, far = owner_of(s, at_r)
            for ab, turn in ((0, at_r[1]), (1, at_r[0])):
                for h in range(2):
                    val = res[s * piece + ab * half : s * piece + (ab + 1) * half, h * wide : (h + 1) * wide]
                    rel = lax.rem(h + turn, 2)
                    for ref, cond in ((other_o, far), (own_o, ~far)):

                        @pl.when(cond)
                        def _(val=val, rel=rel, kk=kk, ab=ab, ref=ref):
                            ref[ab, rel, kk, 0:half] = val

        if mode == "third":
            sums = [r[...] for r in (db0, db1, db_o)]
            dbq = jnp.concatenate([r[:, :width] for r in sums], axis=1)
            dbv = jnp.concatenate([r[:, 2 * width :] for r in sums], axis=1)
            table = jnp.concatenate([dbq, dbv, tbl[...]], axis=0).astype(bf16)
            extra = jnp.zeros((4, 16, wide), bf16)
            for ab in range(2):
                for h in range(2):
                    own_o[ab, h, :, half : half + 16, :] = extra
                    other_o[ab, h, :, half : half + 16, :] = extra
            for s in range(8):
                blk = nt(table, select_lanes(s, piece, table.shape[1])).astype(bf16)
                kk, far = owner_of(s, at_r)
                for ref, cond in ((other_o, far), (own_o, ~far)):

                    @pl.when(cond)
                    def _(blk=blk, kk=kk, ref=ref):
                        ref[0, at_r[1], kk, half : half + 16, 0:128] = blk


def attend_back(mode, g, at, saved, gc, aq, ak, tokens, w, dx, length, extra=()):
    rows, width = tokens.shape
    groups = width // GW
    seqs = rows // length
    half = width // 16
    col = lambda o: pl.BlockSpec((width, GW), lambda b: (0, o * groups + g))
    seq = pl.BlockSpec((length, width), lambda b: (b, 0))
    blk = pl.BlockSpec((length, GW), lambda b: (b, 0))
    whole = lambda s: pl.BlockSpec(s, lambda b: (0,) * len(s))
    S = jax.ShapeDtypeStruct
    tall = {"first": 2 * half, "second": 2 * half, "third": half + 16, "plain": 0}[mode]
    at_row = 1 if mode == "second" else 0
    block = half + 16 if mode == "third" else half
    part = pl.BlockSpec((2, 2, 4, block, 3 * GW // 2), lambda b: (0, 0, 0, at_row, 0))
    if mode == "plain":
        out_specs, out_shape = [whole((3, width, GW))], [S((3, width, GW), bf16)]
    else:
        out_specs, out_shape = [part, part], [S((2, 2, 4, tall, 3 * GW // 2), bf16)] * 2
    out_specs += [seq, whole((1, 3 * GW))]
    out_shape += [S((rows, width), bf16 if mode == "third" or g == groups - 1 else f32), S((1, 3 * GW), f32)]
    in_specs = [SMEM, blk, blk, blk, pl.BlockSpec((length, GW), lambda b: (b, g)), blk]
    in_specs += [pl.BlockSpec((1, 8, length), lambda b: (b, 0, 0)), blk, blk, seq, col(0), col(1), col(2), seq]
    aliases = {}
    if mode == "second":
        in_specs += [pl.BlockSpec(memory_space=pl.ANY)] * 2
        aliases = {len(in_specs) - 2: 0, len(in_specs) - 1: 1}
    elif mode == "third":
        in_specs += [whole(e.shape) for e in extra]
    q, k, v, ctx, lse = saved
    return pl.pallas_call(
        functools.partial(attend_back_kernel, mode),
        grid=(seqs,),
        in_specs=in_specs,
        out_specs=out_specs,
        out_shape=out_shape,
        scratch_shapes=[pltpu.VMEM((width, 3 * GW), f32)],
        input_output_aliases=aliases,
        compiler_params=params(),
        cost_estimate=cost(8_000_000_000, 8_000_000),
        name="attend_back",
    )(at, q, k, v, gc, ctx, lse, aq, ak, tokens, w, w, w, dx, *extra)


def masks(segment_ids, valid):
    code = (segment_ids + 8 * valid).reshape(-1, 1)
    lane = lax.broadcasted_iota(jnp.int32, (1, GW), 1) % HD
    same = code == lane
    aq = same.astype(bf16)
    ak = jnp.where((lane < 16) & ~same, -BIG, 0.0).astype(bf16)
    return aq, ak


def phi(x):
    return 0.5 * (1.0 + lax.erf(x * 0.7071067811865476)), jnp.exp(-0.5 * x * x) * 0.3989422804014327


def middle_kernel(groups, tok, *refs):
    ctx_r = refs[:groups]
    cot, wo, vecs, wu, bu, wd, out_o, low_o, hid_o, gd_o, gu_o, gb_o, gc_o, vec_o, bup_o, slope = refs[groups:]
    i = pl.program_id(0)
    width = tok.shape[1]
    ff = wd.shape[0]
    step = width
    chunks = ff // step
    bo, g1, s1, bd, g2, s2 = (vecs[j : j + 1, :].astype(f32) for j in range(2, 8))
    ctx = jnp.concatenate([r[...] for r in ctx_r], axis=1)
    pre = tok[...].astype(f32) + nn(ctx, wo[...]) + bo
    mean = lambda v: jnp.mean(v, axis=1, keepdims=True)
    centre = pre - mean(pre)
    r1 = lax.rsqrt(mean(centre * centre) + 1e-05)
    n1 = centre * r1
    normed = n1 * g1 + s1
    low = normed.astype(bf16)
    low_o[...] = low
    acc = normed + bd
    for c in range(chunks):
        cols = slice(c * step, (c + 1) * step)
        hp = nn(low, wu[:, cols]) + bu[:, cols].astype(f32)
        cdf, pdf = phi(hp)
        slope[:, cols] = cdf + hp * pdf
        hid = (hp * cdf).astype(bf16)
        hid_o[:, cols] = hid
        acc = acc + nn(hid, wd[cols, :])
    centre = acc - mean(acc)
    r2 = lax.rsqrt(mean(centre * centre) + 1e-05)
    n2 = centre * r2
    out_o[...] = (n2 * g2 + s2).astype(bf16)
    ct = cot[...].astype(f32)
    e = ct * g2
    gp2 = r2 * (e - mean(e) - n2 * mean(e * n2))
    gd = gp2.astype(bf16)
    gd_o[...] = gd
    acc = gp2
    total = lambda v: jnp.sum(v, axis=0, keepdims=True)

    def put(ref, at, v):
        @pl.when(i == 0)
        def _():
            ref[at] = v

        @pl.when(i > 0)
        def _():
            ref[at] += v

    for c in range(chunks):
        cols = slice(c * step, (c + 1) * step)
        gu = (nt(gd, wd[cols, :]) * slope[:, cols]).astype(bf16)
        gu_o[:, cols] = gu
        put(bup_o, (slice(0, 1), cols), total(gu.astype(f32)))
        acc = acc + nt(gu, wu[:, cols])
    e = acc * g1
    gp1 = r1 * (e - mean(e) - n1 * mean(e * n1))
    gb = gp1.astype(bf16)
    gb_o[...] = gb
    gc_o[...] = nt(gb, wo[...]).astype(bf16)
    for at, v in enumerate((gb.astype(f32), acc * n1, acc, gd.astype(f32), ct * n2, ct)):
        put(vec_o, (slice(at, at + 1), slice(None)), total(v))


def middle(tokens, ctx, cot, wo, vecs, wu, bu, wd, tile=256):
    rows, width = tokens.shape
    ff = wd.shape[0]
    act = pl.BlockSpec((tile, width), lambda i: (i, 0))
    wide = pl.BlockSpec((tile, ff), lambda i: (i, 0))
    whole = lambda a: pl.BlockSpec(a.shape, lambda i: (0, 0), pipeline_mode=pl.Buffered(1))
    S = jax.ShapeDtypeStruct
    shapes = [(rows, width), (rows, width), (rows, ff), (rows, width), (rows, ff), (rows, width), (rows, width)]
    return pl.pallas_call(
        functools.partial(middle_kernel, len(ctx)),
        grid=(rows // tile,),
        in_specs=[act] + [pl.BlockSpec((tile, GW), lambda i: (i, 0)) for _ in ctx] + [act] + [whole(a) for a in (wo, vecs, wu, bu, wd)],
        out_specs=[act, act, wide, act, wide, act, act, pl.BlockSpec((8, width), lambda i: (0, 0)), pl.BlockSpec((8, ff), lambda i: (0, 0))],
        out_shape=[S(s, bf16) for s in shapes] + [S((8, width), f32), S((8, ff), f32)],
        scratch_shapes=[pltpu.VMEM((tile, ff), f32)],
        compiler_params=params(),
        cost_estimate=cost(30_000_000_000, 40_000_000),
        name="middle",
    )(tokens, *ctx, cot, wo, vecs, wu, bu, wd)


def grad_down_kernel(groups, at_r, *refs):
    ctx = refs[:groups]
    gb, hid, gd, own_o, other_o = refs[groups:]
    p = pl.program_id(0)
    turns = ((0, at_r[1]), (1, at_r[0]))
    wide = gd.shape[1] // 2
    tall = hid.shape[1] // 2

    @pl.when(p == 0)
    def _():
        lhs = jnp.concatenate([r[...] for r in ctx], axis=1)
        res = tn(lhs, gb[...]).astype(bf16)
        piece = res.shape[0] // 8
        half = piece // 2
        for s in range(8):
            kk, far = owner_of(s, at_r)
            for ab, turn in turns:
                for h in range(2):
                    val = res[s * piece + ab * half : s * piece + (ab + 1) * half, h * wide : (h + 1) * wide]
                    rel = lax.rem(h + turn, 2)
                    for ref, cond in ((other_o, far), (own_o, ~far)):

                        @pl.when(cond)
                        def _(val=val, rel=rel, kk=kk, ab=ab, ref=ref):
                            ref[ab, rel, kk, tall : tall + half] = val

    @pl.when(p > 0)
    def _():
        res = tn(hid[...], gd[...]).astype(bf16)
        kk = lax.rem(p - 1, 4)
        for ab, turn in turns:
            for h in range(2):
                val = res[ab * tall : (ab + 1) * tall, h * wide : (h + 1) * wide]
                rel = lax.rem(h + turn, 2)
                for ref, cond in ((other_o, p < 5), (own_o, p >= 5)):

                    @pl.when(cond)
                    def _(val=val, rel=rel, ab=ab, ref=ref):
                        ref[ab, rel, kk, 0:tall] = val


def grad_down(at, ctx, gb, hid, gd):
    rows, ff = hid.shape
    width = gd.shape[1]
    piece = ff // 8
    part = (2, 2, 4, (piece + width // 8) // 2, width // 2)

    def owner(p, at_r):
        j = jnp.maximum(p - 1, 0)
        z = lax.rem(at_r[2] + lax.rem(j, 4), 4)
        return 0, 2 * z + jnp.where(j < 4, 1 - at_r[3], at_r[3])

    whole = lambda s: pl.BlockSpec(s, lambda p, at_r: (0,) * len(s))
    return pl.pallas_call(
        functools.partial(grad_down_kernel, len(ctx)),
        grid_spec=pltpu.PrefetchScalarGridSpec(
            num_scalar_prefetch=1,
            grid=(9,),
            in_specs=[whole(c.shape) for c in ctx] + [whole(gb.shape), pl.BlockSpec((rows, piece), owner), whole(gd.shape)],
            out_specs=[whole(part), whole(part)],
        ),
        out_shape=[jax.ShapeDtypeStruct(part, bf16)] * 2,
        compiler_params=params(),
        cost_estimate=cost(9_000_000_000, 14_000_000),
        name="grad_down",
    )(at, *ctx, gb, hid, gd)


def grad_up_kernel(at_r, low, gu, own_o, other_o, turned):
    j = pl.program_id(0)
    y, x = at_r[0], at_r[1]

    @pl.when(j == 0)
    def _():
        turned[...] = low[...].T

    res = nn(turned[...], gu[...]).astype(bf16)
    piece = res.shape[0] // 8
    half = piece // 2
    h = j // 4
    row = pl.multiple_of(lax.rem(j, 4) * half, 16)
    for s in range(8):
        kk, far = owner_of(s, at_r)
        for ab, turn in ((0, x), (1, y)):
            val = res[s * piece + ab * half : s * piece + (ab + 1) * half]
            for ref, cond in ((other_o, far), (own_o, ~far)):

                @pl.when(cond)
                def _(val=val, kk=kk, ab=ab, turn=turn, ref=ref):
                    ref[ab, lax.rem(h + turn, 2), kk, pl.ds(row, half), :] = val


def grad_up(at, low, gu):
    rows, width = low.shape
    ff = gu.shape[1]
    step = ff // 8
    part = (2, 2, 4, width // 4, ff // 8)
    whole = pl.BlockSpec(part, lambda j: (0, 0, 0, 0, 0))
    return pl.pallas_call(
        grad_up_kernel,
        grid=(8,),
        in_specs=[SMEM, pl.BlockSpec((rows, width), lambda j: (0, 0)), pl.BlockSpec((rows, step), lambda j: (0, j))],
        out_specs=[whole, whole],
        out_shape=[jax.ShapeDtypeStruct(part, bf16)] * 2,
        scratch_shapes=[pltpu.VMEM((width, rows), bf16)],
        compiler_params=params(),
        cost_estimate=cost(9_000_000_000, 14_000_000),
        name="grad_up",
    )(at, low, gu)


AXES = ("rep", "shard")


def pairs(move):
    found = []
    for y in range(2):
        for x in range(2):
            for z in range(4):
                for c in range(2):
                    j, i, k, d = move(y, x, z, c)
                    found.append(((y * 2 + x) * 8 + z * 2 + c, (j * 2 + i) * 8 + k * 2 + d))
    return found


CORE = pairs(lambda y, x, z, c: (y, x, z, 1 - c))
ACROSS = pairs(lambda y, x, z, c: (y, 1 - x, z, c))
ALONG = pairs(lambda y, x, z, c: (1 - y, x, z, c))
SHIFT = [None] + [pairs(lambda y, x, z, c, n=n: (y, x, (z + n) % 4, c)) for n in (1, 2, 3)]


def send(a, where):
    return lax.ppermute(a, AXES, where)


def tie(values, *after):
    flat, tree = jax.tree.flatten(values)
    return jax.tree.unflatten(tree, lax.optimization_barrier(tuple(flat) + tuple(jax.tree.leaves(after)))[: len(flat)])


def place(own, received, at_r, rows, out, base, quarter):
    y, x, z = at_r[0], at_r[1], at_r[2]
    cols = out.shape[1]
    half = rows // 2
    out[pl.ds(pl.multiple_of(base(z), 16), rows), :] = own
    for k in range(1, 4):
        start = base(lax.rem(z - k + 4, 4))
        for ab in range(2):
            at = pl.ds(pl.multiple_of(start + ab * half, 16), half)
            if quarter:
                wide = cols // 4
                for i in range(2):
                    for l in range(2):
                        one, two = (i, l) if ab == 0 else (l, i)
                        col = (lax.rem(x + i, 2) * 2 + lax.rem(y + l, 2)) * wide
                        out[at, pl.ds(pl.multiple_of(col, 128), wide)] = received(ab, one, two, k)
            else:
                wide = cols // 2
                for one in range(2):
                    col = lax.rem((x, y)[ab] + one, 2) * wide
                    out[at, pl.ds(pl.multiple_of(col, 128), wide)] = received(ab, one, 0, k)


def assemble_half_kernel(out_rows, at_r, *refs):
    n = len(out_rows)
    outs = refs[-n:]
    c = at_r[3]
    for turn, (own, ring, far_x, far_y) in ((c, refs[:4]), (1 - c, refs[4:8])):
        off = 0
        total_half = sum(out_rows) // 2
        for out, rows in zip(outs, out_rows):
            half = rows // 2

            def received(ab, one, two, k):
                if one == 0:
                    return ring[k - 1, ab * total_half + off : ab * total_half + off + half, :]
                return (far_x, far_y)[ab][k - 1, off : off + half, :]

            whole = jnp.concatenate([own[off : off + half], own[total_half + off : total_half + off + half]], axis=0)
            place(whole, received, at_r, rows, out, lambda z: (2 * z + turn) * rows, False)
            off += half


def assemble_quarter_kernel(at_r, *refs):
    out = refs[-1]
    c = at_r[3]
    for turn, (own, near_a, near_b, far) in ((c, refs[:4]), (1 - c, refs[4:8])):
        rows = own.shape[0]

        def received(ab, one, two, k):
            if two == 1:
                return far[ab, one, k - 1]
            return (near_a, near_b)[ab][one, k - 1]

        place(own[...], received, at_r, rows, out, lambda z: (2 * z + turn) * rows, True)


def assemble(kernel, at, parts, shapes):
    return pl.pallas_call(
        kernel,
        in_specs=[SMEM] + [VMEM] * len(parts),
        out_specs=[VMEM] * len(shapes),
        out_shape=[jax.ShapeDtypeStruct(s, bf16) for s in shapes],
        compiler_params=params(),
        cost_estimate=cost(0, sum(4 * s[0] * s[1] for s in shapes)),
        name="assemble",
    )(at, *parts)


def halves(w, x, y):
    half, wide = w.shape[0] // 2, w.shape[1] // 2
    a = lax.dynamic_slice(w, (0, x * wide), (half, wide))
    b = lax.dynamic_slice(w, (half, y * wide), (half, wide))
    return jnp.concatenate([a, b], axis=0)


def spread_half(ring, half):
    return send(ring[:, :half], ACROSS), send(ring[:, half : 2 * half], ALONG)


def swap(parts):
    return tuple(send(p, CORE) for p in parts)


def total(*terms):
    out = terms[0].astype(f32)
    for t in terms[1:]:
        out = out + t.astype(f32)
    return out.astype(bf16)


def finish_kernel(kind, at_r, *refs):
    y, x = at_r[0], at_r[1]
    blocks, outs = refs[:4], refs[4:]
    for ab, turn in ((0, x), (1, y)):
        one, two = (blocks[2 * ab + i][...].astype(f32) for i in range(2))
        left = jnp.where(turn == 0, one, two)
        right = jnp.where(turn == 0, two, one)
        both = jnp.concatenate([left, right], axis=1)
        if kind == "ffn":
            off = 0
            for out in outs[:2]:
                half = out.shape[0] // 2
                out[ab * half : (ab + 1) * half, :] = both[off : off + half]
                off += half
            half = outs[2].shape[0] // 2
            eighth = left.shape[1]
            for i in range(4):
                for h, val in ((0, left), (1, right)):
                    col = (4 * h + i) * eighth
                    outs[2][ab * half : (ab + 1) * half, col : col + eighth] = val[off + i * half : off + (i + 1) * half]
        else:
            half = outs[0].shape[0] // 2
            groups = outs[0].shape[1] // (3 * GW)
            for g in range(groups):
                for i in range(3):
                    col = (i * groups + g) * GW
                    outs[0][ab * half : (ab + 1) * half, col : col + GW] = both[g * half : (g + 1) * half, i * GW : (i + 1) * GW]
            if ab == 0:
                rows = groups * half
                outs[1][...] = left[rows : rows + 16, :128]


def finish(at, kind, blocks, shapes):
    return pl.pallas_call(
        functools.partial(finish_kernel, kind),
        in_specs=[SMEM] + [VMEM] * len(blocks),
        out_specs=[VMEM] * len(shapes),
        out_shape=[jax.ShapeDtypeStruct(s, f32) for s in shapes],
        compiler_params=params(),
        cost_estimate=cost(0, 4_000_000),
        name="finish_" + kind,
    )(at, *blocks)


def pack(vectors, wide):
    block = jnp.concatenate([v.reshape(-1, vectors[1].shape[0]) for v in vectors] + [wide.reshape(4, -1)], axis=0)
    return jnp.pad(block, ((0, 16 - block.shape[0]), (0, 128 - block.shape[1])))


def whole_vectors(every, z, c, piece):
    k = lax.broadcasted_iota(jnp.int32, (2, 4, 8), 1)
    d = lax.broadcasted_iota(jnp.int32, (2, 4, 8), 0)
    s = lax.broadcasted_iota(jnp.int32, (2, 4, 8), 2)
    pick = (s == 2 * ((z - k) % 4) + (c + d) % 2).astype(bf16)
    table = jnp.einsum("dks,dkrl->srl", pick, every, preferred_element_type=f32).astype(bf16)
    table = table[:, :, :piece]
    wide = table[:, 8:12].reshape(1, -1)
    return table.transpose(1, 0, 2).reshape(16, -1), wide


class Sum:
    def __init__(self):
        self.own, self.got = [], []

    def add(self, own, other):
        self.own.append(own)
        self.got.append(send(other, CORE))

    def after(self, *values):
        self.got, self.far, self.parts = tie((self.got, self.far, self.parts), *values)

    far = parts = ()

    def pair(self, pick, *more):
        found = [total(pick(o), pick(g)) for o, g in zip(self.own, self.got)]
        found = found[0] if len(found) == 1 else jnp.concatenate(found, axis=-2)
        return total(found, *more) if more else found

    def halve(self):
        self.sent = self.pair(lambda a: a[0, 1]), self.pair(lambda a: a[1, 1])
        self.far = send(self.sent[0], ACROSS), send(self.sent[1], ALONG)

    def along_z(self):
        far = self.far
        self.mine = [jnp.stack([self.near(i, k) for i in range(2)]) for k in range(4)]
        self.sent = self.mine[1:]
        self.far = ()
        self.parts = [send(self.mine[k], SHIFT[k]) for k in range(1, 4)]

    def near(self, i, k):
        terms = []
        at = 0
        for o, g in zip(self.own, self.got):
            rows = o.shape[3]
            terms.append(total(o[i, 0, k], g[i, 0, k], self.far[i][k, at : at + rows]))
            at += rows
        return terms[0] if len(terms) == 1 else jnp.concatenate(terms, axis=0)

    def across(self, *more):
        both = [total(v.mine[0], *v.parts) for v in (self,) + more]
        both = both[0] if len(both) == 1 else jnp.concatenate(both, axis=1)
        self.got = self.parts = ()
        self.sent = both[0], both[1]
        self.far = send(both[0], ALONG), send(both[1], ACROSS)

    def share(self):
        a, b = (total(self.sent[i], self.far[i]) for i in range(2))
        self.sent = a, b
        self.out = a, send(a, ACROSS), b, send(b, ALONG)


def shards_near(
    tokens,
    cotangent,
    qkv_weight,
    query_value_bias,
    out_weight,
    out_bias,
    norm_one_gain,
    norm_one_shift,
    up_weight,
    up_bias,
    down_weight,
    down_bias,
    norm_two_gain,
    norm_two_shift,
    segment_ids,
    valid,
):
    length = segment_ids.shape[1]
    width = tokens.shape[1]
    groups = width // GW
    ff = up_bias.shape[0] * 8
    piece = out_bias.shape[0]
    r, s = lax.axis_index("rep"), lax.axis_index("shard")
    y, x, z, c = r // 2, r % 2, s // 2, s % 2
    at = jnp.stack([y, x, z, c]).astype(jnp.int32)

    half = piece // 2
    block = pack(
        (query_value_bias, out_bias, norm_one_gain, norm_one_shift, down_bias, norm_two_gain, norm_two_shift), up_bias
    )
    lines = lambda n, cols: jnp.pad(block.reshape(n, -1), ((0, 8 - n), (0, cols - 2048 // n)))
    dr = down_weight.shape[0] // 2
    own_q = jnp.concatenate([qkv_weight, lines(1, 3 * width)], axis=0)
    own_d = jnp.concatenate([down_weight[:dr], out_weight[:half], down_weight[dr:], out_weight[half:]], axis=0)
    other_q, other_u, other_d = swap((own_q, up_weight, own_d))
    held = jnp.concatenate([halves(qkv_weight, x, y), lines(2, 3 * width // 2)], axis=0)
    ring = []
    for step in range(3):
        if step == 2:
            held = tie(held, other_q, other_u, other_d)
        held = send(held, SHIFT[1])
        ring.append(held)
    ring_q = jnp.stack(ring)
    far_q = spread_half(ring_q, half)
    first_u = lax.dynamic_slice(up_weight, (0, (2 * x + y) * (ff // 4)), (piece, ff // 4))
    first_u = tie(first_u, held)
    ring_u = [send(first_u, SHIFT[k]) for k in range(1, 4)]
    rest_q = swap(tie((ring_q,) + far_q, ring_u))
    swapped_q = rest_q[0]
    parts_q = (own_q, ring_q) + far_q + (other_q,) + rest_q
    (wqkv,) = assemble(
        functools.partial(assemble_half_kernel, [qkv_weight.shape[0]]), at, parts_q, [(width, 3 * width)]
    )
    blocks = lambda own, ring: jnp.concatenate([own[None, piece : piece + 1, :2048].reshape(1, 16, 128), ring[:, piece : piece + 2, :1024].reshape(3, 16, 128)])
    vecs, bu = whole_vectors(jnp.stack([blocks(own_q, ring_q), blocks(other_q, swapped_q)]), z, c, piece)

    aq, ak = masks(segment_ids, valid)
    ring_u = jnp.stack(tie(ring_u, far_q))
    first_d = tie(halves(own_d, x, y), ring_u)
    ring_d = [send(first_d, SHIFT[k]) for k in range(1, 4)]
    a, b = ring_u[:, :half], ring_u[:, half:]
    a2, b2 = send(a, ACROSS), send(b, ALONG)
    saved = [attend(0, tie(tokens, a, b, first_d), wqkv, vecs, aq, ak, length)]
    a2, b2 = tie((a2, b2), saved[0][3])
    a3, b3 = jnp.stack([a, a2]), jnp.stack([b, b2])
    a4, b4 = send(a3, ALONG), send(b3, ACROSS)
    saved.append(attend(1, tie(tokens, a3, b3), wqkv, vecs, aq, ak, length))
    a4, b4, ring_d = tie((a4, b4, ring_d), saved[1][3])
    ring_d = jnp.stack(ring_d)
    ab4 = jnp.stack([a4, b4])
    far_d = spread_half(ring_d, dr + half)
    rest_u = swap((a3, b3, ab4))
    saved.append(attend(2, tie(tokens, ring_d, ab4), wqkv, vecs, aq, ak, length))
    far_d, rest_u = tie((far_d, rest_u), saved[2][3])
    rest_d = swap(tie((ring_d,) + far_d, rest_u))
    (wu,) = assemble(assemble_quarter_kernel, at, tie((up_weight, a3, b3, ab4, other_u) + rest_u, far_d), [(width, ff)])
    wd, wo = assemble(
        functools.partial(assemble_half_kernel, [2 * dr, piece]),
        at,
        (own_d, ring_d) + far_d + (other_d,) + tie(rest_d, wu),
        [(ff, width), (width, width)],
    )

    ctx = [f[3] for f in saved]
    result, low, hid, gd, gu, gb, gc, vec, bup = middle(tokens, ctx, cotangent, wo, vecs, wu, bu, wd)

    down, up, qkv = Sum(), Sum(), Sum()
    own, other = grad_down(at, ctx, gb, hid, gd)
    down.add(own, other)
    own, other = grad_up(at, *tie((low, gu), other))
    up.add(own, other)
    down.after(other)
    down.halve()
    own, other, dx, db0 = attend_back("first", 0, at, saved[0], tie(gc, down.sent, other), aq, ak, tokens, wqkv, gb, length)
    down.after(dx)
    up.after(dx)
    down.along_z()
    up.halve()
    dx = tie(dx, down.sent, up.sent)
    own, other, dx, db1 = attend_back("second", 1, at, saved[1], gc, aq, ak, tokens, wqkv, dx, length, (own, other))
    qkv.add(own, other)
    up.after(dx)
    wide = bup[0].reshape(8, 4, piece).transpose(1, 0, 2).reshape(4, width)
    table = jnp.concatenate([vec[:6], wide, jnp.zeros((4, width), f32)], axis=0)
    own, other, dx, _ = attend_back(
        "third", 2, at, saved[2], gc, aq, ak, tokens, wqkv, tie(dx, up.far), length, (db0, db1, table)
    )
    down.after(dx)
    qkv.after(dx)
    qkv.add(own, other)
    up.after(down.parts)
    up.along_z()
    qkv.halve()
    up.after(qkv.far)
    qkv.after(up.parts)
    qkv.along_z()
    down.across(up)
    down.share()
    dwd, dwo, dwu = finish(at, "ffn", down.out, [down_weight.shape, out_weight.shape, up_weight.shape])
    qkv.after(dwd, dwo, dwu)
    qkv.across()
    qkv.share()
    dwq, small = finish(at, "qkv", qkv.out, [qkv_weight.shape, (16, 128)])
    one = lambda i: small[i, :piece]
    return (
        result,
        dx,
        dwq,
        small[:2, :piece],
        dwo,
        one(2),
        one(3),
        one(4),
        dwu,
        small[8:12, :piece].reshape(-1),
        dwd,
        one(5),
        one(6),
        one(7),
    )


def spread(args):
    flat = [a.reshape(-1) for a in args]
    packed = jnp.concatenate(flat)
    every = lax.all_gather(packed, "shard", axis=0)
    out, at = [], 0
    for a in args:
        part = every[:, at : at + a.size].reshape((-1,) + a.shape)
        at += a.size
        out.append(jnp.moveaxis(part, 0, -2).reshape(a.shape[:-1] + (-1,)))
    return out


def shards(
    tokens,
    cotangent,
    qkv_weight,
    query_value_bias,
    out_weight,
    out_bias,
    norm_one_gain,
    norm_one_shift,
    up_weight,
    up_bias,
    down_weight,
    down_bias,
    norm_two_gain,
    norm_two_shift,
    segment_ids,
    valid,
):
    length = segment_ids.shape[1]
    width = tokens.shape[1]
    groups = width // GW
    gather = lambda a: lax.all_gather(a, "shard", axis=0, tiled=True)
    *rest, bu = spread(
        (query_value_bias, out_bias, norm_one_gain, norm_one_shift, down_bias, norm_two_gain, norm_two_shift, up_bias)
    )
    vecs = jnp.concatenate([v.reshape(-1, width) for v in rest] + [jnp.zeros((8, width), bf16)], axis=0)
    wqkv, wd, wo, wu = gather(qkv_weight), gather(down_weight), gather(out_weight), gather(up_weight)
    at = jnp.zeros((4,), jnp.int32)
    aq, ak = masks(segment_ids, valid)
    saved = [attend(g, tokens, wqkv, vecs, aq, ak, length) for g in range(groups)]
    ctx = [f[3] for f in saved]
    result, low, hid, gd, gu, gb, gc, vec, bup = middle(tokens, ctx, cotangent, wo, vecs, wu, bu[None], wd)
    dwd = tn(hid, gd).astype(bf16)
    dwu = tn(low, gu).astype(bf16)
    dwo = tn(jnp.concatenate(ctx, axis=1), gb).astype(bf16)
    dx, dws, dbs = gb, [], []
    for g in range(groups):
        dw, dx, db = attend_back("plain", g, at, saved[g], gc, aq, ak, tokens, wqkv, dx, length)
        dws.append(dw)
        dbs.append(db)
    dwq = jnp.concatenate([dw[i] for i in range(3) for dw in dws], axis=1)
    db = jnp.stack(dbs).reshape(groups, 3, GW).transpose(1, 0, 2).reshape(3, width)
    small = jnp.concatenate([db[0], db[2], vec[:6].reshape(-1), bup[0]])
    small = lax.psum(small.reshape(-1, 128), ("rep", "shard")).reshape(-1)

    def owned(a):
        part = lax.psum_scatter(a, "shard", scatter_dimension=0, tiled=True)
        return lax.psum(part, "rep").astype(f32)

    rank = lax.axis_index("shard")
    own = lambda at, size: lax.dynamic_slice(small, (at + rank * size,), (size,))
    piece = out_bias.shape[0]
    vs = [own(width * i, piece) for i in range(8)]
    dbu = own(8 * width, up_bias.shape[0])
    gd_w, gu_w, go_w, gq_w = owned(dwd), owned(dwu), owned(dwo), owned(dwq)
    return result, dx, gq_w, jnp.stack(vs[:2]), go_w, vs[2], vs[3], vs[4], gu_w, dbu, gd_w, vs[5], vs[6], vs[7]


def solution(mesh):
    rows, one = P(("rep", "shard"), None), P("shard")
    mat, two = P("shard", None), P(None, "shard")
    near = mesh.shape["rep"] == 4 and mesh.shape["shard"] == 8
    return jax.shard_map(
        shards_near if near else shards,
        mesh=mesh,
        in_specs=(rows, rows, mat, two, mat, one, one, one, mat, one, mat, one, one, one, rows, rows),
        out_specs=(rows, rows, mat, two, mat, one, one, one, mat, one, mat, one, one, one),
        check_vma=False,
    )
```

profile of v0, /device:TPU:0, one launch (start us, length us, event | category | flops | bytes accessed | tf_op | source)
XLA Modules:
  0.0 353.0 jit_solution(4817450580301507353)
XLA Ops:
  10.1 5.1 %collective-permute-done = bf16[104,1152]{1,0:T(8,128)(2,1)} collective-permute-done((bf16[104,1152]{1,0:T(8,128)(2,1)}, bf16[104,1152]{1,0:T(8,128)(2,1)}, u32[]{:S(2)}, u32[]{:S(2)}) %collective-permute-start) | collective-permute-done | bytes 239648 | tf_op jit(solution)/shard_map/ppermute | solution.py:470
  16.2 8.0 %collective-permute-done.1 = bf16[104,1152]{1,0:T(8,128)(2,1)S(1)} collective-permute-done((bf16[104,1152]{1,0:T(8,128)(2,1)}, bf16[104,1152]{1,0:T(8,128)(2,1)S(1)}, u32[]{:S(2)}, u32[]{:S(2)}) %collective-permute-start.1) | collective-permute-done | bytes 239648 | tf_op jit(solution)/shard_map/ppermute | solution.py:470
  25.5 6.8 %collective-permute-done.5 = bf16[104,1152]{1,0:T(8,128)(2,1)S(1)} collective-permute-done((bf16[104,1152]{1,0:T(8,128)(2,1)S(1)}, bf16[104,1152]{1,0:T(8,128)(2,1)S(1)}, u32[]{:S(2)}, u32[]{:S(2)}) %collective-permute-start.5) | collective-permute-done | bytes 239648 | tf_op jit(solution)/shard_map/ppermute | solution.py:470
  36.4 3.7 %collective-permute-start.8 = (bf16[96,768]{1,0:T(8,128)(2,1)}, bf16[96,768]{1,0:T(8,128)(2,1)S(1)}, u32[]{:S(2)}, u32[]{:S(2)}) collective-permute-start(bf16[96,768]{1,0:T(8,128)(2,1)} %constant_dynamic-slice_fusion.2), channel_id=1, source_target_pairs={{0,6},{1,7},{2,0},{3,1},{4,2},{5,3},{6,4},{7,5},{8,14},{9,15},{10,... | collective-permute-start | bytes 442376 | tf_op jit(solution)/shard_map/ppermute | solution.py:470
  40.2 3.7 %collective-permute-done.6 = bf16[96,768]{1,0:T(8,128)(2,1)S(1)} collective-permute-done((bf16[96,768]{1,0:T(8,128)(2,1)}, bf16[96,768]{1,0:T(8,128)(2,1)S(1)}, u32[]{:S(2)}, u32[]{:S(2)}) %collective-permute-start.6) | collective-permute-done | bytes 147488 | tf_op jit(solution)/shard_map/ppermute | solution.py:470
  52.8 4.1 %assemble.3.wq.wk.wv = bf16[768,2304]{1,0:T(8,128)(2,1)} custom-call(s32[4]{0:T(128)} %pad_add_fusion.at_r, bf16[104,2304]{1,0:T(8,128)(2,1)} %copy-done.6, bf16[3,104,1152]{2,1,0:T(8,128)(2,1)} %copy-done.1, bf16[3,48,1152]{2,1,0:T(8,128)(2,1)} %copy-done.28, bf16[3,48,1152]{2,1,0:T(8,128)(2,1)} %copy-done.27, ...), custom_call_target="tpu_custom_call" | custom-call | bytes 7077888 | tf_op jit(solution)/shard_map/assemble/pallas_call | solution.py:536
  56.9 7.9 %attend.3 = (bf16[1024,256]{1,0:T(8,128)(2,1)}, bf16[1024,256]{1,0:T(8,128)(2,1)}, bf16[1024,256]{1,0:T(8,128)(2,1)}, bf16[1024,256]{1,0:T(8,128)(2,1)}, f32[2,8,512]{2,1,0:T(8,128)}) custom-call(bf16[1024,768]{1,0:T(8,128)(2,1)} %tok.10, bf16[768,2304]{1,0:T(8,128)(2,1)} %assemble.3.wq.wk.wv, bf16[768,2304]{1,0:T(8,128)(2,1)} %assemble.3.wq.wk.wv, ...), custom_call_target="tpu_custom_call" | custom-call | flops 4000000000 | bytes 5000000 | tf_op jit(solution)/shard_map/attend/pallas_call | solution.py:80
  72.9 7.9 %attend.4 = (bf16[1024,256]{1,0:T(8,128)(2,1)}, bf16[1024,256]{1,0:T(8,128)(2,1)}, bf16[1024,256]{1,0:T(8,128)(2,1)}, bf16[1024,256]{1,0:T(8,128)(2,1)}, f32[2,8,512]{2,1,0:T(8,128)}) custom-call(bf16[1024,768]{1,0:T(8,128)(2,1)} %tok.10, bf16[768,2304]{1,0:T(8,128)(2,1)} %assemble.3.wq.wk.wv, bf16[768,2304]{1,0:T(8,128)(2,1)} %assemble.3.wq.wk.wv, ...), custom_call_target="tpu_custom_call" | custom-call | flops 4000000000 | bytes 5000000 | tf_op jit(solution)/shard_map/attend/pallas_call | solution.py:80
  81.4 14.1 %collective-permute-done.19 = bf16[480,384]{1,0:T(8,128)(2,1)S(1)} collective-permute-done((bf16[480,384]{1,0:T(8,128)(2,1)S(1)}, bf16[480,384]{1,0:T(8,128)(2,1)S(1)}, u32[]{:S(2)}, u32[]{:S(2)}) %collective-permute-start.19) | collective-permute-done | bytes 368672 | tf_op jit(solution)/shard_map/ppermute | solution.py:470
  100.5 8.0 %attend.5 = (bf16[1024,256]{1,0:T(8,128)(2,1)}, bf16[1024,256]{1,0:T(8,128)(2,1)}, bf16[1024,256]{1,0:T(8,128)(2,1)}, bf16[1024,256]{1,0:T(8,128)(2,1)}, f32[2,8,512]{2,1,0:T(8,128)}) custom-call(bf16[1024,768]{1,0:T(8,128)(2,1)} %tok.10, bf16[768,2304]{1,0:T(8,128)(2,1)} %assemble.3.wq.wk.wv, bf16[768,2304]{1,0:T(8,128)(2,1)} %assemble.3.wq.wk.wv, ...), custom_call_target="tpu_custom_call" | custom-call | flops 4000000000 | bytes 5000000 | tf_op jit(solution)/shard_map/attend/pallas_call | solution.py:80
  108.5 4.7 %collective-permute-done.21.refs_2_ = bf16[3,240,384]{2,1,0:T(8,128)(2,1)} collective-permute-done((bf16[3,240,384]{2,1,0:T(8,128)(2,1)S(1)}, bf16[3,240,384]{2,1,0:T(8,128)(2,1)}, u32[]{:S(2)}, u32[]{:S(2)}) %collective-permute-start.21) | collective-permute-done | bytes 552992 | tf_op jit(solution)/shard_map/ppermute | solution.py:470
  114.8 4.8 %assemble.4.refs_6_ = bf16[768,3072]{1,0:T(8,128)(2,1)} custom-call(s32[4]{0:T(128)} %pad_add_fusion.at_r, bf16[96,3072]{1,0:T(8,128)(2,1)} %refs_0_, bf16[2,3,48,768]{3,2,1,0:T(8,128)(2,1)} %copy-done.8, bf16[2,3,48,768]{3,2,1,0:T(8,128)(2,1)} %copy-done.7, bf16[2,2,3,48,768]{4,3,2,1,0:T(8,128)(2,1)} %copy-done.3, bf16[96,3072]{1,0:T(8,128)(2,1)} %copy-done.18, ...), custom_call_target="tpu_custom_call" | custom-call | bytes 9437184 | tf_op jit(solution)/shard_map/assemble/pallas_call | solution.py:536
  121.5 5.7 %assemble.5 = (bf16[3072,768]{1,0:T(8,128)(2,1)}, bf16[768,768]{1,0:T(8,128)(2,1)}) custom-call(s32[4]{0:T(128)} %pad_add_fusion.at_r, bf16[480,768]{1,0:T(8,128)(2,1)} %copy-done.2, bf16[3,480,384]{2,1,0:T(8,128)(2,1)} %copy-done, bf16[3,240,384]{2,1,0:T(8,128)(2,1)} %collective-permute-done.21.refs_2_, ...), custom_call_target="tpu_custom_call" | custom-call | bytes 11796480 | tf_op jit(solution)/shard_map/assemble/pallas_call | solution.py:536
  127.2 43.4 %middle.1 = (bf16[1024,768]{1,0:T(8,128)(2,1)}, bf16[1024,768]{1,0:T(8,128)(2,1)}, bf16[1024,3072]{1,0:T(8,128)(2,1)}, bf16[1024,768]{1,0:T(8,128)(2,1)}, bf16[1...) custom-call(bf16[1024,768]{1,0:T(8,128)(2,1)} %tok.10, ...), custom_call_target="tpu_custom_call" | custom-call | flops 30000001024 | bytes 40000000 | tf_op jit(solution)/shard_map/middle/pallas_call | solution.py:325
  170.6 15.9 %grad_down.1 = (bf16[2,2,4,240,384]{4,3,2,1,0:T(8,128)(2,1)}, bf16[2,2,4,240,384]{4,3,2,1,0:T(8,128)(2,1)}) custom-call(s32[4]{0:T(128)} %pad_add_fusion.at_r, bf16[1024,256]{1,0:T(8,128)(2,1)} %get-tuple-element.138.refs_0_.ctx_r, bf16[1024,256]{1,0:T(8,128)(2,1)} %get-tuple-element.142.refs_1_.ctx_r, bf16[1024,256]{1,0:T(8,128)(2,1)} %get-tuple-element.149.refs_2_.ctx_r, ...), custom_call_target="tpu_custom_call" | custom-call | flops 8999999488 | bytes 14000000 | tf_op jit(solution)/shard_map/grad_down/pallas_call | solution.py:391
  186.9 14.7 %grad_up.1 = (bf16[2,2,4,192,384]{4,3,2,1,0:T(8,128)(2,1)}, bf16[2,2,4,192,384]{4,3,2,1,0:T(8,128)(2,1)}) custom-call(s32[4]{0:T(128)} %pad_add_fusion.at_r, bf16[1024,768]{1,0:T(8,128)(2,1)} %get-tuple-element.191.low, bf16[1024,3072]{1,0:T(8,128)(2,1)} %get-tuple-element.192.gu), custom_call_target="tpu_custom_call" | custom-call | flops 8999999488 | bytes 14000000 | tf_op jit(solution)/shard_map/grad_up/pallas_call | solution.py:436
  208.4 14.1 %attend_back.3 = (bf16[2,2,4,96,384]{4,3,2,1,0:T(8,128)(2,1)}, bf16[2,2,4,96,384]{4,3,2,1,0:T(8,128)(2,1)}, f32[1024,768]{1,0:T(8,128)}, f32[1,768]{1,0:T(1,128)}) custom-call(s32[4]{0:T(128)} %pad_add_fusion.at_r, bf16[1024,256]{1,0:T(8,128)(2,1)} %get-tuple-element.181.q_r, bf16[1024,256]{1,0:T(8,128)(2,1)} %get-tuple-element.182.k_r, ...), custom_call_target="tpu_custom_call" | custom-call | flops 8000000000 | bytes 8000000 | tf_op jit(solution)/shard_map/attend_back/pallas_call | solution.py:227
  231.6 8.7 %collective-permute-start.41 = (bf16[2,240,384]{2,1,0:T(8,128)(2,1)}, bf16[2,240,384]{2,1,0:T(8,128)(2,1)}, u32[]{:S(2)}, u32[]{:S(2)}) collective-permute-start(bf16[2,240,384]{2,1,0:T(8,128)(2,1)} %pad_maximum_fusion.12), channel_id=1, source_target_pairs={{0,6},{1,7},{2,0},{3,1},{4,2},{5,3},{6,4},{7,5},{8,14},{9,15},{10,... | collective-permute-start | bytes 1105928 | tf_op jit(solution)/shard_map/ppermute | solution.py:470
  243.1 14.1 %attend_back.4 = (bf16[2,2,4,96,384]{4,3,2,1,0:T(8,128)(2,1)}, bf16[2,2,4,96,384]{4,3,2,1,0:T(8,128)(2,1)}, f32[1024,768]{1,0:T(8,128)}, f32[1,768]{1,0:T(1,128)}) custom-call(s32[4]{0:T(128)} %pad_add_fusion.at_r, bf16[1024,256]{1,0:T(8,128)(2,1)} %get-tuple-element.177.q_r, ...), custom_call_target="tpu_custom_call", output_to_operand_aliasing={{0}: (14, {}), {1}: (15, {})} | custom-call | flops 8000000000 | bytes 8000000 | tf_op jit(solution)/shard_map/attend_back/pallas_call | solution.py:227
  257.4 15.4 %attend_back.5 = (bf16[2,2,4,64,384]{4,3,2,1,0:T(8,128)(2,1)}, bf16[2,2,4,64,384]{4,3,2,1,0:T(8,128)(2,1)}, bf16[1024,768]{1,0:T(8,128)(2,1)}, f32[1,768]{1,0:T(1,128)}) custom-call(s32[4]{0:T(128)} %pad_add_fusion.at_r, bf16[1024,256]{1,0:T(8,128)(2,1)} %get-tuple-element.172.q_r, bf16[1024,256]{1,0:T(8,128)(2,1)} %get-tuple-element.173.k_r, ...), custom_call_target="tpu_custom_call" | custom-call | flops 8000000000 | bytes 8000000 | tf_op jit(solution)/shard_map/attend_back/pallas_call | solution.py:227
  276.6 4.1 %collective-permute-start.44 = (bf16[2,192,384]{2,1,0:T(8,128)(2,1)S(1)}, bf16[2,192,384]{2,1,0:T(8,128)(2,1)S(1)}, u32[]{:S(2)}, u32[]{:S(2)}) collective-permute-start(bf16[2,192,384]{2,1,0:T(8,128)(2,1)S(1)} %pad_maximum_fusion.16), channel_id=1, source_target_pairs={{0,6},{1,7},{2,0},{3,1},{4,2},{5,3},{6,4},{7,5},{8,14},{9,15},{10,... | collective-permute-start | bytes 884744 | tf_op jit(solution)/shard_map/ppermute | solution.py:470
  288.2 18.4 %collective-permute-done.43 = bf16[2,192,384]{2,1,0:T(8,128)(2,1)S(1)} collective-permute-done((bf16[2,192,384]{2,1,0:T(8,128)(2,1)S(1)}, bf16[2,192,384]{2,1,0:T(8,128)(2,1)S(1)}, u32[]{:S(2)}, u32[]{:S(2)}) %collective-permute-start.43) | collective-permute-done | bytes 294944 | tf_op jit(solution)/shard_map/ppermute | solution.py:470
  320.5 4.0 %collective-permute-done.51.refs_3_ = bf16[432,384]{1,0:T(8,128)(2,1)S(1)} collective-permute-done((bf16[432,384]{1,0:T(8,128)(2,1)S(1)}, bf16[432,384]{1,0:T(8,128)(2,1)S(1)}, u32[]{:S(2)}, u32[]{:S(2)}) %collective-permute-start.51) | collective-permute-done | bytes 331808 | tf_op jit(solution)/shard_map/ppermute | solution.py:470
  328.9 4.9 %collective-permute-done.46 = bf16[2,160,384]{2,1,0:T(8,128)(2,1)S(1)} collective-permute-done((bf16[2,160,384]{2,1,0:T(8,128)(2,1)S(1)}, bf16[2,160,384]{2,1,0:T(8,128)(2,1)S(1)}, u32[]{:S(2)}, u32[]{:S(2)}) %collective-permute-start.46) | collective-permute-done | bytes 245792 | tf_op jit(solution)/shard_map/ppermute | solution.py:470
  (275 shorter events, 109.0 us)
Async XLA Ops:
  8.3 15.9 %collective-permute-start.4 = (bf16[480,768]{1,0:T(8,128)(2,1)S(1)}, bf16[480,768]{1,0:T(8,128)(2,1)S(1)}, u32[]{:S(2)}, u32[]{:S(2)}) collective-permute-start(bf16[480,768]{1,0:T(8,128)(2,1)S(1)} %pad_maximum_fusion.2.refs_0_), channel_id=1, source_target_pairs={{0,1},{1,0},{2,3},{3,2},{4,5},{5,4},{6,7},{7,6},{8,9},{9,8},{10,11... | collective-permute-start | bytes 2211848 | tf_op jit(solution)/shard_map/ppermute | solution.py:470
  8.4 15.8 %collective-permute-start.2 = (bf16[104,2304]{1,0:T(8,128)(2,1)S(1)}, bf16[104,2304]{1,0:T(8,128)(2,1)}, u32[]{:S(2)}, u32[]{:S(2)}) collective-permute-start(bf16[104,2304]{1,0:T(8,128)(2,1)S(1)} %fusion.7.refs_0_), channel_id=1, source_target_pairs={{0,1},{1,0},{2,3},{3,2},{4,5},{5,4},{6,7},{7,6},{8,9},{9,8},{10,11... | collective-permute-start | bytes 1437704 | tf_op jit(solution)/shard_map/ppermute | solution.py:470
  64.9 30.6 %collective-permute-start.17 = (bf16[2,3,48,768]{3,2,1,0:T(8,128)(2,1)S(1)}, bf16[2,3,48,768]{3,2,1,0:T(8,128)(2,1)S(1)}, u32[]{:S(2)}, u32[]{:S(2)}) collective-permute-start(bf16[2,3,48,768]{3,2,1,0:T(8,128)(2,1)S(1)} %pad_maximum_fusion.8.refs_2_), channel_id=1, source_target_pairs={{0,8},{1,9},{2,10},{3,11},{4,12},{5,13},{6,14},{7,15},{8,0},{9,1},... | collective-permute-start | bytes 1327112 | tf_op jit(solution)/shard_map/ppermute | solution.py:470
  66.4 29.1 %collective-permute-start.16 = (bf16[2,3,48,768]{3,2,1,0:T(8,128)(2,1)S(1)}, bf16[2,3,48,768]{3,2,1,0:T(8,128)(2,1)S(1)}, u32[]{:S(2)}, u32[]{:S(2)}) collective-permute-start(bf16[2,3,48,768]{3,2,1,0:T(8,128)(2,1)S(1)} %pad_maximum_fusion.7.refs_1_), channel_id=1, source_target_pairs={{0,16},{1,17},{2,18},{3,19},{4,20},{5,21},{6,22},{7,23},{8,24},{9,... | collective-permute-start | bytes 1327112 | tf_op jit(solution)/shard_map/ppermute | solution.py:470
  70.3 25.2 %collective-permute-start.19 = (bf16[480,384]{1,0:T(8,128)(2,1)S(1)}, bf16[480,384]{1,0:T(8,128)(2,1)S(1)}, u32[]{:S(2)}, u32[]{:S(2)}) collective-permute-start(bf16[480,384]{1,0:T(8,128)(2,1)S(1)} %pad_maximum_fusion.9), channel_id=1, source_target_pairs={{0,4},{1,5},{2,6},{3,7},{4,0},{5,1},{6,2},{7,3},{8,12},{9,13},{10,... | collective-permute-start | bytes 1105928 | tf_op jit(solution)/shard_map/ppermute | solution.py:470
  70.9 24.6 %collective-permute-start.20 = (bf16[480,384]{1,0:T(8,128)(2,1)S(1)}, bf16[480,384]{1,0:T(8,128)(2,1)S(1)}, u32[]{:S(2)}, u32[]{:S(2)}) collective-permute-start(bf16[480,384]{1,0:T(8,128)(2,1)S(1)} %pad_maximum_fusion.9), channel_id=1, source_target_pairs={{0,6},{1,7},{2,0},{3,1},{4,2},{5,3},{6,4},{7,5},{8,14},{9,15},{10,... | collective-permute-start | bytes 1105928 | tf_op jit(solution)/shard_map/ppermute | solution.py:470
  96.4 17.1 %collective-permute-start.25 = (bf16[2,2,3,48,768]{4,3,2,1,0:T(8,128)(2,1)S(1)}, bf16[2,2,3,48,768]{4,3,2,1,0:T(8,128)(2,1)}, u32[]{:S(2)}, u32[]{:S(2)}) collective-permute-start(bf16[2,2,3,48,768]{4,3,2,1,0:T(8,128)(2,1)S(1)} %pad_maximum_fusion.1.refs_3_), channel_id=1, source_target_pairs={{0,1},{1,0},{2,3},{3,2},{4,5},{5,4},{6,7},{7,6},{8,9},{9,8},{10,11... | collective-permute-start | bytes 2654216 | tf_op jit(solution)/shard_map/ppermute | solution.py:470
  186.4 17.1 %collective-permute-start.29 = (bf16[2,2,4,240,384]{4,3,2,1,0:T(8,128)(2,1)}, bf16[2,2,4,240,384]{4,3,2,1,0:T(8,128)(2,1)}, u32[]{:S(2)}, u32[]{:S(2)}) collective-permute-start(bf16[2,2,4,240,384]{4,3,2,1,0:T(8,128)(2,1)} %get-tuple-element.188), channel_id=1, source_target_pairs={{0,1},{1,0},{2,3},{3,2},{4,5},{5,4},{6,7},{7,6},{8,9},{9,8},{10,11... | collective-permute-start | bytes 8847368 | tf_op jit(solution)/shard_map/ppermute | solution.py:470
  201.6 20.8 %collective-permute-start.32 = (bf16[2,2,4,192,384]{4,3,2,1,0:T(8,128)(2,1)}, bf16[2,2,4,192,384]{4,3,2,1,0:T(8,128)(2,1)}, u32[]{:S(2)}, u32[]{:S(2)}) collective-permute-start(bf16[2,2,4,192,384]{4,3,2,1,0:T(8,128)(2,1)} %get-tuple-element.193), channel_id=1, source_target_pairs={{0,1},{1,0},{2,3},{3,2},{4,5},{5,4},{6,7},{7,6},{8,9},{9,8},{10,11... | collective-permute-start | bytes 7077896 | tf_op jit(solution)/shard_map/ppermute | solution.py:470
  206.4 21.1 %collective-permute-start.30 = (bf16[4,240,384]{2,1,0:T(8,128)(2,1)}, bf16[4,240,384]{2,1,0:T(8,128)(2,1)}, u32[]{:S(2)}, u32[]{:S(2)}) collective-permute-start(bf16[4,240,384]{2,1,0:T(8,128)(2,1)} %get-tuple-element.251), channel_id=1, source_target_pairs={{0,8},{1,9},{2,10},{3,11},{4,12},{5,13},{6,14},{7,15},{8,0},{9,1},... | collective-permute-start | bytes 2211848 | tf_op jit(solution)/shard_map/ppermute | solution.py:470
  207.8 19.6 %collective-permute-start.31 = (bf16[4,240,384]{2,1,0:T(8,128)(2,1)}, bf16[4,240,384]{2,1,0:T(8,128)(2,1)}, u32[]{:S(2)}, u32[]{:S(2)}) collective-permute-start(bf16[4,240,384]{2,1,0:T(8,128)(2,1)} %get-tuple-element.250), channel_id=1, source_target_pairs={{0,16},{1,17},{2,18},{3,19},{4,20},{5,21},{6,22},{7,23},{8,24},{9,... | collective-permute-start | bytes 2211848 | tf_op jit(solution)/shard_map/ppermute | solution.py:470
  225.4 31.9 %collective-permute-start.33 = (bf16[4,192,384]{2,1,0:T(8,128)(2,1)}, bf16[4,192,384]{2,1,0:T(8,128)(2,1)}, u32[]{:S(2)}, u32[]{:S(2)}) collective-permute-start(bf16[4,192,384]{2,1,0:T(8,128)(2,1)} %get-tuple-element.261), channel_id=1, source_target_pairs={{0,8},{1,9},{2,10},{3,11},{4,12},{5,13},{6,14},{7,15},{8,0},{9,1},... | collective-permute-start | bytes 1769480 | tf_op jit(solution)/shard_map/ppermute | solution.py:470
  226.1 31.2 %collective-permute-start.34 = (bf16[4,192,384]{2,1,0:T(8,128)(2,1)}, bf16[4,192,384]{2,1,0:T(8,128)(2,1)}, u32[]{:S(2)}, u32[]{:S(2)}) collective-permute-start(bf16[4,192,384]{2,1,0:T(8,128)(2,1)} %get-tuple-element.260), channel_id=1, source_target_pairs={{0,16},{1,17},{2,18},{3,19},{4,20},{5,21},{6,22},{7,23},{8,24},{9,... | collective-permute-start | bytes 1769480 | tf_op jit(solution)/shard_map/ppermute | solution.py:470
  231.6 41.7 %collective-permute-start.41 = (bf16[2,240,384]{2,1,0:T(8,128)(2,1)}, bf16[2,240,384]{2,1,0:T(8,128)(2,1)}, u32[]{:S(2)}, u32[]{:S(2)}) collective-permute-start(bf16[2,240,384]{2,1,0:T(8,128)(2,1)} %pad_maximum_fusion.12), channel_id=1, source_target_pairs={{0,6},{1,7},{2,0},{3,1},{4,2},{5,3},{6,4},{7,5},{8,14},{9,15},{10,... | collective-permute-start | bytes 1105928 | tf_op jit(solution)/shard_map/ppermute | solution.py:470
  241.2 32.2 %collective-permute-start.40 = (bf16[2,240,384]{2,1,0:T(8,128)(2,1)}, bf16[2,240,384]{2,1,0:T(8,128)(2,1)}, u32[]{:S(2)}, u32[]{:S(2)}) collective-permute-start(bf16[2,240,384]{2,1,0:T(8,128)(2,1)} %pad_maximum_fusion.11), channel_id=1, source_target_pairs={{0,4},{1,5},{2,6},{3,7},{4,0},{5,1},{6,2},{7,3},{8,12},{9,13},{10,... | collective-permute-start | bytes 1105928 | tf_op jit(solution)/shard_map/ppermute | solution.py:470
  243.1 30.2 %collective-permute-start.39 = (bf16[2,240,384]{2,1,0:T(8,128)(2,1)}, bf16[2,240,384]{2,1,0:T(8,128)(2,1)}, u32[]{:S(2)}, u32[]{:S(2)}) collective-permute-start(bf16[2,240,384]{2,1,0:T(8,128)(2,1)} %pad_maximum_fusion.10), channel_id=1, source_target_pairs={{0,2},{1,3},{2,4},{3,5},{4,6},{5,7},{6,0},{7,1},{8,10},{9,11},{10,... | collective-permute-start | bytes 1105928 | tf_op jit(solution)/shard_map/ppermute | solution.py:470
  257.3 23.5 %collective-permute-start.35 = (bf16[2,2,4,96,384]{4,3,2,1,0:T(8,128)(2,1)}, bf16[2,2,4,96,384]{4,3,2,1,0:T(8,128)(2,1)S(1)}, u32[]{:S(2)}, u32[]{:S(2)}) collective-permute-start(bf16[2,2,4,96,384]{4,3,2,1,0:T(8,128)(2,1)} %get-tuple-element.216), channel_id=1, source_target_pairs={{0,1},{1,0},{2,3},{3,2},{4,5},{5,4},{6,7},{7,6},{8,9},{9,8},{10,11... | collective-permute-start | bytes 3538952 | tf_op jit(solution)/shard_map/ppermute | solution.py:470
  281.0 25.5 %collective-permute-start.38 = (bf16[4,160,384]{2,1,0:T(8,128)(2,1)S(1)}, bf16[4,160,384]{2,1,0:T(8,128)(2,1)S(1)}, u32[]{:S(2)}, u32[]{:S(2)}) collective-permute-start(bf16[4,160,384]{2,1,0:T(8,128)(2,1)S(1)} %pad_maximum_fusion.5), channel_id=1, source_target_pairs={{0,16},{1,17},{2,18},{3,19},{4,20},{5,21},{6,22},{7,23},{8,24},{9,... | collective-permute-start | bytes 1474568 | tf_op jit(solution)/shard_map/ppermute | solution.py:470
  281.8 24.7 %collective-permute-start.37 = (bf16[4,160,384]{2,1,0:T(8,128)(2,1)S(1)}, bf16[4,160,384]{2,1,0:T(8,128)(2,1)S(1)}, u32[]{:S(2)}, u32[]{:S(2)}) collective-permute-start(bf16[4,160,384]{2,1,0:T(8,128)(2,1)S(1)} %pad_maximum_fusion.4), channel_id=1, source_target_pairs={{0,8},{1,9},{2,10},{3,11},{4,12},{5,13},{6,14},{7,15},{8,0},{9,1},... | collective-permute-start | bytes 1474568 | tf_op jit(solution)/shard_map/ppermute | solution.py:470
  283.2 23.3 %collective-permute-start.43 = (bf16[2,192,384]{2,1,0:T(8,128)(2,1)S(1)}, bf16[2,192,384]{2,1,0:T(8,128)(2,1)S(1)}, u32[]{:S(2)}, u32[]{:S(2)}) collective-permute-start(bf16[2,192,384]{2,1,0:T(8,128)(2,1)S(1)} %pad_maximum_fusion.15), channel_id=1, source_target_pairs={{0,4},{1,5},{2,6},{3,7},{4,0},{5,1},{6,2},{7,3},{8,12},{9,13},{10,... | collective-permute-start | bytes 884744 | tf_op jit(solution)/shard_map/ppermute | solution.py:470
  283.4 23.2 %collective-permute-start.42 = (bf16[2,192,384]{2,1,0:T(8,128)(2,1)S(1)}, bf16[2,192,384]{2,1,0:T(8,128)(2,1)S(1)}, u32[]{:S(2)}, u32[]{:S(2)}) collective-permute-start(bf16[2,192,384]{2,1,0:T(8,128)(2,1)S(1)} %pad_maximum_fusion.14), channel_id=1, source_target_pairs={{0,2},{1,3},{2,4},{3,5},{4,6},{5,7},{6,0},{7,1},{8,10},{9,11},{10,... | collective-permute-start | bytes 884744 | tf_op jit(solution)/shard_map/ppermute | solution.py:470
  309.4 19.5 %collective-permute-start.47 = (bf16[2,160,384]{2,1,0:T(8,128)(2,1)S(1)}, bf16[2,160,384]{2,1,0:T(8,128)(2,1)S(1)}, u32[]{:S(2)}, u32[]{:S(2)}) collective-permute-start(bf16[2,160,384]{2,1,0:T(8,128)(2,1)S(1)} %pad_maximum_fusion.19), channel_id=1, source_target_pairs={{0,6},{1,7},{2,0},{3,1},{4,2},{5,3},{6,4},{7,5},{8,14},{9,15},{10,... | collective-permute-start | bytes 737288 | tf_op jit(solution)/shard_map/ppermute | solution.py:470
  309.5 24.3 %collective-permute-start.46 = (bf16[2,160,384]{2,1,0:T(8,128)(2,1)S(1)}, bf16[2,160,384]{2,1,0:T(8,128)(2,1)S(1)}, u32[]{:S(2)}, u32[]{:S(2)}) collective-permute-start(bf16[2,160,384]{2,1,0:T(8,128)(2,1)S(1)} %pad_maximum_fusion.18), channel_id=1, source_target_pairs={{0,4},{1,5},{2,6},{3,7},{4,0},{5,1},{6,2},{7,3},{8,12},{9,13},{10,... | collective-permute-start | bytes 737288 | tf_op jit(solution)/shard_map/ppermute | solution.py:470
  318.5 15.2 %collective-permute-start.45 = (bf16[2,160,384]{2,1,0:T(8,128)(2,1)S(1)}, bf16[2,160,384]{2,1,0:T(8,128)(2,1)S(1)}, u32[]{:S(2)}, u32[]{:S(2)}) collective-permute-start(bf16[2,160,384]{2,1,0:T(8,128)(2,1)S(1)} %pad_maximum_fusion.17), channel_id=1, source_target_pairs={{0,2},{1,3},{2,4},{3,5},{4,6},{5,7},{6,0},{7,1},{8,10},{9,11},{10,... | collective-permute-start | bytes 737288 | tf_op jit(solution)/shard_map/ppermute | solution.py:470
  (69 other events, 597.5 us)
where the time goes:
time: 359 us; the launch traced here: 353 us
  Pallas kernels  161 us (45%)
  waiting for transfers between devices  89.1 us (25%)
  starting transfers between devices  57.8 us (16%)
  other arithmetic  24.7 us (7%)
  local copies, waits for them, and re-layouts  18.4 us (5%)
    ppermute x56, waiting for transfers between devices, send(): return lax.ppermute(a, AXES, where)  89.1 us
    ppermute x56, starting transfers between devices, send(): return lax.ppermute(a, AXES, where)  57.8 us
    pallas_call x3, Pallas kernels, attend_back(): pl.pallas_call(functools.partial(attend_back_kernel, mode), grid=(seqs,),...  43.6 us
    pallas_call x1, Pallas kernels, middle(): pl.pallas_call(functools.partial(middle_kernel, len(ctx)), grid=(rows //...  43.4 us
    pallas_call x3, Pallas kernels, attend(): pl.pallas_call(attend_kernel, grid=(seqs,), in_specs=[seq, col(0), col(1)...  23.8 us
    pallas_call x1, Pallas kernels, grad_down(): pl.pallas_call(functools.partial(grad_down_kernel, len(ctx)), grid_spec=p...  15.9 us
    convert_element_type x18, other arithmetic, total(): return out.astype(bf16)  14.9 us
    pallas_call x1, Pallas kernels, grad_up(): pl.pallas_call(grad_up_kernel, grid=(8,), in_specs=[SMEM, pl.BlockSpec((r...  14.7 us
  transfers between devices with their start and end apart: 56, of which 20 were waited for; matrix products, arithmetic and copies ran while one was open for 8% of the time, Pallas kernels for 27%

commit v1 on v0

--- a/solution.py
+++ b/solution.py
@@ -414,25 +414,26 @@
     res = nn(turned[...], gu[...]).astype(bf16)
     piece = res.shape[0] // 8
     half = piece // 2
-    h = j // 4
-    row = pl.multiple_of(lax.rem(j, 4) * half, 16)
+    h, l = j // 4, lax.rem(j // 2, 2)
+    row = pl.multiple_of(lax.rem(j, 2) * half, 16)
     for s in range(8):
         kk, far = owner_of(s, at_r)
-        for ab, turn in ((0, x), (1, y)):
+        for ab, turn, other_turn in ((0, x, y), (1, y, x)):
             val = res[s * piece + ab * half : s * piece + (ab + 1) * half]
+            one, two = lax.rem(h + turn, 2), lax.rem(l + other_turn, 2)
             for ref, cond in ((other_o, far), (own_o, ~far)):
 
                 @pl.when(cond)
-                def _(val=val, kk=kk, ab=ab, turn=turn, ref=ref):
-                    ref[ab, lax.rem(h + turn, 2), kk, pl.ds(row, half), :] = val
+                def _(val=val, kk=kk, ab=ab, one=one, two=two, ref=ref):
+                    ref[ab, one, two, kk, pl.ds(row, half), :] = val
 
 
 def grad_up(at, low, gu):
     rows, width = low.shape
     ff = gu.shape[1]
     step = ff // 8
-    part = (2, 2, 4, width // 4, ff // 8)
-    whole = pl.BlockSpec(part, lambda j: (0, 0, 0, 0, 0))
+    part = (2, 2, 2, 4, width // 8, ff // 8)
+    whole = pl.BlockSpec(part, lambda j: (0, 0, 0, 0, 0, 0))
     return pl.pallas_call(
         grad_up_kernel,
         grid=(8,),
@@ -569,7 +570,7 @@
 def finish_kernel(kind, at_r, *refs):
     y, x = at_r[0], at_r[1]
     blocks, outs = refs[:4], refs[4:]
-    for ab, turn in ((0, x), (1, y)):
+    for ab, turn, other_turn in ((0, x, y), (1, y, x)):
         one, two = (blocks[2 * ab + i][...].astype(f32) for i in range(2))
         left = jnp.where(turn == 0, one, two)
         right = jnp.where(turn == 0, two, one)
@@ -582,10 +583,12 @@
                 off += half
             half = outs[2].shape[0] // 2
             eighth = left.shape[1]
-            for i in range(4):
-                for h, val in ((0, left), (1, right)):
-                    col = (4 * h + i) * eighth
-                    outs[2][ab * half : (ab + 1) * half, col : col + eighth] = val[off + i * half : off + (i + 1) * half]
+            for h, val in ((0, left), (1, right)):
+                near, far = val[off : off + 2 * half], val[off + 2 * half : off + 4 * half]
+                quarters = jnp.where(other_turn == 0, near, far), jnp.where(other_turn == 0, far, near)
+                for i in range(4):
+                    row, col = i % 2 * half, (4 * h + i) * eighth
+                    outs[2][ab * half : (ab + 1) * half, col : col + eighth] = quarters[i // 2][row : row + half]
         else:
             half = outs[0].shape[0] // 2
             groups = outs[0].shape[1] // (3 * GW)
@@ -635,7 +638,7 @@
         self.got.append(send(other, CORE))
 
     def after(self, *values):
-        self.got, self.far, self.parts = tie((self.got, self.far, self.parts), *values)
+        self.got, self.far, self.parts, self.rest = tie((self.got, self.far, self.parts, self.rest), *values)
 
     far = parts = ()
 
@@ -655,7 +658,16 @@
         self.far = ()
         self.parts = [send(self.mine[k], SHIFT[k]) for k in range(1, 4)]
 
+    def joined(self, i):
+        one, two, rows = self.sent[i], self.far[i], self.rows
+        summed = total(one[:rows], two[:rows])
+        return jnp.concatenate([summed, one[rows:], two[rows:]], axis=0)
+
+    rest = ()
+
     def near(self, i, k):
+        if self.rest:
+            return total(self.rest[i][k], self.far[i][k])
         terms = []
         at = 0
         for o, g in zip(self.own, self.got):
@@ -664,15 +676,26 @@
             at += rows
         return terms[0] if len(terms) == 1 else jnp.concatenate(terms, axis=0)
 
-    def across(self, *more):
-        both = [total(v.mine[0], *v.parts) for v in (self,) + more]
-        both = both[0] if len(both) == 1 else jnp.concatenate(both, axis=1)
+    def quarter(self):
+        own, got, far = self.own[0], self.got[0], self.far
+        part = lambda i, j: total(own[i, 0, j], got[i, 0, j], far[i][j])
+        self.sent = part(0, 1), part(1, 1)
+        self.rest = part(0, 0), part(1, 0)
+        self.far = send(self.sent[0], ALONG), send(self.sent[1], ACROSS)
+
+    def across(self, more=None):
+        both = total(self.mine[0], *self.parts)
+        rows = both.shape[1]
+        if more is not None:
+            extra = total(more.mine[0], *more.parts)
+            both = jnp.concatenate([both, extra], axis=1)
         self.got = self.parts = ()
         self.sent = both[0], both[1]
         self.far = send(both[0], ALONG), send(both[1], ACROSS)
+        self.rows = rows
 
     def share(self):
-        a, b = (total(self.sent[i], self.far[i]) for i in range(2))
+        a, b = (self.joined(i) for i in range(2))
         self.sent = a, b
         self.out = a, send(a, ACROSS), b, send(b, ALONG)
 
@@ -737,15 +760,16 @@
     aq, ak = masks(segment_ids, valid)
     ring_u = jnp.stack(tie(ring_u, far_q))
     first_d = tie(halves(own_d, x, y), ring_u)
-    ring_d = [send(first_d, SHIFT[k]) for k in range(1, 4)]
+    d2 = send(first_d, SHIFT[2])
     a, b = ring_u[:, :half], ring_u[:, half:]
     a2, b2 = send(a, ACROSS), send(b, ALONG)
     saved = [attend(0, tie(tokens, a, b, first_d), wqkv, vecs, aq, ak, length)]
-    a2, b2 = tie((a2, b2), saved[0][3])
+    a2, b2, d2, first_d = tie((a2, b2, d2, first_d), saved[0][3])
     a3, b3 = jnp.stack([a, a2]), jnp.stack([b, b2])
     a4, b4 = send(a3, ALONG), send(b3, ACROSS)
-    saved.append(attend(1, tie(tokens, a3, b3), wqkv, vecs, aq, ak, length))
-    a4, b4, ring_d = tie((a4, b4, ring_d), saved[1][3])
+    d1, d3 = send(first_d, SHIFT[1]), send(first_d, SHIFT[3])
+    saved.append(attend(1, tie(tokens, a3, b3, d2), wqkv, vecs, aq, ak, length))
+    a4, b4, ring_d = tie((a4, b4, [d1, d2, d3]), saved[1][3])
     ring_d = jnp.stack(ring_d)
     ab4 = jnp.stack([a4, b4])
     far_d = spread_half(ring_d, dr + half)
@@ -778,17 +802,18 @@
     up.halve()
     dx = tie(dx, down.sent, up.sent)
     own, other, dx, db1 = attend_back("second", 1, at, saved[1], gc, aq, ak, tokens, wqkv, dx, length, (own, other))
-    qkv.add(own, other)
+    two = own, other
     up.after(dx)
+    up.quarter()
     wide = bup[0].reshape(8, 4, piece).transpose(1, 0, 2).reshape(4, width)
     table = jnp.concatenate([vec[:6], wide, jnp.zeros((4, width), f32)], axis=0)
     own, other, dx, _ = attend_back(
-        "third", 2, at, saved[2], gc, aq, ak, tokens, wqkv, tie(dx, up.far), length, (db0, db1, table)
+        "third", 2, at, saved[2], gc, aq, ak, tokens, wqkv, tie(dx, up.sent), length, (db0, db1, table)
     )
     down.after(dx)
-    qkv.after(dx)
+    qkv.add(two[0], tie(two[1], dx))
     qkv.add(own, other)
-    up.after(down.parts)
+    up.after(down.parts, dx)
     up.along_z()
     qkv.halve()
     up.after(qkv.far)

time: 359 us -> 342 us (0.953)
  waiting for transfers between devices: 89.1 us -> 79.9 us
  starting transfers between devices: 57.8 us -> 50 us
    ppermute x56 -> x58, waiting for transfers between devices: 89.1 us -> 79.9 us  [send(): return lax.ppermute(a, AXES, where)]
    ppermute x56 -> x58, starting transfers between devices: 57.8 us -> 50 us  [send(): return lax.ppermute(a, AXES, where)]
  transfers between devices with their start and end apart: 56 -> 58, of which waited for: 20 -> 22; matrix products, arithmetic and copies ran while one was open for 8% -> 8% of each run, Pallas kernels for 27% -> 28%
where the time goes in v1:
time: 342 us; the launch traced here: 336 us
  Pallas kernels  161 us (47%)
  waiting for transfers between devices  79.9 us (23%)
  starting transfers between devices  50 us (15%)
  other arithmetic  24.2 us (7%)
  local copies, waits for them, and re-layouts  18.8 us (5%)
    ppermute x58, waiting for transfers between devices, send(): return lax.ppermute(a, AXES, where)  79.9 us
    ppermute x58, starting transfers between devices, send(): return lax.ppermute(a, AXES, where)  50 us
    pallas_call x3, Pallas kernels, attend_back(): pl.pallas_call(functools.partial(attend_back_kernel, mode), grid=(seqs,),...  43.6 us
    pallas_call x1, Pallas kernels, middle(): pl.pallas_call(functools.partial(middle_kernel, len(ctx)), grid=(rows //...  43.3 us
    pallas_call x3, Pallas kernels, attend(): pl.pallas_call(attend_kernel, grid=(seqs,), in_specs=[seq, col(0), col(1)...  23.8 us
    pallas_call x1, Pallas kernels, grad_down(): pl.pallas_call(functools.partial(grad_down_kernel, len(ctx)), grid_spec=p...  15.9 us
    pallas_call x3, Pallas kernels, assemble(): pl.pallas_call(kernel, in_specs=[SMEM] + [VMEM] * len(parts), out_specs=[...  14.6 us
    pallas_call x1, Pallas kernels, grad_up(): pl.pallas_call(grad_up_kernel, grid=(8,), in_specs=[SMEM, pl.BlockSpec((r...  14.5 us
  transfers between devices with their start and end apart: 58, of which 22 were waited for; matrix products, arithmetic and copies ran while one was open for 8% of the time, Pallas kernels for 28%

profile of v1, /device:TPU:0, one launch (start us, length us, event | category | flops | bytes accessed | tf_op | source)
XLA Modules:
  0.0 335.7 jit_solution(4838012674333235128)
XLA Ops:
  10.1 5.1 %collective-permute-done = bf16[104,1152]{1,0:T(8,128)(2,1)} collective-permute-done((bf16[104,1152]{1,0:T(8,128)(2,1)}, bf16[104,1152]{1,0:T(8,128)(2,1)}, u32[]{:S(2)}, u32[]{:S(2)}) %collective-permute-start) | collective-permute-done | bytes 239648 | tf_op jit(solution)/shard_map/ppermute | solution.py:471
  16.3 8.0 %collective-permute-done.1 = bf16[104,1152]{1,0:T(8,128)(2,1)S(1)} collective-permute-done((bf16[104,1152]{1,0:T(8,128)(2,1)}, bf16[104,1152]{1,0:T(8,128)(2,1)S(1)}, u32[]{:S(2)}, u32[]{:S(2)}) %collective-permute-start.1) | collective-permute-done | bytes 239648 | tf_op jit(solution)/shard_map/ppermute | solution.py:471
  25.4 6.8 %collective-permute-done.5 = bf16[104,1152]{1,0:T(8,128)(2,1)S(1)} collective-permute-done((bf16[104,1152]{1,0:T(8,128)(2,1)S(1)}, bf16[104,1152]{1,0:T(8,128)(2,1)S(1)}, u32[]{:S(2)}, u32[]{:S(2)}) %collective-permute-start.5) | collective-permute-done | bytes 239648 | tf_op jit(solution)/shard_map/ppermute | solution.py:471
  36.4 3.7 %collective-permute-start.8 = (bf16[96,768]{1,0:T(8,128)(2,1)}, bf16[96,768]{1,0:T(8,128)(2,1)S(1)}, u32[]{:S(2)}, u32[]{:S(2)}) collective-permute-start(bf16[96,768]{1,0:T(8,128)(2,1)} %constant_dynamic-slice_fusion.2), channel_id=1, source_target_pairs={{0,6},{1,7},{2,0},{3,1},{4,2},{5,3},{6,4},{7,5},{8,14},{9,15},{10,... | collective-permute-start | bytes 442376 | tf_op jit(solution)/shard_map/ppermute | solution.py:471
  40.2 3.7 %collective-permute-done.6 = bf16[96,768]{1,0:T(8,128)(2,1)S(1)} collective-permute-done((bf16[96,768]{1,0:T(8,128)(2,1)}, bf16[96,768]{1,0:T(8,128)(2,1)S(1)}, u32[]{:S(2)}, u32[]{:S(2)}) %collective-permute-start.6) | collective-permute-done | bytes 147488 | tf_op jit(solution)/shard_map/ppermute | solution.py:471
  55.8 4.1 %assemble.3.wq.wk.wv = bf16[768,2304]{1,0:T(8,128)(2,1)} custom-call(s32[4]{0:T(128)} %pad_add_fusion.at_r, bf16[104,2304]{1,0:T(8,128)(2,1)} %copy-done.6, bf16[3,104,1152]{2,1,0:T(8,128)(2,1)} %copy-done.1, bf16[3,48,1152]{2,1,0:T(8,128)(2,1)} %collective-permute-done.9.refs_2_, bf16[3,48,1152]{2,1,0:T(8,128)(2,1)} %copy-done.27, ...), custom_call_target="tpu_custom_call" | custom-call | bytes 7077888 | tf_op jit(solution)/shard_map/assemble/pallas_call | solution.py:537
  59.9 7.9 %attend.3 = (bf16[1024,256]{1,0:T(8,128)(2,1)}, bf16[1024,256]{1,0:T(8,128)(2,1)}, bf16[1024,256]{1,0:T(8,128)(2,1)}, bf16[1024,256]{1,0:T(8,128)(2,1)}, f32[2,8,512]{2,1,0:T(8,128)}) custom-call(bf16[1024,768]{1,0:T(8,128)(2,1)} %tok.10, bf16[768,2304]{1,0:T(8,128)(2,1)} %assemble.3.wq.wk.wv, bf16[768,2304]{1,0:T(8,128)(2,1)} %assemble.3.wq.wk.wv, ...), custom_call_target="tpu_custom_call" | custom-call | flops 4000000000 | bytes 5000000 | tf_op jit(solution)/shard_map/attend/pallas_call | solution.py:80
  75.5 8.0 %attend.4 = (bf16[1024,256]{1,0:T(8,128)(2,1)}, bf16[1024,256]{1,0:T(8,128)(2,1)}, bf16[1024,256]{1,0:T(8,128)(2,1)}, bf16[1024,256]{1,0:T(8,128)(2,1)}, f32[2,8,512]{2,1,0:T(8,128)}) custom-call(bf16[1024,768]{1,0:T(8,128)(2,1)} %tok.10, bf16[768,2304]{1,0:T(8,128)(2,1)} %assemble.3.wq.wk.wv, bf16[768,2304]{1,0:T(8,128)(2,1)} %assemble.3.wq.wk.wv, ...), custom_call_target="tpu_custom_call" | custom-call | flops 4000000000 | bytes 5000000 | tf_op jit(solution)/shard_map/attend/pallas_call | solution.py:80
  84.8 6.0 %collective-permute-done.20 = bf16[480,384]{1,0:T(8,128)(2,1)S(1)} collective-permute-done((bf16[480,384]{1,0:T(8,128)(2,1)S(1)}, bf16[480,384]{1,0:T(8,128)(2,1)S(1)}, u32[]{:S(2)}, u32[]{:S(2)}) %collective-permute-start.20) | collective-permute-done | bytes 368672 | tf_op jit(solution)/shard_map/ppermute | solution.py:471
  95.0 7.9 %attend.5 = (bf16[1024,256]{1,0:T(8,128)(2,1)}, bf16[1024,256]{1,0:T(8,128)(2,1)}, bf16[1024,256]{1,0:T(8,128)(2,1)}, bf16[1024,256]{1,0:T(8,128)(2,1)}, f32[2,8,512]{2,1,0:T(8,128)}) custom-call(bf16[1024,768]{1,0:T(8,128)(2,1)} %tok.10, bf16[768,2304]{1,0:T(8,128)(2,1)} %assemble.3.wq.wk.wv, bf16[768,2304]{1,0:T(8,128)(2,1)} %assemble.3.wq.wk.wv, ...), custom_call_target="tpu_custom_call" | custom-call | flops 4000000000 | bytes 5000000 | tf_op jit(solution)/shard_map/attend/pallas_call | solution.py:80
  102.9 4.6 %collective-permute-done.21.refs_2_ = bf16[3,240,384]{2,1,0:T(8,128)(2,1)} collective-permute-done((bf16[3,240,384]{2,1,0:T(8,128)(2,1)S(1)}, bf16[3,240,384]{2,1,0:T(8,128)(2,1)}, u32[]{:S(2)}, u32[]{:S(2)}) %collective-permute-start.21) | collective-permute-done | bytes 552992 | tf_op jit(solution)/shard_map/ppermute | solution.py:471
  109.1 4.8 %assemble.4.refs_6_ = bf16[768,3072]{1,0:T(8,128)(2,1)} custom-call(s32[4]{0:T(128)} %pad_add_fusion.at_r, bf16[96,3072]{1,0:T(8,128)(2,1)} %refs_0_, bf16[2,3,48,768]{3,2,1,0:T(8,128)(2,1)} %copy-done.8, bf16[2,3,48,768]{3,2,1,0:T(8,128)(2,1)} %copy-done.7, bf16[2,2,3,48,768]{4,3,2,1,0:T(8,128)(2,1)} %copy-done.3, bf16[96,3072]{1,0:T(8,128)(2,1)} %copy-done.18, ...), custom_call_target="tpu_custom_call" | custom-call | bytes 9437184 | tf_op jit(solution)/shard_map/assemble/pallas_call | solution.py:537
  115.8 5.7 %assemble.5 = (bf16[3072,768]{1,0:T(8,128)(2,1)}, bf16[768,768]{1,0:T(8,128)(2,1)}) custom-call(s32[4]{0:T(128)} %pad_add_fusion.at_r, bf16[480,768]{1,0:T(8,128)(2,1)} %copy-done.2, bf16[3,480,384]{2,1,0:T(8,128)(2,1)} %copy-done, bf16[3,240,384]{2,1,0:T(8,128)(2,1)} %collective-permute-done.21.refs_2_, ...), custom_call_target="tpu_custom_call" | custom-call | bytes 11796480 | tf_op jit(solution)/shard_map/assemble/pallas_call | solution.py:537
  121.6 43.3 %middle.1 = (bf16[1024,768]{1,0:T(8,128)(2,1)}, bf16[1024,768]{1,0:T(8,128)(2,1)}, bf16[1024,3072]{1,0:T(8,128)(2,1)}, bf16[1024,768]{1,0:T(8,128)(2,1)}, bf16[1...) custom-call(bf16[1024,768]{1,0:T(8,128)(2,1)} %tok.10, ...), custom_call_target="tpu_custom_call" | custom-call | flops 30000001024 | bytes 40000000 | tf_op jit(solution)/shard_map/middle/pallas_call | solution.py:325
  164.9 15.9 %grad_down.1 = (bf16[2,2,4,240,384]{4,3,2,1,0:T(8,128)(2,1)}, bf16[2,2,4,240,384]{4,3,2,1,0:T(8,128)(2,1)}) custom-call(s32[4]{0:T(128)} %pad_add_fusion.at_r, bf16[1024,256]{1,0:T(8,128)(2,1)} %get-tuple-element.141.refs_0_.ctx_r, bf16[1024,256]{1,0:T(8,128)(2,1)} %get-tuple-element.146.refs_1_.ctx_r, bf16[1024,256]{1,0:T(8,128)(2,1)} %get-tuple-element.154.refs_2_.ctx_r, ...), custom_call_target="tpu_custom_call" | custom-call | flops 8999999488 | bytes 14000000 | tf_op jit(solution)/shard_map/grad_down/pallas_call | solution.py:391
  181.2 14.5 %grad_up.1 = (bf16[2,2,2,4,96,384]{5,4,3,2,1,0:T(8,128)(2,1)}, bf16[2,2,2,4,96,384]{5,4,3,2,1,0:T(8,128)(2,1)}) custom-call(s32[4]{0:T(128)} %pad_add_fusion.at_r, bf16[1024,768]{1,0:T(8,128)(2,1)} %get-tuple-element.196.low, bf16[1024,3072]{1,0:T(8,128)(2,1)} %get-tuple-element.197.gu), custom_call_target="tpu_custom_call" | custom-call | flops 8999999488 | bytes 14000000 | tf_op jit(solution)/shard_map/grad_up/pallas_call | solution.py:437
  202.4 14.0 %attend_back.3 = (bf16[2,2,4,96,384]{4,3,2,1,0:T(8,128)(2,1)}, bf16[2,2,4,96,384]{4,3,2,1,0:T(8,128)(2,1)}, f32[1024,768]{1,0:T(8,128)}, f32[1,768]{1,0:T(1,128)}) custom-call(s32[4]{0:T(128)} %pad_add_fusion.at_r, bf16[1024,256]{1,0:T(8,128)(2,1)} %get-tuple-element.186.q_r, bf16[1024,256]{1,0:T(8,128)(2,1)} %get-tuple-element.187.k_r, ...), custom_call_target="tpu_custom_call" | custom-call | flops 8000000000 | bytes 8000000 | tf_op jit(solution)/shard_map/attend_back/pallas_call | solution.py:227
  230.4 14.3 %attend_back.4 = (bf16[2,2,4,96,384]{4,3,2,1,0:T(8,128)(2,1)}, bf16[2,2,4,96,384]{4,3,2,1,0:T(8,128)(2,1)}, f32[1024,768]{1,0:T(8,128)}, f32[1,768]{1,0:T(1,128)}) custom-call(s32[4]{0:T(128)} %pad_add_fusion.at_r, bf16[1024,256]{1,0:T(8,128)(2,1)} %get-tuple-element.182.q_r, ...), custom_call_target="tpu_custom_call", output_to_operand_aliasing={{0}: (14, {}), {1}: (15, {})} | custom-call | flops 8000000000 | bytes 8000000 | tf_op jit(solution)/shard_map/attend_back/pallas_call | solution.py:227
  247.5 15.3 %attend_back.5 = (bf16[2,2,4,64,384]{4,3,2,1,0:T(8,128)(2,1)}, bf16[2,2,4,64,384]{4,3,2,1,0:T(8,128)(2,1)}, bf16[1024,768]{1,0:T(8,128)(2,1)}, f32[1,768]{1,0:T(1,128)}) custom-call(s32[4]{0:T(128)} %pad_add_fusion.at_r, bf16[1024,256]{1,0:T(8,128)(2,1)} %get-tuple-element.177.q_r, bf16[1024,256]{1,0:T(8,128)(2,1)} %get-tuple-element.178.k_r, ...), custom_call_target="tpu_custom_call" | custom-call | flops 8000000000 | bytes 8000000 | tf_op jit(solution)/shard_map/attend_back/pallas_call | solution.py:227
  265.0 7.3 %collective-permute-done.39 = bf16[4,96,384]{2,1,0:T(8,128)(2,1)S(1)} collective-permute-done((bf16[4,96,384]{2,1,0:T(8,128)(2,1)S(1)}, bf16[4,96,384]{2,1,0:T(8,128)(2,1)S(1)}, u32[]{:S(2)}, u32[]{:S(2)}) %collective-permute-start.39) | collective-permute-done | bytes 294944 | tf_op jit(solution)/shard_map/ppermute | solution.py:471
  273.3 3.5 %collective-permute-start.46 = (bf16[2,96,384]{2,1,0:T(8,128)(2,1)S(1)}, bf16[2,96,384]{2,1,0:T(8,128)(2,1)S(1)}, u32[]{:S(2)}, u32[]{:S(2)}) collective-permute-start(bf16[2,96,384]{2,1,0:T(8,128)(2,1)S(1)} %pad_maximum_fusion.21), channel_id=1, source_target_pairs={{0,6},{1,7},{2,0},{3,1},{4,2},{5,3},{6,4},{7,5},{8,14},{9,15},{10,... | collective-permute-start | bytes 442376 | tf_op jit(solution)/shard_map/ppermute | solution.py:471
  282.6 8.3 %collective-permute-done.45 = bf16[2,96,384]{2,1,0:T(8,128)(2,1)S(1)} collective-permute-done((bf16[2,96,384]{2,1,0:T(8,128)(2,1)S(1)}, bf16[2,96,384]{2,1,0:T(8,128)(2,1)S(1)}, u32[]{:S(2)}, u32[]{:S(2)}) %collective-permute-start.45) | collective-permute-done | bytes 147488 | tf_op jit(solution)/shard_map/ppermute | solution.py:471
  295.8 4.0 %collective-permute-done.52 = bf16[336,384]{1,0:T(8,128)(2,1)S(1)} collective-permute-done((bf16[336,384]{1,0:T(8,128)(2,1)S(1)}, bf16[336,384]{1,0:T(8,128)(2,1)S(1)}, u32[]{:S(2)}, u32[]{:S(2)}) %collective-permute-start.52) | collective-permute-done | bytes 258080 | tf_op jit(solution)/shard_map/ppermute | solution.py:471
  302.4 6.1 %collective-permute-done.53.refs_3_ = bf16[432,384]{1,0:T(8,128)(2,1)S(1)} collective-permute-done((bf16[432,384]{1,0:T(8,128)(2,1)S(1)}, bf16[432,384]{1,0:T(8,128)(2,1)S(1)}, u32[]{:S(2)}, u32[]{:S(2)}) %collective-permute-start.53) | collective-permute-done | bytes 331808 | tf_op jit(solution)/shard_map/ppermute | solution.py:471
  (288 shorter events, 110.9 us)
Async XLA Ops:
  8.3 15.9 %collective-permute-start.4 = (bf16[480,768]{1,0:T(8,128)(2,1)S(1)}, bf16[480,768]{1,0:T(8,128)(2,1)S(1)}, u32[]{:S(2)}, u32[]{:S(2)}) collective-permute-start(bf16[480,768]{1,0:T(8,128)(2,1)S(1)} %pad_maximum_fusion.2.refs_0_), channel_id=1, source_target_pairs={{0,1},{1,0},{2,3},{3,2},{4,5},{5,4},{6,7},{7,6},{8,9},{9,8},{10,11... | collective-permute-start | bytes 2211848 | tf_op jit(solution)/shard_map/ppermute | solution.py:471
  8.4 15.8 %collective-permute-start.2 = (bf16[104,2304]{1,0:T(8,128)(2,1)S(1)}, bf16[104,2304]{1,0:T(8,128)(2,1)}, u32[]{:S(2)}, u32[]{:S(2)}) collective-permute-start(bf16[104,2304]{1,0:T(8,128)(2,1)S(1)} %fusion.11.refs_0_), channel_id=1, source_target_pairs={{0,1},{1,0},{2,3},{3,2},{4,5},{5,4},{6,7},{7,6},{8,9},{9,8},{10,11... | collective-permute-start | bytes 1437704 | tf_op jit(solution)/shard_map/ppermute | solution.py:471
  9.3 14.9 %collective-permute-start.3 = (bf16[96,3072]{1,0:T(8,128)(2,1)S(1)}, bf16[96,3072]{1,0:T(8,128)(2,1)S(1)}, u32[]{:S(2)}, u32[]{:S(2)}) collective-permute-start(bf16[96,3072]{1,0:T(8,128)(2,1)S(1)} %copy-done.14), channel_id=1, source_target_pairs={{0,1},{1,0},{2,3},{3,2},{4,5},{5,4},{6,7},{7,6},{8,9},{9,8},{10,11... | collective-permute-start | bytes 1769480 | tf_op jit(solution)/shard_map/ppermute | solution.py:471
  49.6 19.4 %collective-permute-start.16 = (bf16[480,384]{1,0:T(8,128)(2,1)S(1)}, bf16[480,384]{1,0:T(8,128)(2,1)S(1)}, u32[]{:S(2)}, u32[]{:S(2)}) collective-permute-start(bf16[480,384]{1,0:T(8,128)(2,1)S(1)} %pad_maximum_fusion.9), channel_id=1, source_target_pairs={{0,4},{1,5},{2,6},{3,7},{4,0},{5,1},{6,2},{7,3},{8,12},{9,13},{10,... | collective-permute-start | bytes 1105928 | tf_op jit(solution)/shard_map/ppermute | solution.py:471
  51.9 15.9 %collective-permute-start.14 = (bf16[3,48,768]{2,1,0:T(8,128)(2,1)}, bf16[3,48,768]{2,1,0:T(8,128)(2,1)S(1)}, u32[]{:S(2)}, u32[]{:S(2)}) collective-permute-start(bf16[3,48,768]{2,1,0:T(8,128)(2,1)} %get-tuple-element.307), channel_id=1, source_target_pairs={{0,8},{1,9},{2,10},{3,11},{4,12},{5,13},{6,14},{7,15},{8,0},{9,1},... | collective-permute-start | bytes 663560 | tf_op jit(solution)/shard_map/ppermute | solution.py:471
  52.5 15.4 %collective-permute-start.15 = (bf16[3,48,768]{2,1,0:T(8,128)(2,1)}, bf16[3,48,768]{2,1,0:T(8,128)(2,1)S(1)}, u32[]{:S(2)}, u32[]{:S(2)}) collective-permute-start(bf16[3,48,768]{2,1,0:T(8,128)(2,1)} %get-tuple-element.306), channel_id=1, source_target_pairs={{0,16},{1,17},{2,18},{3,19},{4,20},{5,21},{6,22},{7,23},{8,24},{9,... | collective-permute-start | bytes 663560 | tf_op jit(solution)/shard_map/ppermute | solution.py:471
  69.8 21.0 %collective-permute-start.18 = (bf16[2,3,48,768]{3,2,1,0:T(8,128)(2,1)S(1)}, bf16[2,3,48,768]{3,2,1,0:T(8,128)(2,1)S(1)}, u32[]{:S(2)}, u32[]{:S(2)}) collective-permute-start(bf16[2,3,48,768]{3,2,1,0:T(8,128)(2,1)S(1)} %pad_maximum_fusion.8.refs_2_), channel_id=1, source_target_pairs={{0,8},{1,9},{2,10},{3,11},{4,12},{5,13},{6,14},{7,15},{8,0},{9,1},... | collective-permute-start | bytes 1327112 | tf_op jit(solution)/shard_map/ppermute | solution.py:471
  70.4 20.4 %collective-permute-start.17 = (bf16[2,3,48,768]{3,2,1,0:T(8,128)(2,1)S(1)}, bf16[2,3,48,768]{3,2,1,0:T(8,128)(2,1)S(1)}, u32[]{:S(2)}, u32[]{:S(2)}) collective-permute-start(bf16[2,3,48,768]{3,2,1,0:T(8,128)(2,1)S(1)} %pad_maximum_fusion.7.refs_1_), channel_id=1, source_target_pairs={{0,16},{1,17},{2,18},{3,19},{4,20},{5,21},{6,22},{7,23},{8,24},{9,... | collective-permute-start | bytes 1327112 | tf_op jit(solution)/shard_map/ppermute | solution.py:471
  73.0 17.8 %collective-permute-start.20 = (bf16[480,384]{1,0:T(8,128)(2,1)S(1)}, bf16[480,384]{1,0:T(8,128)(2,1)S(1)}, u32[]{:S(2)}, u32[]{:S(2)}) collective-permute-start(bf16[480,384]{1,0:T(8,128)(2,1)S(1)} %pad_maximum_fusion.9), channel_id=1, source_target_pairs={{0,6},{1,7},{2,0},{3,1},{4,2},{5,3},{6,4},{7,5},{8,14},{9,15},{10,... | collective-permute-start | bytes 1105928 | tf_op jit(solution)/shard_map/ppermute | solution.py:471
  90.9 16.9 %collective-permute-start.25 = (bf16[2,2,3,48,768]{4,3,2,1,0:T(8,128)(2,1)S(1)}, bf16[2,2,3,48,768]{4,3,2,1,0:T(8,128)(2,1)}, u32[]{:S(2)}, u32[]{:S(2)}) collective-permute-start(bf16[2,2,3,48,768]{4,3,2,1,0:T(8,128)(2,1)S(1)} %pad_maximum_fusion.1.refs_3_), channel_id=1, source_target_pairs={{0,1},{1,0},{2,3},{3,2},{4,5},{5,4},{6,7},{7,6},{8,9},{9,8},{10,11... | collective-permute-start | bytes 2654216 | tf_op jit(solution)/shard_map/ppermute | solution.py:471
  93.0 14.6 %collective-permute-start.21 = (bf16[3,240,384]{2,1,0:T(8,128)(2,1)S(1)}, bf16[3,240,384]{2,1,0:T(8,128)(2,1)}, u32[]{:S(2)}, u32[]{:S(2)}) collective-permute-start(bf16[3,240,384]{2,1,0:T(8,128)(2,1)S(1)} %get-tuple-element.287), channel_id=1, source_target_pairs={{0,8},{1,9},{2,10},{3,11},{4,12},{5,13},{6,14},{7,15},{8,0},{9,1},... | collective-permute-start | bytes 1658888 | tf_op jit(solution)/shard_map/ppermute | solution.py:471
  93.6 14.2 %collective-permute-start.22 = (bf16[3,240,384]{2,1,0:T(8,128)(2,1)S(1)}, bf16[3,240,384]{2,1,0:T(8,128)(2,1)}, u32[]{:S(2)}, u32[]{:S(2)}) collective-permute-start(bf16[3,240,384]{2,1,0:T(8,128)(2,1)S(1)} %get-tuple-element.286), channel_id=1, source_target_pairs={{0,16},{1,17},{2,18},{3,19},{4,20},{5,21},{6,22},{7,23},{8,24},{9,... | collective-permute-start | bytes 1658888 | tf_op jit(solution)/shard_map/ppermute | solution.py:471
  180.7 16.9 %collective-permute-start.29 = (bf16[2,2,4,240,384]{4,3,2,1,0:T(8,128)(2,1)}, bf16[2,2,4,240,384]{4,3,2,1,0:T(8,128)(2,1)}, u32[]{:S(2)}, u32[]{:S(2)}) collective-permute-start(bf16[2,2,4,240,384]{4,3,2,1,0:T(8,128)(2,1)} %get-tuple-element.193), channel_id=1, source_target_pairs={{0,1},{1,0},{2,3},{3,2},{4,5},{5,4},{6,7},{7,6},{8,9},{9,8},{10,11... | collective-permute-start | bytes 8847368 | tf_op jit(solution)/shard_map/ppermute | solution.py:471
  195.7 20.8 %collective-permute-start.32 = (bf16[2,2,2,4,96,384]{5,4,3,2,1,0:T(8,128)(2,1)}, bf16[2,2,2,4,96,384]{5,4,3,2,1,0:T(8,128)(2,1)}, u32[]{:S(2)}, u32[]{:S(2)}) collective-permute-start(bf16[2,2,2,4,96,384]{5,4,3,2,1,0:T(8,128)(2,1)} %get-tuple-element.198), channel_id=1, source_target_pairs={{0,1},{1,0},{2,3},{3,2},{4,5},{5,4},{6,7},{7,6},{8,9},{9,8},{10,11... | collective-permute-start | bytes 7077896 | tf_op jit(solution)/shard_map/ppermute | solution.py:471
  200.4 21.1 %collective-permute-start.30 = (bf16[4,240,384]{2,1,0:T(8,128)(2,1)}, bf16[4,240,384]{2,1,0:T(8,128)(2,1)}, u32[]{:S(2)}, u32[]{:S(2)}) collective-permute-start(bf16[4,240,384]{2,1,0:T(8,128)(2,1)} %get-tuple-element.257), channel_id=1, source_target_pairs={{0,8},{1,9},{2,10},{3,11},{4,12},{5,13},{6,14},{7,15},{8,0},{9,1},... | collective-permute-start | bytes 2211848 | tf_op jit(solution)/shard_map/ppermute | solution.py:471
  201.9 19.6 %collective-permute-start.31 = (bf16[4,240,384]{2,1,0:T(8,128)(2,1)}, bf16[4,240,384]{2,1,0:T(8,128)(2,1)}, u32[]{:S(2)}, u32[]{:S(2)}) collective-permute-start(bf16[4,240,384]{2,1,0:T(8,128)(2,1)} %get-tuple-element.256), channel_id=1, source_target_pairs={{0,16},{1,17},{2,18},{3,19},{4,20},{5,21},{6,22},{7,23},{8,24},{9,... | collective-permute-start | bytes 2211848 | tf_op jit(solution)/shard_map/ppermute | solution.py:471
  219.4 25.2 %collective-permute-start.33 = (bf16[2,4,96,384]{3,2,1,0:T(8,128)(2,1)}, bf16[2,4,96,384]{3,2,1,0:T(8,128)(2,1)}, u32[]{:S(2)}, u32[]{:S(2)}) collective-permute-start(bf16[2,4,96,384]{3,2,1,0:T(8,128)(2,1)} %get-tuple-element.265), channel_id=1, source_target_pairs={{0,8},{1,9},{2,10},{3,11},{4,12},{5,13},{6,14},{7,15},{8,0},{9,1},... | collective-permute-start | bytes 1769480 | tf_op jit(solution)/shard_map/ppermute | solution.py:471
  220.4 24.3 %collective-permute-start.34 = (bf16[2,4,96,384]{3,2,1,0:T(8,128)(2,1)}, bf16[2,4,96,384]{3,2,1,0:T(8,128)(2,1)}, u32[]{:S(2)}, u32[]{:S(2)}) collective-permute-start(bf16[2,4,96,384]{3,2,1,0:T(8,128)(2,1)} %get-tuple-element.264), channel_id=1, source_target_pairs={{0,16},{1,17},{2,18},{3,19},{4,20},{5,21},{6,22},{7,23},{8,24},{9,... | collective-permute-start | bytes 1769480 | tf_op jit(solution)/shard_map/ppermute | solution.py:471
  225.7 38.3 %collective-permute-start.43 = (bf16[2,240,384]{2,1,0:T(8,128)(2,1)}, bf16[2,240,384]{2,1,0:T(8,128)(2,1)S(1)}, u32[]{:S(2)}, u32[]{:S(2)}) collective-permute-start(bf16[2,240,384]{2,1,0:T(8,128)(2,1)} %pad_maximum_fusion.12), channel_id=1, source_target_pairs={{0,6},{1,7},{2,0},{3,1},{4,2},{5,3},{6,4},{7,5},{8,14},{9,15},{10,... | collective-permute-start | bytes 1105928 | tf_op jit(solution)/shard_map/ppermute | solution.py:471
  228.4 36.6 %collective-permute-start.42 = (bf16[2,240,384]{2,1,0:T(8,128)(2,1)}, bf16[2,240,384]{2,1,0:T(8,128)(2,1)}, u32[]{:S(2)}, u32[]{:S(2)}) collective-permute-start(bf16[2,240,384]{2,1,0:T(8,128)(2,1)} %pad_maximum_fusion.11), channel_id=1, source_target_pairs={{0,4},{1,5},{2,6},{3,7},{4,0},{5,1},{6,2},{7,3},{8,12},{9,13},{10,... | collective-permute-start | bytes 1105928 | tf_op jit(solution)/shard_map/ppermute | solution.py:471
  229.8 35.2 %collective-permute-start.41 = (bf16[2,240,384]{2,1,0:T(8,128)(2,1)}, bf16[2,240,384]{2,1,0:T(8,128)(2,1)}, u32[]{:S(2)}, u32[]{:S(2)}) collective-permute-start(bf16[2,240,384]{2,1,0:T(8,128)(2,1)} %pad_maximum_fusion.10), channel_id=1, source_target_pairs={{0,2},{1,3},{2,4},{3,5},{4,6},{5,7},{6,0},{7,1},{8,10},{9,11},{10,... | collective-permute-start | bytes 1105928 | tf_op jit(solution)/shard_map/ppermute | solution.py:471
  293.2 20.3 %collective-permute-start.49 = (bf16[2,160,384]{2,1,0:T(8,128)(2,1)S(1)}, bf16[2,160,384]{2,1,0:T(8,128)(2,1)S(1)}, u32[]{:S(2)}, u32[]{:S(2)}) collective-permute-start(bf16[2,160,384]{2,1,0:T(8,128)(2,1)S(1)} %pad_maximum_fusion.18), channel_id=1, source_target_pairs={{0,6},{1,7},{2,0},{3,1},{4,2},{5,3},{6,4},{7,5},{8,14},{9,15},{10,... | collective-permute-start | bytes 737288 | tf_op jit(solution)/shard_map/ppermute | solution.py:471
  294.1 22.9 %collective-permute-start.48 = (bf16[2,160,384]{2,1,0:T(8,128)(2,1)S(1)}, bf16[2,160,384]{2,1,0:T(8,128)(2,1)S(1)}, u32[]{:S(2)}, u32[]{:S(2)}) collective-permute-start(bf16[2,160,384]{2,1,0:T(8,128)(2,1)S(1)} %pad_maximum_fusion.17), channel_id=1, source_target_pairs={{0,4},{1,5},{2,6},{3,7},{4,0},{5,1},{6,2},{7,3},{8,12},{9,13},{10,... | collective-permute-start | bytes 737288 | tf_op jit(solution)/shard_map/ppermute | solution.py:471
  302.2 14.7 %collective-permute-start.47 = (bf16[2,160,384]{2,1,0:T(8,128)(2,1)S(1)}, bf16[2,160,384]{2,1,0:T(8,128)(2,1)S(1)}, u32[]{:S(2)}, u32[]{:S(2)}) collective-permute-start(bf16[2,160,384]{2,1,0:T(8,128)(2,1)S(1)} %pad_maximum_fusion.16), channel_id=1, source_target_pairs={{0,2},{1,3},{2,4},{3,5},{4,6},{5,7},{6,0},{7,1},{8,10},{9,11},{10,... | collective-permute-start | bytes 737288 | tf_op jit(solution)/shard_map/ppermute | solution.py:471
  (73 other events, 628.2 us)

commit v2 on v1

--- a/solution.py
+++ b/solution.py
@@ -251,12 +251,26 @@
     return 0.5 * (1.0 + lax.erf(x * 0.7071067811865476)), jnp.exp(-0.5 * x * x) * 0.3989422804014327
 
 
-def middle_kernel(groups, tok, *refs):
+def middle_kernel(groups, split, at_r, tok, *refs):
     ctx_r = refs[:groups]
-    cot, wo, vecs, wu, bu, wd, out_o, low_o, hid_o, gd_o, gu_o, gb_o, gc_o, vec_o, bup_o, slope = refs[groups:]
+    cot, vecs, bu = refs[groups : groups + 3]
+    refs = refs[groups + 3 :]
     i = pl.program_id(0)
+    if split:
+        up_parts, down_parts, refs = refs[:8], refs[8:16], refs[16:]
+        wu, wd, wo = refs[-3:]
+        refs = refs[:-3]
+
+        @pl.when(i == 0)
+        def _():
+            assemble_quarter_kernel(at_r, *up_parts, wu)
+            assemble_half_kernel(split, at_r, *down_parts, wd, wo)
+
+    else:
+        wu, wd, wo, refs = *refs[:3], refs[3:]
+    out_o, low_o, hid_o, gd_o, gu_o, gb_o, gc_o, vec_o, bup_o, slope = refs
     width = tok.shape[1]
-    ff = wd.shape[0]
+    ff = bu.shape[1]
     step = width
     chunks = ff // step
     bo, g1, s1, bd, g2, s2 = (vecs[j : j + 1, :].astype(f32) for j in range(2, 8))
@@ -314,25 +328,29 @@
         put(vec_o, (slice(at, at + 1), slice(None)), total(v))
 
 
-def middle(tokens, ctx, cot, wo, vecs, wu, bu, wd, tile=256):
+def middle(at, tokens, ctx, cot, vecs, bu, weights, split=None, tile=256):
     rows, width = tokens.shape
-    ff = wd.shape[0]
+    ff = bu.shape[1]
     act = pl.BlockSpec((tile, width), lambda i: (i, 0))
     wide = pl.BlockSpec((tile, ff), lambda i: (i, 0))
-    whole = lambda a: pl.BlockSpec(a.shape, lambda i: (0, 0), pipeline_mode=pl.Buffered(1))
+    whole = lambda a: pl.BlockSpec(a.shape, lambda i: (0,) * a.ndim, pipeline_mode=pl.Buffered(1))
     S = jax.ShapeDtypeStruct
     shapes = [(rows, width), (rows, width), (rows, ff), (rows, width), (rows, ff), (rows, width), (rows, width)]
+    scratch = [pltpu.VMEM((tile, ff), f32)]
+    if split:
+        scratch += [pltpu.VMEM(s, bf16) for s in ((width, ff), (ff, width), (width, width))]
+    blocks = [pl.BlockSpec((tile, GW), lambda i: (i, 0)) for _ in ctx]
     return pl.pallas_call(
-        functools.partial(middle_kernel, len(ctx)),
+        functools.partial(middle_kernel, len(ctx), split),
         grid=(rows // tile,),
-        in_specs=[act] + [pl.BlockSpec((tile, GW), lambda i: (i, 0)) for _ in ctx] + [act] + [whole(a) for a in (wo, vecs, wu, bu, wd)],
+        in_specs=[SMEM, act] + blocks + [act] + [whole(a) for a in (vecs, bu) + weights],
         out_specs=[act, act, wide, act, wide, act, act, pl.BlockSpec((8, width), lambda i: (0, 0)), pl.BlockSpec((8, ff), lambda i: (0, 0))],
         out_shape=[S(s, bf16) for s in shapes] + [S((8, width), f32), S((8, ff), f32)],
-        scratch_shapes=[pltpu.VMEM((tile, ff), f32)],
+        scratch_shapes=scratch,
         compiler_params=params(),
         cost_estimate=cost(30_000_000_000, 40_000_000),
         name="middle",
-    )(tokens, *ctx, cot, wo, vecs, wu, bu, wd)
+    )(at, tokens, *ctx, cot, vecs, bu, *weights)
 
 
 def grad_down_kernel(groups, at_r, *refs):
@@ -768,25 +786,22 @@
     a3, b3 = jnp.stack([a, a2]), jnp.stack([b, b2])
     a4, b4 = send(a3, ALONG), send(b3, ACROSS)
     d1, d3 = send(first_d, SHIFT[1]), send(first_d, SHIFT[3])
+    other_a = send(a3, CORE)
     saved.append(attend(1, tie(tokens, a3, b3, d2), wqkv, vecs, aq, ak, length))
-    a4, b4, ring_d = tie((a4, b4, [d1, d2, d3]), saved[1][3])
+    a4, b4, other_a, ring_d = tie((a4, b4, other_a, [d1, d2, d3]), saved[1][3])
     ring_d = jnp.stack(ring_d)
     ab4 = jnp.stack([a4, b4])
     far_d = spread_half(ring_d, dr + half)
-    rest_u = swap((a3, b3, ab4))
+    other_b, other_ab, other_ring = swap((b3, ab4, ring_d))
     saved.append(attend(2, tie(tokens, ring_d, ab4), wqkv, vecs, aq, ak, length))
-    far_d, rest_u = tie((far_d, rest_u), saved[2][3])
-    rest_d = swap(tie((ring_d,) + far_d, rest_u))
-    (wu,) = assemble(assemble_quarter_kernel, at, tie((up_weight, a3, b3, ab4, other_u) + rest_u, far_d), [(width, ff)])
-    wd, wo = assemble(
-        functools.partial(assemble_half_kernel, [2 * dr, piece]),
-        at,
-        (own_d, ring_d) + far_d + (other_d,) + tie(rest_d, wu),
-        [(ff, width), (width, width)],
+    far_d, other_b, other_ab, other_ring = tie((far_d, other_b, other_ab, other_ring), saved[2][3])
+    parts_u = (up_weight, a3, b3, ab4, other_u, other_a, other_b, other_ab)
+    parts_d = (own_d, ring_d) + far_d + (other_d, other_ring) + swap(far_d)
+
+    ctx = [f[3] for f in saved]
+    result, low, hid, gd, gu, gb, gc, vec, bup = middle(
+        at, tokens, ctx, cotangent, vecs, bu, parts_u + parts_d, (2 * dr, piece)
     )
-
-    ctx = [f[3] for f in saved]
-    result, low, hid, gd, gu, gb, gc, vec, bup = middle(tokens, ctx, cotangent, wo, vecs, wu, bu, wd)
 
     down, up, qkv = Sum(), Sum(), Sum()
     own, other = grad_down(at, ctx, gb, hid, gd)
@@ -811,9 +826,11 @@
         "third", 2, at, saved[2], gc, aq, ak, tokens, wqkv, tie(dx, up.sent), length, (db0, db1, table)
     )
     down.after(dx)
-    qkv.add(two[0], tie(two[1], dx))
+    up.after(dx)
+    other, first_other = tie((other, two[1]), up.far)
+    qkv.add(two[0], first_other)
     qkv.add(own, other)
-    up.after(down.parts, dx)
+    up.after(down.parts)
     up.along_z()
     qkv.halve()
     up.after(qkv.far)
@@ -888,7 +905,7 @@
     aq, ak = masks(segment_ids, valid)
     saved = [attend(g, tokens, wqkv, vecs, aq, ak, length) for g in range(groups)]
     ctx = [f[3] for f in saved]
-    result, low, hid, gd, gu, gb, gc, vec, bup = middle(tokens, ctx, cotangent, wo, vecs, wu, bu[None], wd)
+    result, low, hid, gd, gu, gb, gc, vec, bup = middle(at, tokens, ctx, cotangent, vecs, bu[None], (wu, wd, wo))
     dwd = tn(hid, gd).astype(bf16)
     dwu = tn(low, gu).astype(bf16)
     dwo = tn(jnp.concatenate(ctx, axis=1), gb).astype(bf16)

time: 342 us -> 329 us (0.962)
  Pallas kernels: 161 us -> 151 us
  waiting for transfers between devices: 79.9 us -> 71.5 us
  starting transfers between devices: 50 us -> 53.9 us
    pallas_call x3 -> x1, Pallas kernels: 14.6 us -> 4 us  [assemble(): pl.pallas_call(kernel, in_specs=[SMEM] + [VMEM] * len(parts), out_specs=[...]
    ppermute x58, waiting for transfers between devices: 79.9 us -> 71.5 us  [send(): return lax.ppermute(a, AXES, where)]
    ppermute x58, starting transfers between devices: 50 us -> 53.9 us  [send(): return lax.ppermute(a, AXES, where)]
  transfers between devices with their start and end apart: 58 -> 58, of which waited for: 22 -> 21; matrix products, arithmetic and copies ran while one was open for 8% -> 10% of each run, Pallas kernels for 28% -> 28%
where the time goes in v2:
time: 329 us; the launch traced here: 323 us
  Pallas kernels  151 us (46%)
  waiting for transfers between devices  71.5 us (22%)
  starting transfers between devices  53.9 us (16%)
  other arithmetic  26.5 us (8%)
  local copies, waits for them, and re-layouts  17.2 us (5%)
    ppermute x58, waiting for transfers between devices, send(): return lax.ppermute(a, AXES, where)  71.5 us
    ppermute x58, starting transfers between devices, send(): return lax.ppermute(a, AXES, where)  53.9 us
    pallas_call x1, Pallas kernels, middle(): pl.pallas_call(functools.partial(middle_kernel, len(ctx), split), grid=(r...  44.1 us
    pallas_call x3, Pallas kernels, attend_back(): pl.pallas_call(functools.partial(attend_back_kernel, mode), grid=(seqs,),...  43.6 us
    pallas_call x3, Pallas kernels, attend(): pl.pallas_call(attend_kernel, grid=(seqs,), in_specs=[seq, col(0), col(1)...  23.7 us
    pallas_call x1, Pallas kernels, grad_down(): pl.pallas_call(functools.partial(grad_down_kernel, len(ctx)), grid_spec=p...  15.9 us
    pallas_call x1, Pallas kernels, grad_up(): pl.pallas_call(grad_up_kernel, grid=(8,), in_specs=[SMEM, pl.BlockSpec((r...  14.8 us
    convert_element_type x18, other arithmetic, total(): return out.astype(bf16)  14.3 us
  transfers between devices with their start and end apart: 58, of which 21 were waited for; matrix products, arithmetic and copies ran while one was open for 10% of the time, Pallas kernels for 28%

profile of v2, /device:TPU:0, one launch (start us, length us, event | category | flops | bytes accessed | tf_op | source)
XLA Modules:
  0.0 323.1 jit_solution(12138870108656437943)
XLA Ops:
  3.3 3.1 collective-permute-start
  10.0 4.3 %collective-permute-done = bf16[104,1152]{1,0:T(8,128)(2,1)S(1)} collective-permute-done((bf16[104,1152]{1,0:T(8,128)(2,1)S(1)}, bf16[104,1152]{1,0:T(8,128)(2,1)S(1)}, u32[]{:S(2)}, u32[]{:S(2)}) %collective-permute-start) | collective-permute-done | bytes 239648 | tf_op jit(solution)/shard_map/ppermute | solution.py:489
  15.8 7.2 %collective-permute-done.1 = bf16[104,1152]{1,0:T(8,128)(2,1)S(1)} collective-permute-done((bf16[104,1152]{1,0:T(8,128)(2,1)S(1)}, bf16[104,1152]{1,0:T(8,128)(2,1)S(1)}, u32[]{:S(2)}, u32[]{:S(2)}) %collective-permute-start.1) | collective-permute-done | bytes 239648 | tf_op jit(solution)/shard_map/ppermute | solution.py:489
  24.3 6.8 %collective-permute-done.5 = bf16[104,1152]{1,0:T(8,128)(2,1)S(1)} collective-permute-done((bf16[104,1152]{1,0:T(8,128)(2,1)S(1)}, bf16[104,1152]{1,0:T(8,128)(2,1)S(1)}, u32[]{:S(2)}, u32[]{:S(2)}) %collective-permute-start.5) | collective-permute-done | bytes 239648 | tf_op jit(solution)/shard_map/ppermute | solution.py:489
  35.5 3.7 %collective-permute-start.8 = (bf16[96,768]{1,0:T(8,128)(2,1)}, bf16[96,768]{1,0:T(8,128)(2,1)S(1)}, u32[]{:S(2)}, u32[]{:S(2)}) collective-permute-start(bf16[96,768]{1,0:T(8,128)(2,1)} %constant_dynamic-slice_fusion.2), channel_id=1, source_target_pairs={{0,6},{1,7},{2,0},{3,1},{4,2},{5,3},{6,4},{7,5},{8,14},{9,15},{10,... | collective-permute-start | bytes 442376 | tf_op jit(solution)/shard_map/ppermute | solution.py:489
  39.9 3.3 %collective-permute-done.6 = bf16[96,768]{1,0:T(8,128)(2,1)} collective-permute-done((bf16[96,768]{1,0:T(8,128)(2,1)}, bf16[96,768]{1,0:T(8,128)(2,1)}, u32[]{:S(2)}, u32[]{:S(2)}) %collective-permute-start.6) | collective-permute-done | bytes 147488 | tf_op jit(solution)/shard_map/ppermute | solution.py:489
  43.2 3.4 %collective-permute-done.7 = bf16[96,768]{1,0:T(8,128)(2,1)} collective-permute-done((bf16[96,768]{1,0:T(8,128)(2,1)}, bf16[96,768]{1,0:T(8,128)(2,1)}, u32[]{:S(2)}, u32[]{:S(2)}) %collective-permute-start.7) | collective-permute-done | bytes 147488 | tf_op jit(solution)/shard_map/ppermute | solution.py:489
  55.5 4.0 %assemble.1.wq.wk.wv = bf16[768,2304]{1,0:T(8,128)(2,1)} custom-call(s32[4]{0:T(128)} %pad_add_fusion.at_r, bf16[104,2304]{1,0:T(8,128)(2,1)} %copy-done.4, bf16[3,104,1152]{2,1,0:T(8,128)(2,1)} %copy-done, bf16[3,48,1152]{2,1,0:T(8,128)(2,1)} %copy-done.23, bf16[3,48,1152]{2,1,0:T(8,128)(2,1)} %copy-done.22, bf16[104,2304]{1,0:T(8,128)(2,1)} %copy-done.13, ...), custom_call_target="tpu_custom_call" | custom-call | bytes 7077888 | tf_op jit(solution)/shard_map/assemble/pallas_call | solution.py:555
  59.5 7.9 %attend.3 = (bf16[1024,256]{1,0:T(8,128)(2,1)}, bf16[1024,256]{1,0:T(8,128)(2,1)}, bf16[1024,256]{1,0:T(8,128)(2,1)}, bf16[1024,256]{1,0:T(8,128)(2,1)}, f32[2,8,512]{2,1,0:T(8,128)}) custom-call(bf16[1024,768]{1,0:T(8,128)(2,1)} %tok.10, bf16[768,2304]{1,0:T(8,128)(2,1)} %assemble.1.wq.wk.wv, bf16[768,2304]{1,0:T(8,128)(2,1)} %assemble.1.wq.wk.wv, ...), custom_call_target="tpu_custom_call" | custom-call | flops 4000000000 | bytes 5000000 | tf_op jit(solution)/shard_map/attend/pallas_call | solution.py:80
  76.4 7.9 %attend.4 = (bf16[1024,256]{1,0:T(8,128)(2,1)}, bf16[1024,256]{1,0:T(8,128)(2,1)}, bf16[1024,256]{1,0:T(8,128)(2,1)}, bf16[1024,256]{1,0:T(8,128)(2,1)}, f32[2,8,512]{2,1,0:T(8,128)}) custom-call(bf16[1024,768]{1,0:T(8,128)(2,1)} %tok.10, bf16[768,2304]{1,0:T(8,128)(2,1)} %assemble.1.wq.wk.wv, bf16[768,2304]{1,0:T(8,128)(2,1)} %assemble.1.wq.wk.wv, ...), custom_call_target="tpu_custom_call" | custom-call | flops 4000000000 | bytes 5000000 | tf_op jit(solution)/shard_map/attend/pallas_call | solution.py:80
  85.7 7.2 %collective-permute-done.21 = bf16[480,384]{1,0:T(8,128)(2,1)S(1)} collective-permute-done((bf16[480,384]{1,0:T(8,128)(2,1)S(1)}, bf16[480,384]{1,0:T(8,128)(2,1)S(1)}, u32[]{:S(2)}, u32[]{:S(2)}) %collective-permute-start.21) | collective-permute-done | bytes 368672 | tf_op jit(solution)/shard_map/ppermute | solution.py:489
  95.5 7.9 %attend.5 = (bf16[1024,256]{1,0:T(8,128)(2,1)}, bf16[1024,256]{1,0:T(8,128)(2,1)}, bf16[1024,256]{1,0:T(8,128)(2,1)}, bf16[1024,256]{1,0:T(8,128)(2,1)}, f32[2,8,512]{2,1,0:T(8,128)}) custom-call(bf16[1024,768]{1,0:T(8,128)(2,1)} %tok.10, bf16[768,2304]{1,0:T(8,128)(2,1)} %assemble.1.wq.wk.wv, bf16[768,2304]{1,0:T(8,128)(2,1)} %assemble.1.wq.wk.wv, ...), custom_call_target="tpu_custom_call" | custom-call | flops 4000000000 | bytes 5000000 | tf_op jit(solution)/shard_map/attend/pallas_call | solution.py:80
  103.4 5.5 %collective-permute-done.22.refs_16_ = bf16[3,240,384]{2,1,0:T(8,128)(2,1)} collective-permute-done((bf16[3,240,384]{2,1,0:T(8,128)(2,1)S(1)}, bf16[3,240,384]{2,1,0:T(8,128)(2,1)}, u32[]{:S(2)}, u32[]{:S(2)}) %collective-permute-start.22) | collective-permute-done | bytes 552992 | tf_op jit(solution)/shard_map/ppermute | solution.py:489
  112.9 44.1 %middle.1 = (bf16[1024,768]{1,0:T(8,128)(2,1)}, bf16[1024,768]{1,0:T(8,128)(2,1)}, bf16[1024,3072]{1,0:T(8,128)(2,1)}, bf16[1024,768]{1,0:T(8,128)(2,1)}, bf16[1...) custom-call(s32[4]{0:T(128)} %pad_add_fusion.at_r, ...), custom_call_target="tpu_custom_call" | custom-call | flops 30000001024 | bytes 40000000 | tf_op jit(solution)/shard_map/middle/pallas_call | solution.py:343
  157.0 15.9 %grad_down.1 = (bf16[2,2,4,240,384]{4,3,2,1,0:T(8,128)(2,1)}, bf16[2,2,4,240,384]{4,3,2,1,0:T(8,128)(2,1)}) custom-call(s32[4]{0:T(128)} %pad_add_fusion.at_r, bf16[1024,256]{1,0:T(8,128)(2,1)} %get-tuple-element.131.refs_0_.ctx_r, bf16[1024,256]{1,0:T(8,128)(2,1)} %get-tuple-element.136.refs_1_.ctx_r, bf16[1024,256]{1,0:T(8,128)(2,1)} %get-tuple-element.144.refs_2_.ctx_r, ...), custom_call_target="tpu_custom_call" | custom-call | flops 8999999488 | bytes 14000000 | tf_op jit(solution)/shard_map/grad_down/pallas_call | solution.py:409
  173.1 14.8 %grad_up.1 = (bf16[2,2,2,4,96,384]{5,4,3,2,1,0:T(8,128)(2,1)}, bf16[2,2,2,4,96,384]{5,4,3,2,1,0:T(8,128)(2,1)}) custom-call(s32[4]{0:T(128)} %pad_add_fusion.at_r, bf16[1024,768]{1,0:T(8,128)(2,1)} %get-tuple-element.171.low, bf16[1024,3072]{1,0:T(8,128)(2,1)} %get-tuple-element.172.gu), custom_call_target="tpu_custom_call" | custom-call | flops 8999999488 | bytes 14000000 | tf_op jit(solution)/shard_map/grad_up/pallas_call | solution.py:455
  195.0 13.9 %attend_back.3 = (bf16[2,2,4,96,384]{4,3,2,1,0:T(8,128)(2,1)}, bf16[2,2,4,96,384]{4,3,2,1,0:T(8,128)(2,1)}, f32[1024,768]{1,0:T(8,128)}, f32[1,768]{1,0:T(1,128)}) custom-call(s32[4]{0:T(128)} %pad_add_fusion.at_r, bf16[1024,256]{1,0:T(8,128)(2,1)} %get-tuple-element.161.q_r, bf16[1024,256]{1,0:T(8,128)(2,1)} %get-tuple-element.162.k_r, ...), custom_call_target="tpu_custom_call" | custom-call | flops 8000000000 | bytes 8000000 | tf_op jit(solution)/shard_map/attend_back/pallas_call | solution.py:227
  222.9 14.4 %attend_back.4 = (bf16[2,2,4,96,384]{4,3,2,1,0:T(8,128)(2,1)}, bf16[2,2,4,96,384]{4,3,2,1,0:T(8,128)(2,1)}, f32[1024,768]{1,0:T(8,128)}, f32[1,768]{1,0:T(1,128)}) custom-call(s32[4]{0:T(128)} %pad_add_fusion.at_r, bf16[1024,256]{1,0:T(8,128)(2,1)} %get-tuple-element.157.q_r, ...), custom_call_target="tpu_custom_call", output_to_operand_aliasing={{0}: (14, {}), {1}: (15, {})} | custom-call | flops 8000000000 | bytes 8000000 | tf_op jit(solution)/shard_map/attend_back/pallas_call | solution.py:227
  242.1 15.3 %attend_back.5 = (bf16[2,2,4,64,384]{4,3,2,1,0:T(8,128)(2,1)}, bf16[2,2,4,64,384]{4,3,2,1,0:T(8,128)(2,1)}, bf16[1024,768]{1,0:T(8,128)(2,1)}, f32[1,768]{1,0:T(1,128)}) custom-call(s32[4]{0:T(128)} %pad_add_fusion.at_r, bf16[1024,256]{1,0:T(8,128)(2,1)} %get-tuple-element.152.q_r, bf16[1024,256]{1,0:T(8,128)(2,1)} %get-tuple-element.153.k_r, ...), custom_call_target="tpu_custom_call" | custom-call | flops 8000000000 | bytes 8000000 | tf_op jit(solution)/shard_map/attend_back/pallas_call | solution.py:227
  258.3 3.2 collective-permute-start.46
  269.1 7.6 %collective-permute-done.45 = bf16[2,96,384]{2,1,0:T(8,128)(2,1)S(1)} collective-permute-done((bf16[2,96,384]{2,1,0:T(8,128)(2,1)S(1)}, bf16[2,96,384]{2,1,0:T(8,128)(2,1)S(1)}, u32[]{:S(2)}, u32[]{:S(2)}) %collective-permute-start.45) | collective-permute-done | bytes 147488 | tf_op jit(solution)/shard_map/ppermute | solution.py:489
  282.5 3.3 %collective-permute-done.52 = bf16[336,384]{1,0:T(8,128)(2,1)S(1)} collective-permute-done((bf16[336,384]{1,0:T(8,128)(2,1)S(1)}, bf16[336,384]{1,0:T(8,128)(2,1)S(1)}, u32[]{:S(2)}, u32[]{:S(2)}) %collective-permute-start.52) | collective-permute-done | bytes 258080 | tf_op jit(solution)/shard_map/ppermute | solution.py:489
  289.1 4.6 %collective-permute-done.53.refs_3_ = bf16[432,384]{1,0:T(8,128)(2,1)S(1)} collective-permute-done((bf16[432,384]{1,0:T(8,128)(2,1)S(1)}, bf16[432,384]{1,0:T(8,128)(2,1)S(1)}, u32[]{:S(2)}, u32[]{:S(2)}) %collective-permute-start.53) | collective-permute-done | bytes 331808 | tf_op jit(solution)/shard_map/ppermute | solution.py:489
  298.1 4.5 %collective-permute-done.48 = bf16[2,160,384]{2,1,0:T(8,128)(2,1)S(1)} collective-permute-done((bf16[2,160,384]{2,1,0:T(8,128)(2,1)S(1)}, bf16[2,160,384]{2,1,0:T(8,128)(2,1)S(1)}, u32[]{:S(2)}, u32[]{:S(2)}) %collective-permute-start.48) | collective-permute-done | bytes 245792 | tf_op jit(solution)/shard_map/ppermute | solution.py:489
  (286 shorter events, 107.4 us)
Async XLA Ops:
  7.7 15.4 %collective-permute-start.4 = (bf16[480,768]{1,0:T(8,128)(2,1)S(1)}, bf16[480,768]{1,0:T(8,128)(2,1)}, u32[]{:S(2)}, u32[]{:S(2)}) collective-permute-start(bf16[480,768]{1,0:T(8,128)(2,1)S(1)} %pad_maximum_fusion.2.refs_14_), channel_id=1, source_target_pairs={{0,1},{1,0},{2,3},{3,2},{4,5},{5,4},{6,7},{7,6},{8,9},{9,8},{10,11... | collective-permute-start | bytes 2211848 | tf_op jit(solution)/shard_map/ppermute | solution.py:489
  49.1 19.4 %collective-permute-start.16 = (bf16[480,384]{1,0:T(8,128)(2,1)S(1)}, bf16[480,384]{1,0:T(8,128)(2,1)S(1)}, u32[]{:S(2)}, u32[]{:S(2)}) collective-permute-start(bf16[480,384]{1,0:T(8,128)(2,1)S(1)} %pad_maximum_fusion.9), channel_id=1, source_target_pairs={{0,4},{1,5},{2,6},{3,7},{4,0},{5,1},{6,2},{7,3},{8,12},{9,13},{10,... | collective-permute-start | bytes 1105928 | tf_op jit(solution)/shard_map/ppermute | solution.py:489
  51.3 16.1 %collective-permute-start.14 = (bf16[3,48,768]{2,1,0:T(8,128)(2,1)}, bf16[3,48,768]{2,1,0:T(8,128)(2,1)}, u32[]{:S(2)}, u32[]{:S(2)}) collective-permute-start(bf16[3,48,768]{2,1,0:T(8,128)(2,1)} %get-tuple-element.287), channel_id=1, source_target_pairs={{0,8},{1,9},{2,10},{3,11},{4,12},{5,13},{6,14},{7,15},{8,0},{9,1},... | collective-permute-start | bytes 663560 | tf_op jit(solution)/shard_map/ppermute | solution.py:489
  51.9 15.6 %collective-permute-start.15 = (bf16[3,48,768]{2,1,0:T(8,128)(2,1)}, bf16[3,48,768]{2,1,0:T(8,128)(2,1)}, u32[]{:S(2)}, u32[]{:S(2)}) collective-permute-start(bf16[3,48,768]{2,1,0:T(8,128)(2,1)} %get-tuple-element.286), channel_id=1, source_target_pairs={{0,16},{1,17},{2,18},{3,19},{4,20},{5,21},{6,22},{7,23},{8,24},{9,... | collective-permute-start | bytes 663560 | tf_op jit(solution)/shard_map/ppermute | solution.py:489
  69.7 23.2 %collective-permute-start.18 = (bf16[2,3,48,768]{3,2,1,0:T(8,128)(2,1)S(1)}, bf16[2,3,48,768]{3,2,1,0:T(8,128)(2,1)S(1)}, u32[]{:S(2)}, u32[]{:S(2)}) collective-permute-start(bf16[2,3,48,768]{3,2,1,0:T(8,128)(2,1)S(1)} %pad_maximum_fusion.8.refs_8_), channel_id=1, source_target_pairs={{0,8},{1,9},{2,10},{3,11},{4,12},{5,13},{6,14},{7,15},{8,0},{9,1},... | collective-permute-start | bytes 1327112 | tf_op jit(solution)/shard_map/ppermute | solution.py:489
  71.3 21.6 %collective-permute-start.17 = (bf16[2,3,48,768]{3,2,1,0:T(8,128)(2,1)S(1)}, bf16[2,3,48,768]{3,2,1,0:T(8,128)(2,1)S(1)}, u32[]{:S(2)}, u32[]{:S(2)}) collective-permute-start(bf16[2,3,48,768]{3,2,1,0:T(8,128)(2,1)S(1)} %pad_maximum_fusion.7.refs_7_), channel_id=1, source_target_pairs={{0,16},{1,17},{2,18},{3,19},{4,20},{5,21},{6,22},{7,23},{8,24},{9,... | collective-permute-start | bytes 1327112 | tf_op jit(solution)/shard_map/ppermute | solution.py:489
  72.4 20.5 %collective-permute-start.19 = (bf16[2,3,48,768]{3,2,1,0:T(8,128)(2,1)S(1)}, bf16[2,3,48,768]{3,2,1,0:T(8,128)(2,1)S(1)}, u32[]{:S(2)}, u32[]{:S(2)}) collective-permute-start(bf16[2,3,48,768]{3,2,1,0:T(8,128)(2,1)S(1)} %pad_maximum_fusion.7.refs_7_), channel_id=1, source_target_pairs={{0,1},{1,0},{2,3},{3,2},{4,5},{5,4},{6,7},{7,6},{8,9},{9,8},{10,11... | collective-permute-start | bytes 1327112 | tf_op jit(solution)/shard_map/ppermute | solution.py:489
  74.0 18.8 %collective-permute-start.21 = (bf16[480,384]{1,0:T(8,128)(2,1)S(1)}, bf16[480,384]{1,0:T(8,128)(2,1)S(1)}, u32[]{:S(2)}, u32[]{:S(2)}) collective-permute-start(bf16[480,384]{1,0:T(8,128)(2,1)S(1)} %copy-done.19), channel_id=1, source_target_pairs={{0,6},{1,7},{2,0},{3,1},{4,2},{5,3},{6,4},{7,5},{8,14},{9,15},{10,... | collective-permute-start | bytes 1105928 | tf_op jit(solution)/shard_map/ppermute | solution.py:489
  93.1 16.1 %collective-permute-start.26 = (bf16[3,480,384]{2,1,0:T(8,128)(2,1)S(1)}, bf16[3,480,384]{2,1,0:T(8,128)(2,1)}, u32[]{:S(2)}, u32[]{:S(2)}) collective-permute-start(bf16[3,480,384]{2,1,0:T(8,128)(2,1)S(1)} %pad_maximum_fusion.refs_15_), channel_id=1, source_target_pairs={{0,1},{1,0},{2,3},{3,2},{4,5},{5,4},{6,7},{7,6},{8,9},{9,8},{10,11... | collective-permute-start | bytes 3317768 | tf_op jit(solution)/shard_map/ppermute | solution.py:489
  93.6 15.5 %collective-permute-start.25 = (bf16[2,2,3,48,768]{4,3,2,1,0:T(8,128)(2,1)S(1)}, bf16[2,2,3,48,768]{4,3,2,1,0:T(8,128)(2,1)}, u32[]{:S(2)}, u32[]{:S(2)}) collective-permute-start(bf16[2,2,3,48,768]{4,3,2,1,0:T(8,128)(2,1)S(1)} %pad_maximum_fusion.1.refs_9_), channel_id=1, source_target_pairs={{0,1},{1,0},{2,3},{3,2},{4,5},{5,4},{6,7},{7,6},{8,9},{9,8},{10,11... | collective-permute-start | bytes 2654216 | tf_op jit(solution)/shard_map/ppermute | solution.py:489
  172.9 17.3 %collective-permute-start.29 = (bf16[2,2,4,240,384]{4,3,2,1,0:T(8,128)(2,1)}, bf16[2,2,4,240,384]{4,3,2,1,0:T(8,128)(2,1)}, u32[]{:S(2)}, u32[]{:S(2)}) collective-permute-start(bf16[2,2,4,240,384]{4,3,2,1,0:T(8,128)(2,1)} %get-tuple-element.168), channel_id=1, source_target_pairs={{0,1},{1,0},{2,3},{3,2},{4,5},{5,4},{6,7},{7,6},{8,9},{9,8},{10,11... | collective-permute-start | bytes 8847368 | tf_op jit(solution)/shard_map/ppermute | solution.py:489
  187.9 21.0 %collective-permute-start.32 = (bf16[2,2,2,4,96,384]{5,4,3,2,1,0:T(8,128)(2,1)}, bf16[2,2,2,4,96,384]{5,4,3,2,1,0:T(8,128)(2,1)}, u32[]{:S(2)}, u32[]{:S(2)}) collective-permute-start(bf16[2,2,2,4,96,384]{5,4,3,2,1,0:T(8,128)(2,1)} %get-tuple-element.173), channel_id=1, source_target_pairs={{0,1},{1,0},{2,3},{3,2},{4,5},{5,4},{6,7},{7,6},{8,9},{9,8},{10,11... | collective-permute-start | bytes 7077896 | tf_op jit(solution)/shard_map/ppermute | solution.py:489
  193.0 20.9 %collective-permute-start.30 = (bf16[4,240,384]{2,1,0:T(8,128)(2,1)}, bf16[4,240,384]{2,1,0:T(8,128)(2,1)}, u32[]{:S(2)}, u32[]{:S(2)}) collective-permute-start(bf16[4,240,384]{2,1,0:T(8,128)(2,1)} %get-tuple-element.237), channel_id=1, source_target_pairs={{0,8},{1,9},{2,10},{3,11},{4,12},{5,13},{6,14},{7,15},{8,0},{9,1},... | collective-permute-start | bytes 2211848 | tf_op jit(solution)/shard_map/ppermute | solution.py:489
  194.5 19.4 %collective-permute-start.31 = (bf16[4,240,384]{2,1,0:T(8,128)(2,1)}, bf16[4,240,384]{2,1,0:T(8,128)(2,1)}, u32[]{:S(2)}, u32[]{:S(2)}) collective-permute-start(bf16[4,240,384]{2,1,0:T(8,128)(2,1)} %get-tuple-element.236), channel_id=1, source_target_pairs={{0,16},{1,17},{2,18},{3,19},{4,20},{5,21},{6,22},{7,23},{8,24},{9,... | collective-permute-start | bytes 2211848 | tf_op jit(solution)/shard_map/ppermute | solution.py:489
  211.8 25.5 %collective-permute-start.33 = (bf16[2,4,96,384]{3,2,1,0:T(8,128)(2,1)}, bf16[2,4,96,384]{3,2,1,0:T(8,128)(2,1)}, u32[]{:S(2)}, u32[]{:S(2)}) collective-permute-start(bf16[2,4,96,384]{3,2,1,0:T(8,128)(2,1)} %get-tuple-element.245), channel_id=1, source_target_pairs={{0,8},{1,9},{2,10},{3,11},{4,12},{5,13},{6,14},{7,15},{8,0},{9,1},... | collective-permute-start | bytes 1769480 | tf_op jit(solution)/shard_map/ppermute | solution.py:489
  212.7 24.6 %collective-permute-start.34 = (bf16[2,4,96,384]{3,2,1,0:T(8,128)(2,1)}, bf16[2,4,96,384]{3,2,1,0:T(8,128)(2,1)}, u32[]{:S(2)}, u32[]{:S(2)}) collective-permute-start(bf16[2,4,96,384]{3,2,1,0:T(8,128)(2,1)} %get-tuple-element.244), channel_id=1, source_target_pairs={{0,16},{1,17},{2,18},{3,19},{4,20},{5,21},{6,22},{7,23},{8,24},{9,... | collective-permute-start | bytes 1769480 | tf_op jit(solution)/shard_map/ppermute | solution.py:489
  218.0 40.1 %collective-permute-start.43 = (bf16[2,240,384]{2,1,0:T(8,128)(2,1)}, bf16[2,240,384]{2,1,0:T(8,128)(2,1)S(1)}, u32[]{:S(2)}, u32[]{:S(2)}) collective-permute-start(bf16[2,240,384]{2,1,0:T(8,128)(2,1)} %pad_maximum_fusion.12), channel_id=1, source_target_pairs={{0,6},{1,7},{2,0},{3,1},{4,2},{5,3},{6,4},{7,5},{8,14},{9,15},{10,... | collective-permute-start | bytes 1105928 | tf_op jit(solution)/shard_map/ppermute | solution.py:489
  220.7 37.4 %collective-permute-start.42 = (bf16[2,240,384]{2,1,0:T(8,128)(2,1)}, bf16[2,240,384]{2,1,0:T(8,128)(2,1)}, u32[]{:S(2)}, u32[]{:S(2)}) collective-permute-start(bf16[2,240,384]{2,1,0:T(8,128)(2,1)} %pad_maximum_fusion.11), channel_id=1, source_target_pairs={{0,4},{1,5},{2,6},{3,7},{4,0},{5,1},{6,2},{7,3},{8,12},{9,13},{10,... | collective-permute-start | bytes 1105928 | tf_op jit(solution)/shard_map/ppermute | solution.py:489
  222.0 36.0 %collective-permute-start.41 = (bf16[2,240,384]{2,1,0:T(8,128)(2,1)}, bf16[2,240,384]{2,1,0:T(8,128)(2,1)}, u32[]{:S(2)}, u32[]{:S(2)}) collective-permute-start(bf16[2,240,384]{2,1,0:T(8,128)(2,1)} %pad_maximum_fusion.10), channel_id=1, source_target_pairs={{0,2},{1,3},{2,4},{3,5},{4,6},{5,7},{6,0},{7,1},{8,10},{9,11},{10,... | collective-permute-start | bytes 1105928 | tf_op jit(solution)/shard_map/ppermute | solution.py:489
  240.1 17.4 %collective-permute-start.35 = (bf16[4,96,384]{2,1,0:T(8,128)(2,1)}, bf16[4,96,384]{2,1,0:T(8,128)(2,1)S(1)}, u32[]{:S(2)}, u32[]{:S(2)}) collective-permute-start(bf16[4,96,384]{2,1,0:T(8,128)(2,1)} %get-tuple-element.242), channel_id=1, source_target_pairs={{0,16},{1,17},{2,18},{3,19},{4,20},{5,21},{6,22},{7,23},{8,24},{9,... | collective-permute-start | bytes 884744 | tf_op jit(solution)/shard_map/ppermute | solution.py:489
  241.6 15.9 %collective-permute-start.36 = (bf16[4,96,384]{2,1,0:T(8,128)(2,1)S(1)}, bf16[4,96,384]{2,1,0:T(8,128)(2,1)S(1)}, u32[]{:S(2)}, u32[]{:S(2)}) collective-permute-start(bf16[4,96,384]{2,1,0:T(8,128)(2,1)S(1)} %get-tuple-element.239), channel_id=1, source_target_pairs={{0,8},{1,9},{2,10},{3,11},{4,12},{5,13},{6,14},{7,15},{8,0},{9,1},... | collective-permute-start | bytes 884744 | tf_op jit(solution)/shard_map/ppermute | solution.py:489
  279.5 18.6 %collective-permute-start.49 = (bf16[2,160,384]{2,1,0:T(8,128)(2,1)S(1)}, bf16[2,160,384]{2,1,0:T(8,128)(2,1)S(1)}, u32[]{:S(2)}, u32[]{:S(2)}) collective-permute-start(bf16[2,160,384]{2,1,0:T(8,128)(2,1)S(1)} %pad_maximum_fusion.18), channel_id=1, source_target_pairs={{0,6},{1,7},{2,0},{3,1},{4,2},{5,3},{6,4},{7,5},{8,14},{9,15},{10,... | collective-permute-start | bytes 737288 | tf_op jit(solution)/shard_map/ppermute | solution.py:489
  281.8 20.7 %collective-permute-start.48 = (bf16[2,160,384]{2,1,0:T(8,128)(2,1)S(1)}, bf16[2,160,384]{2,1,0:T(8,128)(2,1)S(1)}, u32[]{:S(2)}, u32[]{:S(2)}) collective-permute-start(bf16[2,160,384]{2,1,0:T(8,128)(2,1)S(1)} %pad_maximum_fusion.17), channel_id=1, source_target_pairs={{0,4},{1,5},{2,6},{3,7},{4,0},{5,1},{6,2},{7,3},{8,12},{9,13},{10,... | collective-permute-start | bytes 737288 | tf_op jit(solution)/shard_map/ppermute | solution.py:489
  287.2 15.3 %collective-permute-start.47 = (bf16[2,160,384]{2,1,0:T(8,128)(2,1)S(1)}, bf16[2,160,384]{2,1,0:T(8,128)(2,1)S(1)}, u32[]{:S(2)}, u32[]{:S(2)}) collective-permute-start(bf16[2,160,384]{2,1,0:T(8,128)(2,1)S(1)} %pad_maximum_fusion.16), channel_id=1, source_target_pairs={{0,2},{1,3},{2,4},{3,5},{4,6},{5,7},{6,0},{7,1},{8,10},{9,11},{10,... | collective-permute-start | bytes 737288 | tf_op jit(solution)/shard_map/ppermute | solution.py:489
  (73 other events, 630.9 us)

commit v3 on v2

--- a/solution.py
+++ b/solution.py
@@ -89,8 +89,11 @@
     )(tokens, w, w, w, vecs, aq, ak)
 
 
-def owner_of(s, at_r):
-    return lax.rem(s // 2 - at_r[2] + 4, 4), at_r[3] != s % 2
+def owners(at_r, own, other):
+    for k in range(4):
+        z = lax.rem(k + at_r[2], 4)
+        for core, ref in ((at_r[3], own), (1 - at_r[3], other)):
+            yield k, 2 * z + core, ref
 
 
 def select_lanes(s, piece, width):
@@ -160,20 +163,14 @@
             for i in range(3):
                 dw_o[i] = dw_s[:, i * width : (i + 1) * width].astype(bf16)
             return
-        res = dw_s[...].astype(bf16)
-        piece = res.shape[0] // 8
-        half, wide = piece // 2, res.shape[1] // 2
-        for s in range(8):
-            kk, far = owner_of(s, at_r)
+        piece = dw_s.shape[0] // 8
+        half, wide = piece // 2, dw_s.shape[1] // 2
+        for k, s, ref in owners(at_r, own_o, other_o):
             for ab, turn in ((0, at_r[1]), (1, at_r[0])):
+                row = pl.multiple_of(s * piece + ab * half, 16)
                 for h in range(2):
-                    val = res[s * piece + ab * half : s * piece + (ab + 1) * half, h * wide : (h + 1) * wide]
-                    rel = lax.rem(h + turn, 2)
-                    for ref, cond in ((other_o, far), (own_o, ~far)):
-
-                        @pl.when(cond)
-                        def _(val=val, rel=rel, kk=kk, ab=ab, ref=ref):
-                            ref[ab, rel, kk, 0:half] = val
+                    val = dw_s[pl.ds(row, half), h * wide : (h + 1) * wide]
+                    ref[ab, lax.rem(h + turn, 2), k, 0:half] = val.astype(bf16)
 
         if mode == "third":
             sums = [r[...] for r in (db0, db1, db_o)]
@@ -185,14 +182,9 @@
                 for h in range(2):
                     own_o[ab, h, :, half : half + 16, :] = extra
                     other_o[ab, h, :, half : half + 16, :] = extra
-            for s in range(8):
+            for k, s, ref in owners(at_r, own_o, other_o):
                 blk = nt(table, select_lanes(s, piece, table.shape[1])).astype(bf16)
-                kk, far = owner_of(s, at_r)
-                for ref, cond in ((other_o, far), (own_o, ~far)):
-
-                    @pl.when(cond)
-                    def _(blk=blk, kk=kk, ref=ref):
-                        ref[0, at_r[1], kk, half : half + 16, 0:128] = blk
+                ref[0, at_r[1], k, half : half + 16, 0:128] = blk
 
 
 def attend_back(mode, g, at, saved, gc, aq, ak, tokens, w, dx, length, extra=()):
@@ -355,7 +347,7 @@
 
 def grad_down_kernel(groups, at_r, *refs):
     ctx = refs[:groups]
-    gb, hid, gd, own_o, other_o = refs[groups:]
+    gb, hid, gd, own_o, other_o, res_s = refs[groups:]
     p = pl.program_id(0)
     turns = ((0, at_r[1]), (1, at_r[0]))
     wide = gd.shape[1] // 2
@@ -364,20 +356,14 @@
     @pl.when(p == 0)
     def _():
         lhs = jnp.concatenate([r[...] for r in ctx], axis=1)
-        res = tn(lhs, gb[...]).astype(bf16)
-        piece = res.shape[0] // 8
+        res_s[...] = tn(lhs, gb[...]).astype(bf16)
+        piece = res_s.shape[0] // 8
         half = piece // 2
-        for s in range(8):
-            kk, far = owner_of(s, at_r)
+        for k, s, ref in owners(at_r, own_o, other_o):
             for ab, turn in turns:
+                row = pl.multiple_of(s * piece + ab * half, 16)
                 for h in range(2):
-                    val = res[s * piece + ab * half : s * piece + (ab + 1) * half, h * wide : (h + 1) * wide]
-                    rel = lax.rem(h + turn, 2)
-                    for ref, cond in ((other_o, far), (own_o, ~far)):
-
-                        @pl.when(cond)
-                        def _(val=val, rel=rel, kk=kk, ab=ab, ref=ref):
-                            ref[ab, rel, kk, tall : tall + half] = val
+                    ref[ab, lax.rem(h + turn, 2), k, tall : tall + half] = res_s[pl.ds(row, half), h * wide : (h + 1) * wide]
 
     @pl.when(p > 0)
     def _():
@@ -413,6 +399,7 @@
             grid=(9,),
             in_specs=[whole(c.shape) for c in ctx] + [whole(gb.shape), pl.BlockSpec((rows, piece), owner), whole(gd.shape)],
             out_specs=[whole(part), whole(part)],
+            scratch_shapes=[pltpu.VMEM((width, width), bf16)],
         ),
         out_shape=[jax.ShapeDtypeStruct(part, bf16)] * 2,
         compiler_params=params(),
@@ -421,7 +408,7 @@
     )(at, *ctx, gb, hid, gd)
 
 
-def grad_up_kernel(at_r, low, gu, own_o, other_o, turned):
+def grad_up_kernel(at_r, low, gu, own_o, other_o, turned, res_s):
     j = pl.program_id(0)
     y, x = at_r[0], at_r[1]
 
@@ -429,21 +416,16 @@
     def _():
         turned[...] = low[...].T
 
-    res = nn(turned[...], gu[...]).astype(bf16)
-    piece = res.shape[0] // 8
+    res_s[...] = nn(turned[...], gu[...]).astype(bf16)
+    piece = res_s.shape[0] // 8
     half = piece // 2
     h, l = j // 4, lax.rem(j // 2, 2)
-    row = pl.multiple_of(lax.rem(j, 2) * half, 16)
-    for s in range(8):
-        kk, far = owner_of(s, at_r)
+    to = pl.multiple_of(lax.rem(j, 2) * half, 16)
+    for k, s, ref in owners(at_r, own_o, other_o):
         for ab, turn, other_turn in ((0, x, y), (1, y, x)):
-            val = res[s * piece + ab * half : s * piece + (ab + 1) * half]
+            row = pl.multiple_of(s * piece + ab * half, 16)
             one, two = lax.rem(h + turn, 2), lax.rem(l + other_turn, 2)
-            for ref, cond in ((other_o, far), (own_o, ~far)):
-
-                @pl.when(cond)
-                def _(val=val, kk=kk, ab=ab, one=one, two=two, ref=ref):
-                    ref[ab, one, two, kk, pl.ds(row, half), :] = val
+            ref[ab, one, two, k, pl.ds(to, half), :] = res_s[pl.ds(row, half), :]
 
 
 def grad_up(at, low, gu):
@@ -458,7 +440,7 @@
         in_specs=[SMEM, pl.BlockSpec((rows, width), lambda j: (0, 0)), pl.BlockSpec((rows, step), lambda j: (0, j))],
         out_specs=[whole, whole],
         out_shape=[jax.ShapeDtypeStruct(part, bf16)] * 2,
-        scratch_shapes=[pltpu.VMEM((width, rows), bf16)],
+        scratch_shapes=[pltpu.VMEM((width, rows), bf16), pltpu.VMEM((width, step), bf16)],
         compiler_params=params(),
         cost_estimate=cost(9_000_000_000, 14_000_000),
         name="grad_up",
@@ -615,8 +597,12 @@
                     col = (i * groups + g) * GW
                     outs[0][ab * half : (ab + 1) * half, col : col + GW] = both[g * half : (g + 1) * half, i * GW : (i + 1) * GW]
             if ab == 0:
-                rows = groups * half
-                outs[1][...] = left[rows : rows + 16, :128]
+                small = left[groups * half : groups * half + 16]
+                piece = outs[1].shape[1]
+                outs[1][...] = small[:2, :piece]
+                for i in range(6):
+                    outs[2 + i][...] = small[2 + i : 3 + i, :piece]
+                outs[8][...] = jnp.concatenate([small[8 + i : 9 + i, :piece] for i in range(4)], axis=1)
 
 
 def finish(at, kind, blocks, shapes):
@@ -670,8 +656,7 @@
         self.far = send(self.sent[0], ACROSS), send(self.sent[1], ALONG)
 
     def along_z(self):
-        far = self.far
-        self.mine = [jnp.stack([self.near(i, k) for i in range(2)]) for k in range(4)]
+        self.mine = [self.near(k) for k in range(4)]
         self.sent = self.mine[1:]
         self.far = ()
         self.parts = [send(self.mine[k], SHIFT[k]) for k in range(1, 4)]
@@ -683,16 +668,11 @@
 
     rest = ()
 
-    def near(self, i, k):
+    def near(self, k):
+        far = jnp.stack([f[k] for f in self.far])
         if self.rest:
-            return total(self.rest[i][k], self.far[i][k])
-        terms = []
-        at = 0
-        for o, g in zip(self.own, self.got):
-            rows = o.shape[3]
-            terms.append(total(o[i, 0, k], g[i, 0, k], self.far[i][k, at : at + rows]))
-            at += rows
-        return terms[0] if len(terms) == 1 else jnp.concatenate(terms, axis=0)
+            return total(jnp.stack([r[k] for r in self.rest]), far)
+        return self.pair(lambda a: a[:, 0, k], far)
 
     def quarter(self):
         own, got, far = self.own[0], self.got[0], self.far
@@ -842,19 +822,19 @@
     qkv.after(dwd, dwo, dwu)
     qkv.across()
     qkv.share()
-    dwq, small = finish(at, "qkv", qkv.out, [qkv_weight.shape, (16, 128)])
-    one = lambda i: small[i, :piece]
+    dwq, dqv, *ones, dbu = finish(at, "qkv", qkv.out, [qkv_weight.shape, (2, piece)] + 6 * [(1, piece)] + [(1, 4 * piece)])
+    one = lambda i: ones[i - 2].reshape(piece)
     return (
         result,
         dx,
         dwq,
-        small[:2, :piece],
+        dqv,
         dwo,
         one(2),
         one(3),
         one(4),
         dwu,
-        small[8:12, :piece].reshape(-1),
+        dbu.reshape(-1),
         dwd,
         one(5),
         one(6),

time: 329 us -> 326 us (level)
  local copies, waits for them, and re-layouts: 17.2 us -> 23.4 us
  other arithmetic: 26.5 us -> 22 us
  starting transfers between devices: 53.9 us -> 50 us
    ppermute x58, starting transfers between devices: 53.9 us -> 50 us  [send(): return lax.ppermute(a, AXES, where)]
    pallas_call x0 -> x1, local copies, waits for them, and re-layouts: none -> 3.8 us  [grad_down(): pl.pallas_call(functools.partial(grad_down_kernel, len(ctx)), grid_spec=p...]
    convert_element_type x18 -> x19, other arithmetic: 14.3 us -> 14.3 us  [total(): return out.astype(bf16)]
  transfers between devices with their start and end apart: 58 -> 58, of which waited for: 21 -> 22; matrix products, arithmetic and copies ran while one was open for 10% -> 10% of each run, Pallas kernels for 28% -> 27%
where the time goes in v3:
time: 326 us; the launch traced here: 319 us
  Pallas kernels  148 us (45%)
  waiting for transfers between devices  73.9 us (23%)
  starting transfers between devices  50 us (15%)
  local copies, waits for them, and re-layouts  23.4 us (7%)
  other arithmetic  22 us (7%)
    ppermute x58, waiting for transfers between devices, send(): return lax.ppermute(a, AXES, where)  73.9 us
    ppermute x58, starting transfers between devices, send(): return lax.ppermute(a, AXES, where)  50 us
    pallas_call x1, Pallas kernels, middle(): pl.pallas_call(functools.partial(middle_kernel, len(ctx), split), grid=(r...  44.1 us
    pallas_call x3, Pallas kernels, attend_back(): pl.pallas_call(functools.partial(attend_back_kernel, mode), grid=(seqs,),...  41.7 us
    pallas_call x3, Pallas kernels, attend(): pl.pallas_call(attend_kernel, grid=(seqs,), in_specs=[seq, col(0), col(1)...  23.8 us
    pallas_call x1, Pallas kernels, grad_down(): pl.pallas_call(functools.partial(grad_down_kernel, len(ctx)), grid_spec=p...  15.7 us
    convert_element_type x19, other arithmetic, total(): return out.astype(bf16)  14.3 us
    pallas_call x1, Pallas kernels, grad_up(): pl.pallas_call(grad_up_kernel, grid=(8,), in_specs=[SMEM, pl.BlockSpec((r...  13.6 us
  transfers between devices with their start and end apart: 58, of which 22 were waited for; matrix products, arithmetic and copies ran while one was open for 10% of the time, Pallas kernels for 27%

profile of v3, /device:TPU:0, one launch (start us, length us, event | category | flops | bytes accessed | tf_op | source)
XLA Modules:
  0.0 319.4 jit_solution(14127341755258967948)
XLA Ops:
  3.3 3.1 collective-permute-start
  9.5 4.8 %collective-permute-done = bf16[104,1152]{1,0:T(8,128)(2,1)S(1)} collective-permute-done((bf16[104,1152]{1,0:T(8,128)(2,1)S(1)}, bf16[104,1152]{1,0:T(8,128)(2,1)S(1)}, u32[]{:S(2)}, u32[]{:S(2)}) %collective-permute-start) | collective-permute-done | bytes 239648 | tf_op jit(solution)/shard_map/ppermute | solution.py:471
  15.3 7.7 %collective-permute-done.1 = bf16[104,1152]{1,0:T(8,128)(2,1)S(1)} collective-permute-done((bf16[104,1152]{1,0:T(8,128)(2,1)S(1)}, bf16[104,1152]{1,0:T(8,128)(2,1)S(1)}, u32[]{:S(2)}, u32[]{:S(2)}) %collective-permute-start.1) | collective-permute-done | bytes 239648 | tf_op jit(solution)/shard_map/ppermute | solution.py:471
  24.3 6.8 %collective-permute-done.5 = bf16[104,1152]{1,0:T(8,128)(2,1)S(1)} collective-permute-done((bf16[104,1152]{1,0:T(8,128)(2,1)S(1)}, bf16[104,1152]{1,0:T(8,128)(2,1)S(1)}, u32[]{:S(2)}, u32[]{:S(2)}) %collective-permute-start.5) | collective-permute-done | bytes 239648 | tf_op jit(solution)/shard_map/ppermute | solution.py:471
  35.0 3.7 %collective-permute-start.8 = (bf16[96,768]{1,0:T(8,128)(2,1)}, bf16[96,768]{1,0:T(8,128)(2,1)S(1)}, u32[]{:S(2)}, u32[]{:S(2)}) collective-permute-start(bf16[96,768]{1,0:T(8,128)(2,1)} %constant_dynamic-slice_fusion.2), channel_id=1, source_target_pairs={{0,6},{1,7},{2,0},{3,1},{4,2},{5,3},{6,4},{7,5},{8,14},{9,15},{10,... | collective-permute-start | bytes 442376 | tf_op jit(solution)/shard_map/ppermute | solution.py:471
  38.8 3.7 %collective-permute-done.6 = bf16[96,768]{1,0:T(8,128)(2,1)S(1)} collective-permute-done((bf16[96,768]{1,0:T(8,128)(2,1)}, bf16[96,768]{1,0:T(8,128)(2,1)S(1)}, u32[]{:S(2)}, u32[]{:S(2)}) %collective-permute-start.6) | collective-permute-done | bytes 147488 | tf_op jit(solution)/shard_map/ppermute | solution.py:471
  42.6 3.5 %collective-permute-done.7 = bf16[96,768]{1,0:T(8,128)(2,1)S(1)} collective-permute-done((bf16[96,768]{1,0:T(8,128)(2,1)}, bf16[96,768]{1,0:T(8,128)(2,1)S(1)}, u32[]{:S(2)}, u32[]{:S(2)}) %collective-permute-start.7) | collective-permute-done | bytes 147488 | tf_op jit(solution)/shard_map/ppermute | solution.py:471
  53.7 4.0 %assemble.1.wq.wk.wv = bf16[768,2304]{1,0:T(8,128)(2,1)} custom-call(s32[4]{0:T(128)} %pad_add_fusion.at_r, bf16[104,2304]{1,0:T(8,128)(2,1)} %copy-done.3, bf16[3,104,1152]{2,1,0:T(8,128)(2,1)} %copy-done, bf16[3,48,1152]{2,1,0:T(8,128)(2,1)} %copy-done.23, bf16[3,48,1152]{2,1,0:T(8,128)(2,1)} %copy-done.22, bf16[104,2304]{1,0:T(8,128)(2,1)} %copy-done.13, ...), custom_call_target="tpu_custom_call" | custom-call | bytes 7077888 | tf_op jit(solution)/shard_map/assemble/pallas_call | solution.py:537
  57.7 7.9 %attend.3 = (bf16[1024,256]{1,0:T(8,128)(2,1)}, bf16[1024,256]{1,0:T(8,128)(2,1)}, bf16[1024,256]{1,0:T(8,128)(2,1)}, bf16[1024,256]{1,0:T(8,128)(2,1)}, f32[2,8,512]{2,1,0:T(8,128)}) custom-call(bf16[1024,768]{1,0:T(8,128)(2,1)} %tok.10, bf16[768,2304]{1,0:T(8,128)(2,1)} %assemble.1.wq.wk.wv, bf16[768,2304]{1,0:T(8,128)(2,1)} %assemble.1.wq.wk.wv, ...), custom_call_target="tpu_custom_call" | custom-call | flops 4000000000 | bytes 5000000 | tf_op jit(solution)/shard_map/attend/pallas_call | solution.py:80
  74.7 7.9 %attend.4 = (bf16[1024,256]{1,0:T(8,128)(2,1)}, bf16[1024,256]{1,0:T(8,128)(2,1)}, bf16[1024,256]{1,0:T(8,128)(2,1)}, bf16[1024,256]{1,0:T(8,128)(2,1)}, f32[2,8,512]{2,1,0:T(8,128)}) custom-call(bf16[1024,768]{1,0:T(8,128)(2,1)} %tok.10, bf16[768,2304]{1,0:T(8,128)(2,1)} %assemble.1.wq.wk.wv, bf16[768,2304]{1,0:T(8,128)(2,1)} %assemble.1.wq.wk.wv, ...), custom_call_target="tpu_custom_call" | custom-call | flops 4000000000 | bytes 5000000 | tf_op jit(solution)/shard_map/attend/pallas_call | solution.py:80
  84.0 7.0 %collective-permute-done.21 = bf16[480,384]{1,0:T(8,128)(2,1)S(1)} collective-permute-done((bf16[480,384]{1,0:T(8,128)(2,1)S(1)}, bf16[480,384]{1,0:T(8,128)(2,1)S(1)}, u32[]{:S(2)}, u32[]{:S(2)}) %collective-permute-start.21) | collective-permute-done | bytes 368672 | tf_op jit(solution)/shard_map/ppermute | solution.py:471
  93.6 7.9 %attend.5 = (bf16[1024,256]{1,0:T(8,128)(2,1)}, bf16[1024,256]{1,0:T(8,128)(2,1)}, bf16[1024,256]{1,0:T(8,128)(2,1)}, bf16[1024,256]{1,0:T(8,128)(2,1)}, f32[2,8,512]{2,1,0:T(8,128)}) custom-call(bf16[1024,768]{1,0:T(8,128)(2,1)} %tok.10, bf16[768,2304]{1,0:T(8,128)(2,1)} %assemble.1.wq.wk.wv, bf16[768,2304]{1,0:T(8,128)(2,1)} %assemble.1.wq.wk.wv, ...), custom_call_target="tpu_custom_call" | custom-call | flops 4000000000 | bytes 5000000 | tf_op jit(solution)/shard_map/attend/pallas_call | solution.py:80
  101.5 5.5 %collective-permute-done.22.refs_16_ = bf16[3,240,384]{2,1,0:T(8,128)(2,1)} collective-permute-done((bf16[3,240,384]{2,1,0:T(8,128)(2,1)S(1)}, bf16[3,240,384]{2,1,0:T(8,128)(2,1)}, u32[]{:S(2)}, u32[]{:S(2)}) %collective-permute-start.22) | collective-permute-done | bytes 552992 | tf_op jit(solution)/shard_map/ppermute | solution.py:471
  111.0 44.1 %middle.1 = (bf16[1024,768]{1,0:T(8,128)(2,1)}, bf16[1024,768]{1,0:T(8,128)(2,1)}, bf16[1024,3072]{1,0:T(8,128)(2,1)}, bf16[1024,768]{1,0:T(8,128)(2,1)}, bf16[1...) custom-call(s32[4]{0:T(128)} %pad_add_fusion.at_r, ...), custom_call_target="tpu_custom_call" | custom-call | flops 30000001024 | bytes 40000000 | tf_op jit(solution)/shard_map/middle/pallas_call | solution.py:335
  155.1 15.7 %grad_down.1 = (bf16[2,2,4,240,384]{4,3,2,1,0:T(8,128)(2,1)}, bf16[2,2,4,240,384]{4,3,2,1,0:T(8,128)(2,1)}) custom-call(s32[4]{0:T(128)} %pad_add_fusion.at_r, bf16[1024,256]{1,0:T(8,128)(2,1)} %get-tuple-element.138.refs_0_.ctx_r, bf16[1024,256]{1,0:T(8,128)(2,1)} %get-tuple-element.143.refs_1_.ctx_r, bf16[1024,256]{1,0:T(8,128)(2,1)} %get-tuple-element.151.refs_2_.ctx_r, ...), custom_call_target="tpu_custom_call" | custom-call | flops 8999999488 | bytes 14000000 | tf_op jit(solution)/shard_map/grad_down/pallas_call | solution.py:395
  170.8 3.8 %copy.64 = bf16[2,2,4,240,384]{4,3,0,2,1:T(8,128)(2,1)} copy(bf16[2,2,4,240,384]{4,3,2,1,0:T(8,128)(2,1)} %get-tuple-element.175) | data formatting | bytes 5898240 | tf_op jit(solution)/shard_map/grad_down/pallas_call | solution.py:395
  174.8 13.6 %grad_up.1 = (bf16[2,2,2,4,96,384]{5,4,3,2,1,0:T(8,128)(2,1)}, bf16[2,2,2,4,96,384]{5,4,3,2,1,0:T(8,128)(2,1)}) custom-call(s32[4]{0:T(128)} %pad_add_fusion.at_r, bf16[1024,768]{1,0:T(8,128)(2,1)} %get-tuple-element.178.low, bf16[1024,3072]{1,0:T(8,128)(2,1)} %get-tuple-element.179.gu), custom_call_target="tpu_custom_call" | custom-call | flops 8999999488 | bytes 14000000 | tf_op jit(solution)/shard_map/grad_up/pallas_call | solution.py:437
  195.6 13.6 %attend_back.3 = (bf16[2,2,4,96,384]{4,3,2,1,0:T(8,128)(2,1)}, bf16[2,2,4,96,384]{4,3,2,1,0:T(8,128)(2,1)}, f32[1024,768]{1,0:T(8,128)}, f32[1,768]{1,0:T(1,128)}) custom-call(s32[4]{0:T(128)} %pad_add_fusion.at_r, bf16[1024,256]{1,0:T(8,128)(2,1)} %get-tuple-element.168.q_r, bf16[1024,256]{1,0:T(8,128)(2,1)} %get-tuple-element.169.k_r, ...), custom_call_target="tpu_custom_call" | custom-call | flops 8000000000 | bytes 8000000 | tf_op jit(solution)/shard_map/attend_back/pallas_call | solution.py:219
  223.7 14.0 %attend_back.4 = (bf16[2,2,4,96,384]{4,3,2,1,0:T(8,128)(2,1)}, bf16[2,2,4,96,384]{4,3,2,1,0:T(8,128)(2,1)}, f32[1024,768]{1,0:T(8,128)}, f32[1,768]{1,0:T(1,128)}) custom-call(s32[4]{0:T(128)} %pad_add_fusion.at_r, bf16[1024,256]{1,0:T(8,128)(2,1)} %get-tuple-element.164.q_r, ...), custom_call_target="tpu_custom_call", output_to_operand_aliasing={{0}: (14, {}), {1}: (15, {})} | custom-call | flops 8000000000 | bytes 8000000 | tf_op jit(solution)/shard_map/attend_back/pallas_call | solution.py:219
  237.8 3.2 %fusion.11 = (bf16[4,96,384]{2,1,0:T(8,128)(2,1)S(1)}, bf16[4,96,384]{2,1,0:T(8,128)(2,1)}, bf16[4,96,384]{2,1,0:T(8,128)(2,1)}, bf16[4,96,384]{2,1,0:T(8,128)(2,1)S(1)}) fusion(bf16[2,4,96,384]{3,2,1,0:T(8,128)(2,1)} %collective-permute-done.34, bf16[2,2,2,4,96,384]{5,4,3,2,1,0:T(8,128)(2,1)} %collective-permute-done.32, ...), kind=kLoop, calls=%fused_computation.34 | loop fusion | flops 3538944 | bytes 4718592 | tf_op jit(solution)/shard_map/convert_element_type | solution.py:567
  243.0 14.1 %attend_back.5 = (bf16[2,2,4,64,384]{4,3,2,1,0:T(8,128)(2,1)}, bf16[2,2,4,64,384]{4,3,2,1,0:T(8,128)(2,1)}, bf16[1024,768]{1,0:T(8,128)(2,1)}, f32[1,768]{1,0:T(1,128)}) custom-call(s32[4]{0:T(128)} %pad_add_fusion.at_r, bf16[1024,256]{1,0:T(8,128)(2,1)} %get-tuple-element.159.q_r, bf16[1024,256]{1,0:T(8,128)(2,1)} %get-tuple-element.160.k_r, ...), custom_call_target="tpu_custom_call" | custom-call | flops 8000000000 | bytes 8000000 | tf_op jit(solution)/shard_map/attend_back/pallas_call | solution.py:219
  269.6 8.2 %collective-permute-done.45 = bf16[2,96,384]{2,1,0:T(8,128)(2,1)S(1)} collective-permute-done((bf16[2,96,384]{2,1,0:T(8,128)(2,1)S(1)}, bf16[2,96,384]{2,1,0:T(8,128)(2,1)S(1)}, u32[]{:S(2)}, u32[]{:S(2)}) %collective-permute-start.45) | collective-permute-done | bytes 147488 | tf_op jit(solution)/shard_map/ppermute | solution.py:471
  282.7 4.6 %collective-permute-done.52 = bf16[336,384]{1,0:T(8,128)(2,1)S(1)} collective-permute-done((bf16[336,384]{1,0:T(8,128)(2,1)S(1)}, bf16[336,384]{1,0:T(8,128)(2,1)S(1)}, u32[]{:S(2)}, u32[]{:S(2)}) %collective-permute-start.52) | collective-permute-done | bytes 258080 | tf_op jit(solution)/shard_map/ppermute | solution.py:471
  289.5 6.6 %collective-permute-done.53.refs_3_ = bf16[432,384]{1,0:T(8,128)(2,1)S(1)} collective-permute-done((bf16[432,384]{1,0:T(8,128)(2,1)S(1)}, bf16[432,384]{1,0:T(8,128)(2,1)S(1)}, u32[]{:S(2)}, u32[]{:S(2)}) %collective-permute-start.53) | collective-permute-done | bytes 331808 | tf_op jit(solution)/shard_map/ppermute | solution.py:471
  (274 shorter events, 102.3 us)
Async XLA Ops:
  7.7 15.4 %collective-permute-start.4 = (bf16[480,768]{1,0:T(8,128)(2,1)S(1)}, bf16[480,768]{1,0:T(8,128)(2,1)}, u32[]{:S(2)}, u32[]{:S(2)}) collective-permute-start(bf16[480,768]{1,0:T(8,128)(2,1)S(1)} %pad_maximum_fusion.2.refs_14_), channel_id=1, source_target_pairs={{0,1},{1,0},{2,3},{3,2},{4,5},{5,4},{6,7},{7,6},{8,9},{9,8},{10,11... | collective-permute-start | bytes 2211848 | tf_op jit(solution)/shard_map/ppermute | solution.py:471
  7.8 15.2 %collective-permute-start.2 = (bf16[104,2304]{1,0:T(8,128)(2,1)S(1)}, bf16[104,2304]{1,0:T(8,128)(2,1)S(1)}, u32[]{:S(2)}, u32[]{:S(2)}) collective-permute-start(bf16[104,2304]{1,0:T(8,128)(2,1)S(1)} %fusion.15.refs_0_), channel_id=1, source_target_pairs={{0,1},{1,0},{2,3},{3,2},{4,5},{5,4},{6,7},{7,6},{8,9},{9,8},{10,11... | collective-permute-start | bytes 1437704 | tf_op jit(solution)/shard_map/ppermute | solution.py:471
  47.5 19.4 %collective-permute-start.16 = (bf16[480,384]{1,0:T(8,128)(2,1)S(1)}, bf16[480,384]{1,0:T(8,128)(2,1)S(1)}, u32[]{:S(2)}, u32[]{:S(2)}) collective-permute-start(bf16[480,384]{1,0:T(8,128)(2,1)S(1)} %pad_maximum_fusion.9), channel_id=1, source_target_pairs={{0,4},{1,5},{2,6},{3,7},{4,0},{5,1},{6,2},{7,3},{8,12},{9,13},{10,... | collective-permute-start | bytes 1105928 | tf_op jit(solution)/shard_map/ppermute | solution.py:471
  49.8 15.8 %collective-permute-start.14 = (bf16[3,48,768]{2,1,0:T(8,128)(2,1)}, bf16[3,48,768]{2,1,0:T(8,128)(2,1)}, u32[]{:S(2)}, u32[]{:S(2)}) collective-permute-start(bf16[3,48,768]{2,1,0:T(8,128)(2,1)} %get-tuple-element.296), channel_id=1, source_target_pairs={{0,8},{1,9},{2,10},{3,11},{4,12},{5,13},{6,14},{7,15},{8,0},{9,1},... | collective-permute-start | bytes 663560 | tf_op jit(solution)/shard_map/ppermute | solution.py:471
  50.4 15.3 %collective-permute-start.15 = (bf16[3,48,768]{2,1,0:T(8,128)(2,1)}, bf16[3,48,768]{2,1,0:T(8,128)(2,1)}, u32[]{:S(2)}, u32[]{:S(2)}) collective-permute-start(bf16[3,48,768]{2,1,0:T(8,128)(2,1)} %get-tuple-element.295), channel_id=1, source_target_pairs={{0,16},{1,17},{2,18},{3,19},{4,20},{5,21},{6,22},{7,23},{8,24},{9,... | collective-permute-start | bytes 663560 | tf_op jit(solution)/shard_map/ppermute | solution.py:471
  68.0 22.9 %collective-permute-start.18 = (bf16[2,3,48,768]{3,2,1,0:T(8,128)(2,1)S(1)}, bf16[2,3,48,768]{3,2,1,0:T(8,128)(2,1)S(1)}, u32[]{:S(2)}, u32[]{:S(2)}) collective-permute-start(bf16[2,3,48,768]{3,2,1,0:T(8,128)(2,1)S(1)} %pad_maximum_fusion.8.refs_8_), channel_id=1, source_target_pairs={{0,8},{1,9},{2,10},{3,11},{4,12},{5,13},{6,14},{7,15},{8,0},{9,1},... | collective-permute-start | bytes 1327112 | tf_op jit(solution)/shard_map/ppermute | solution.py:471
  69.6 21.3 %collective-permute-start.17 = (bf16[2,3,48,768]{3,2,1,0:T(8,128)(2,1)S(1)}, bf16[2,3,48,768]{3,2,1,0:T(8,128)(2,1)S(1)}, u32[]{:S(2)}, u32[]{:S(2)}) collective-permute-start(bf16[2,3,48,768]{3,2,1,0:T(8,128)(2,1)S(1)} %pad_maximum_fusion.7.refs_7_), channel_id=1, source_target_pairs={{0,16},{1,17},{2,18},{3,19},{4,20},{5,21},{6,22},{7,23},{8,24},{9,... | collective-permute-start | bytes 1327112 | tf_op jit(solution)/shard_map/ppermute | solution.py:471
  70.6 20.3 %collective-permute-start.19 = (bf16[2,3,48,768]{3,2,1,0:T(8,128)(2,1)S(1)}, bf16[2,3,48,768]{3,2,1,0:T(8,128)(2,1)S(1)}, u32[]{:S(2)}, u32[]{:S(2)}) collective-permute-start(bf16[2,3,48,768]{3,2,1,0:T(8,128)(2,1)S(1)} %pad_maximum_fusion.7.refs_7_), channel_id=1, source_target_pairs={{0,1},{1,0},{2,3},{3,2},{4,5},{5,4},{6,7},{7,6},{8,9},{9,8},{10,11... | collective-permute-start | bytes 1327112 | tf_op jit(solution)/shard_map/ppermute | solution.py:471
  72.1 18.8 %collective-permute-start.21 = (bf16[480,384]{1,0:T(8,128)(2,1)S(1)}, bf16[480,384]{1,0:T(8,128)(2,1)S(1)}, u32[]{:S(2)}, u32[]{:S(2)}) collective-permute-start(bf16[480,384]{1,0:T(8,128)(2,1)S(1)} %copy-done.19), channel_id=1, source_target_pairs={{0,6},{1,7},{2,0},{3,1},{4,2},{5,3},{6,4},{7,5},{8,14},{9,15},{10,... | collective-permute-start | bytes 1105928 | tf_op jit(solution)/shard_map/ppermute | solution.py:471
  91.1 16.1 %collective-permute-start.26 = (bf16[3,480,384]{2,1,0:T(8,128)(2,1)S(1)}, bf16[3,480,384]{2,1,0:T(8,128)(2,1)}, u32[]{:S(2)}, u32[]{:S(2)}) collective-permute-start(bf16[3,480,384]{2,1,0:T(8,128)(2,1)S(1)} %pad_maximum_fusion.refs_15_), channel_id=1, source_target_pairs={{0,1},{1,0},{2,3},{3,2},{4,5},{5,4},{6,7},{7,6},{8,9},{9,8},{10,11... | collective-permute-start | bytes 3317768 | tf_op jit(solution)/shard_map/ppermute | solution.py:471
  91.7 15.5 %collective-permute-start.25 = (bf16[2,2,3,48,768]{4,3,2,1,0:T(8,128)(2,1)S(1)}, bf16[2,2,3,48,768]{4,3,2,1,0:T(8,128)(2,1)}, u32[]{:S(2)}, u32[]{:S(2)}) collective-permute-start(bf16[2,2,3,48,768]{4,3,2,1,0:T(8,128)(2,1)S(1)} %pad_maximum_fusion.1.refs_9_), channel_id=1, source_target_pairs={{0,1},{1,0},{2,3},{3,2},{4,5},{5,4},{6,7},{7,6},{8,9},{9,8},{10,11... | collective-permute-start | bytes 2654216 | tf_op jit(solution)/shard_map/ppermute | solution.py:471
  92.1 14.9 %collective-permute-start.22 = (bf16[3,240,384]{2,1,0:T(8,128)(2,1)S(1)}, bf16[3,240,384]{2,1,0:T(8,128)(2,1)}, u32[]{:S(2)}, u32[]{:S(2)}) collective-permute-start(bf16[3,240,384]{2,1,0:T(8,128)(2,1)S(1)} %get-tuple-element.268), channel_id=1, source_target_pairs={{0,8},{1,9},{2,10},{3,11},{4,12},{5,13},{6,14},{7,15},{8,0},{9,1},... | collective-permute-start | bytes 1658888 | tf_op jit(solution)/shard_map/ppermute | solution.py:471
  174.6 16.1 %collective-permute-start.29 = (bf16[2,2,4,240,384]{4,3,0,2,1:T(8,128)(2,1)}, bf16[2,2,4,240,384]{4,3,0,2,1:T(8,128)(2,1)}, u32[]{:S(2)}, u32[]{:S(2)}) collective-permute-start(bf16[2,2,4,240,384]{4,3,0,2,1:T(8,128)(2,1)} %copy.64), channel_id=1, source_target_pairs={{0,1},{1,0},{2,3},{3,2},{4,5},{5,4},{6,7},{7,6},{8,9},{9,8},{10,11... | collective-permute-start | bytes 8847368 | tf_op jit(solution)/shard_map/ppermute | solution.py:471
  188.4 20.7 %collective-permute-start.32 = (bf16[2,2,2,4,96,384]{5,4,3,2,1,0:T(8,128)(2,1)}, bf16[2,2,2,4,96,384]{5,4,3,2,1,0:T(8,128)(2,1)}, u32[]{:S(2)}, u32[]{:S(2)}) collective-permute-start(bf16[2,2,2,4,96,384]{5,4,3,2,1,0:T(8,128)(2,1)} %get-tuple-element.180), channel_id=1, source_target_pairs={{0,1},{1,0},{2,3},{3,2},{4,5},{5,4},{6,7},{7,6},{8,9},{9,8},{10,11... | collective-permute-start | bytes 7077896 | tf_op jit(solution)/shard_map/ppermute | solution.py:471
  193.6 20.6 %collective-permute-start.30 = (bf16[4,240,384]{2,1,0:T(8,128)(2,1)}, bf16[4,240,384]{2,1,0:T(8,128)(2,1)}, u32[]{:S(2)}, u32[]{:S(2)}) collective-permute-start(bf16[4,240,384]{2,1,0:T(8,128)(2,1)} %get-tuple-element.246), channel_id=1, source_target_pairs={{0,8},{1,9},{2,10},{3,11},{4,12},{5,13},{6,14},{7,15},{8,0},{9,1},... | collective-permute-start | bytes 2211848 | tf_op jit(solution)/shard_map/ppermute | solution.py:471
  195.1 19.1 %collective-permute-start.31 = (bf16[4,240,384]{2,1,0:T(8,128)(2,1)}, bf16[4,240,384]{2,1,0:T(8,128)(2,1)}, u32[]{:S(2)}, u32[]{:S(2)}) collective-permute-start(bf16[4,240,384]{2,1,0:T(8,128)(2,1)} %get-tuple-element.245), channel_id=1, source_target_pairs={{0,16},{1,17},{2,18},{3,19},{4,20},{5,21},{6,22},{7,23},{8,24},{9,... | collective-permute-start | bytes 2211848 | tf_op jit(solution)/shard_map/ppermute | solution.py:471
  212.1 25.7 %collective-permute-start.33 = (bf16[2,4,96,384]{3,2,1,0:T(8,128)(2,1)}, bf16[2,4,96,384]{3,2,1,0:T(8,128)(2,1)}, u32[]{:S(2)}, u32[]{:S(2)}) collective-permute-start(bf16[2,4,96,384]{3,2,1,0:T(8,128)(2,1)} %get-tuple-element.254), channel_id=1, source_target_pairs={{0,8},{1,9},{2,10},{3,11},{4,12},{5,13},{6,14},{7,15},{8,0},{9,1},... | collective-permute-start | bytes 1769480 | tf_op jit(solution)/shard_map/ppermute | solution.py:471
  213.0 24.7 %collective-permute-start.34 = (bf16[2,4,96,384]{3,2,1,0:T(8,128)(2,1)}, bf16[2,4,96,384]{3,2,1,0:T(8,128)(2,1)}, u32[]{:S(2)}, u32[]{:S(2)}) collective-permute-start(bf16[2,4,96,384]{3,2,1,0:T(8,128)(2,1)} %get-tuple-element.253), channel_id=1, source_target_pairs={{0,16},{1,17},{2,18},{3,19},{4,20},{5,21},{6,22},{7,23},{8,24},{9,... | collective-permute-start | bytes 1769480 | tf_op jit(solution)/shard_map/ppermute | solution.py:471
  219.2 40.2 %collective-permute-start.41 = (bf16[2,240,384]{2,1,0:T(8,128)(2,1)}, bf16[2,240,384]{2,1,0:T(8,128)(2,1)}, u32[]{:S(2)}, u32[]{:S(2)}) collective-permute-start(bf16[2,240,384]{2,1,0:T(8,128)(2,1)} %get-tuple-element.244), channel_id=1, source_target_pairs={{0,2},{1,3},{2,4},{3,5},{4,6},{5,7},{6,0},{7,1},{8,10},{9,11},{10,... | collective-permute-start | bytes 1105928 | tf_op jit(solution)/shard_map/ppermute | solution.py:471
  220.4 39.0 %collective-permute-start.42 = (bf16[2,240,384]{2,1,0:T(8,128)(2,1)}, bf16[2,240,384]{2,1,0:T(8,128)(2,1)}, u32[]{:S(2)}, u32[]{:S(2)}) collective-permute-start(bf16[2,240,384]{2,1,0:T(8,128)(2,1)} %get-tuple-element.243), channel_id=1, source_target_pairs={{0,4},{1,5},{2,6},{3,7},{4,0},{5,1},{6,2},{7,3},{8,12},{9,13},{10,... | collective-permute-start | bytes 1105928 | tf_op jit(solution)/shard_map/ppermute | solution.py:471
  221.7 37.7 %collective-permute-start.43 = (bf16[2,240,384]{2,1,0:T(8,128)(2,1)}, bf16[2,240,384]{2,1,0:T(8,128)(2,1)}, u32[]{:S(2)}, u32[]{:S(2)}) collective-permute-start(bf16[2,240,384]{2,1,0:T(8,128)(2,1)} %get-tuple-element.242), channel_id=1, source_target_pairs={{0,6},{1,7},{2,0},{3,1},{4,2},{5,3},{6,4},{7,5},{8,14},{9,15},{10,... | collective-permute-start | bytes 1105928 | tf_op jit(solution)/shard_map/ppermute | solution.py:471
  241.0 16.2 %collective-permute-start.35 = (bf16[4,96,384]{2,1,0:T(8,128)(2,1)}, bf16[4,96,384]{2,1,0:T(8,128)(2,1)}, u32[]{:S(2)}, u32[]{:S(2)}) collective-permute-start(bf16[4,96,384]{2,1,0:T(8,128)(2,1)} %get-tuple-element.251), channel_id=1, source_target_pairs={{0,16},{1,17},{2,18},{3,19},{4,20},{5,21},{6,22},{7,23},{8,24},{9,... | collective-permute-start | bytes 884744 | tf_op jit(solution)/shard_map/ppermute | solution.py:471
  280.6 19.8 %collective-permute-start.49 = (bf16[2,160,384]{2,1,0:T(8,128)(2,1)S(1)}, bf16[2,160,384]{2,1,0:T(8,128)(2,1)S(1)}, u32[]{:S(2)}, u32[]{:S(2)}) collective-permute-start(bf16[2,160,384]{2,1,0:T(8,128)(2,1)S(1)} %add_convert_fusion.12), channel_id=1, source_target_pairs={{0,6},{1,7},{2,0},{3,1},{4,2},{5,3},{6,4},{7,5},{8,14},{9,15},{10,... | collective-permute-start | bytes 737288 | tf_op jit(solution)/shard_map/ppermute | solution.py:471
  281.4 21.6 %collective-permute-start.48 = (bf16[2,160,384]{2,1,0:T(8,128)(2,1)S(1)}, bf16[2,160,384]{2,1,0:T(8,128)(2,1)S(1)}, u32[]{:S(2)}, u32[]{:S(2)}) collective-permute-start(bf16[2,160,384]{2,1,0:T(8,128)(2,1)S(1)} %add_convert_fusion.13), channel_id=1, source_target_pairs={{0,4},{1,5},{2,6},{3,7},{4,0},{5,1},{6,2},{7,3},{8,12},{9,13},{10,... | collective-permute-start | bytes 737288 | tf_op jit(solution)/shard_map/ppermute | solution.py:471
  (71 other events, 584.5 us)

commit v4 on v3

--- a/solution.py
+++ b/solution.py
@@ -656,7 +656,7 @@
         self.far = send(self.sent[0], ACROSS), send(self.sent[1], ALONG)
 
     def along_z(self):
-        self.mine = [self.near(k) for k in range(4)]
+        self.mine = [jnp.stack([self.near(i, k) for i in range(2)]) for k in range(4)]
         self.sent = self.mine[1:]
         self.far = ()
         self.parts = [send(self.mine[k], SHIFT[k]) for k in range(1, 4)]
@@ -668,11 +668,16 @@
 
     rest = ()
 
-    def near(self, k):
-        far = jnp.stack([f[k] for f in self.far])
+    def near(self, i, k):
         if self.rest:
-            return total(jnp.stack([r[k] for r in self.rest]), far)
-        return self.pair(lambda a: a[:, 0, k], far)
+            return total(self.rest[i][k], self.far[i][k])
+        terms = []
+        at = 0
+        for o, g in zip(self.own, self.got):
+            rows = o.shape[3]
+            terms.append(total(o[i, 0, k], g[i, 0, k], self.far[i][k, at : at + rows]))
+            at += rows
+        return terms[0] if len(terms) == 1 else jnp.concatenate(terms, axis=0)
 
     def quarter(self):
         own, got, far = self.own[0], self.got[0], self.far

time: 326 us -> 323 us (level)
  local copies, waits for them, and re-layouts: 23.4 us -> 13.2 us
  other arithmetic: 22 us -> 27.8 us
  starting transfers between devices: 50 us -> 53.9 us
    slice x8 -> x0, local copies, waits for them, and re-layouts: 4.77 us -> none  [the longest x6 4.7 us: near(): far = jnp.stack([f[k] for f in self.far])]
    ppermute x58, starting transfers between devices: 50 us -> 53.9 us  [send(): return lax.ppermute(a, AXES, where)]
    pallas_call x1 -> x0, local copies, waits for them, and re-layouts: 3.8 us -> none  [grad_down(): pl.pallas_call(functools.partial(grad_down_kernel, len(ctx)), grid_spec=p...]
    convert_element_type x19 -> x18, other arithmetic: 14.3 us -> 14.3 us  [total(): return out.astype(bf16)]
where the time goes in v4:
time: 323 us; the launch traced here: 317 us
  Pallas kernels  148 us (46%)
  waiting for transfers between devices  71.4 us (22%)
  starting transfers between devices  53.9 us (17%)
  other arithmetic  27.8 us (9%)
  local copies, waits for them, and re-layouts  13.2 us (4%)
    ppermute x58, waiting for transfers between devices, send(): return lax.ppermute(a, AXES, where)  71.4 us
    ppermute x58, starting transfers between devices, send(): return lax.ppermute(a, AXES, where)  53.9 us
    pallas_call x1, Pallas kernels, middle(): pl.pallas_call(functools.partial(middle_kernel, len(ctx), split), grid=(r...  44.1 us
    pallas_call x3, Pallas kernels, attend_back(): pl.pallas_call(functools.partial(attend_back_kernel, mode), grid=(seqs,),...  41.9 us
    pallas_call x3, Pallas kernels, attend(): pl.pallas_call(attend_kernel, grid=(seqs,), in_specs=[seq, col(0), col(1)...  23.7 us
    pallas_call x1, Pallas kernels, grad_down(): pl.pallas_call(functools.partial(grad_down_kernel, len(ctx)), grid_spec=p...  15.7 us
    convert_element_type x18, other arithmetic, total(): return out.astype(bf16)  14.3 us
    pallas_call x1, Pallas kernels, grad_up(): pl.pallas_call(grad_up_kernel, grid=(8,), in_specs=[SMEM, pl.BlockSpec((r...  13.7 us
  transfers between devices with their start and end apart: 58, of which 22 were waited for; matrix products, arithmetic and copies ran while one was open for 10% of the time, Pallas kernels for 27%

profile of v4, /device:TPU:0, one launch (start us, length us, event | category | flops | bytes accessed | tf_op | source)
XLA Modules:
  0.0 317.4 jit_solution(18308525221327365589)
XLA Ops:
  3.3 3.1 collective-permute-start
  10.0 4.3 %collective-permute-done = bf16[104,1152]{1,0:T(8,128)(2,1)S(1)} collective-permute-done((bf16[104,1152]{1,0:T(8,128)(2,1)S(1)}, bf16[104,1152]{1,0:T(8,128)(2,1)S(1)}, u32[]{:S(2)}, u32[]{:S(2)}) %collective-permute-start) | collective-permute-done | bytes 239648 | tf_op jit(solution)/shard_map/ppermute | solution.py:471
  15.9 7.2 %collective-permute-done.1 = bf16[104,1152]{1,0:T(8,128)(2,1)S(1)} collective-permute-done((bf16[104,1152]{1,0:T(8,128)(2,1)S(1)}, bf16[104,1152]{1,0:T(8,128)(2,1)S(1)}, u32[]{:S(2)}, u32[]{:S(2)}) %collective-permute-start.1) | collective-permute-done | bytes 239648 | tf_op jit(solution)/shard_map/ppermute | solution.py:471
  24.3 6.8 %collective-permute-done.5 = bf16[104,1152]{1,0:T(8,128)(2,1)S(1)} collective-permute-done((bf16[104,1152]{1,0:T(8,128)(2,1)S(1)}, bf16[104,1152]{1,0:T(8,128)(2,1)S(1)}, u32[]{:S(2)}, u32[]{:S(2)}) %collective-permute-start.5) | collective-permute-done | bytes 239648 | tf_op jit(solution)/shard_map/ppermute | solution.py:471
  35.5 3.7 %collective-permute-start.8 = (bf16[96,768]{1,0:T(8,128)(2,1)}, bf16[96,768]{1,0:T(8,128)(2,1)S(1)}, u32[]{:S(2)}, u32[]{:S(2)}) collective-permute-start(bf16[96,768]{1,0:T(8,128)(2,1)} %constant_dynamic-slice_fusion.2), channel_id=1, source_target_pairs={{0,6},{1,7},{2,0},{3,1},{4,2},{5,3},{6,4},{7,5},{8,14},{9,15},{10,... | collective-permute-start | bytes 442376 | tf_op jit(solution)/shard_map/ppermute | solution.py:471
  39.8 3.3 %collective-permute-done.6 = bf16[96,768]{1,0:T(8,128)(2,1)} collective-permute-done((bf16[96,768]{1,0:T(8,128)(2,1)}, bf16[96,768]{1,0:T(8,128)(2,1)}, u32[]{:S(2)}, u32[]{:S(2)}) %collective-permute-start.6) | collective-permute-done | bytes 147488 | tf_op jit(solution)/shard_map/ppermute | solution.py:471
  43.1 3.4 %collective-permute-done.7 = bf16[96,768]{1,0:T(8,128)(2,1)} collective-permute-done((bf16[96,768]{1,0:T(8,128)(2,1)}, bf16[96,768]{1,0:T(8,128)(2,1)}, u32[]{:S(2)}, u32[]{:S(2)}) %collective-permute-start.7) | collective-permute-done | bytes 147488 | tf_op jit(solution)/shard_map/ppermute | solution.py:471
  55.5 4.0 %assemble.1.wq.wk.wv = bf16[768,2304]{1,0:T(8,128)(2,1)} custom-call(s32[4]{0:T(128)} %pad_add_fusion.at_r, bf16[104,2304]{1,0:T(8,128)(2,1)} %copy-done.4, bf16[3,104,1152]{2,1,0:T(8,128)(2,1)} %copy-done, bf16[3,48,1152]{2,1,0:T(8,128)(2,1)} %copy-done.23, bf16[3,48,1152]{2,1,0:T(8,128)(2,1)} %copy-done.22, bf16[104,2304]{1,0:T(8,128)(2,1)} %copy-done.13, ...), custom_call_target="tpu_custom_call" | custom-call | bytes 7077888 | tf_op jit(solution)/shard_map/assemble/pallas_call | solution.py:537
  59.5 7.9 %attend.3 = (bf16[1024,256]{1,0:T(8,128)(2,1)}, bf16[1024,256]{1,0:T(8,128)(2,1)}, bf16[1024,256]{1,0:T(8,128)(2,1)}, bf16[1024,256]{1,0:T(8,128)(2,1)}, f32[2,8,512]{2,1,0:T(8,128)}) custom-call(bf16[1024,768]{1,0:T(8,128)(2,1)} %tok.10, bf16[768,2304]{1,0:T(8,128)(2,1)} %assemble.1.wq.wk.wv, bf16[768,2304]{1,0:T(8,128)(2,1)} %assemble.1.wq.wk.wv, ...), custom_call_target="tpu_custom_call" | custom-call | flops 4000000000 | bytes 5000000 | tf_op jit(solution)/shard_map/attend/pallas_call | solution.py:80
  76.4 7.9 %attend.4 = (bf16[1024,256]{1,0:T(8,128)(2,1)}, bf16[1024,256]{1,0:T(8,128)(2,1)}, bf16[1024,256]{1,0:T(8,128)(2,1)}, bf16[1024,256]{1,0:T(8,128)(2,1)}, f32[2,8,512]{2,1,0:T(8,128)}) custom-call(bf16[1024,768]{1,0:T(8,128)(2,1)} %tok.10, bf16[768,2304]{1,0:T(8,128)(2,1)} %assemble.1.wq.wk.wv, bf16[768,2304]{1,0:T(8,128)(2,1)} %assemble.1.wq.wk.wv, ...), custom_call_target="tpu_custom_call" | custom-call | flops 4000000000 | bytes 5000000 | tf_op jit(solution)/shard_map/attend/pallas_call | solution.py:80
  85.7 7.2 %collective-permute-done.21 = bf16[480,384]{1,0:T(8,128)(2,1)S(1)} collective-permute-done((bf16[480,384]{1,0:T(8,128)(2,1)S(1)}, bf16[480,384]{1,0:T(8,128)(2,1)S(1)}, u32[]{:S(2)}, u32[]{:S(2)}) %collective-permute-start.21) | collective-permute-done | bytes 368672 | tf_op jit(solution)/shard_map/ppermute | solution.py:471
  95.5 7.9 %attend.5 = (bf16[1024,256]{1,0:T(8,128)(2,1)}, bf16[1024,256]{1,0:T(8,128)(2,1)}, bf16[1024,256]{1,0:T(8,128)(2,1)}, bf16[1024,256]{1,0:T(8,128)(2,1)}, f32[2,8,512]{2,1,0:T(8,128)}) custom-call(bf16[1024,768]{1,0:T(8,128)(2,1)} %tok.10, bf16[768,2304]{1,0:T(8,128)(2,1)} %assemble.1.wq.wk.wv, bf16[768,2304]{1,0:T(8,128)(2,1)} %assemble.1.wq.wk.wv, ...), custom_call_target="tpu_custom_call" | custom-call | flops 4000000000 | bytes 5000000 | tf_op jit(solution)/shard_map/attend/pallas_call | solution.py:80
  103.4 5.5 %collective-permute-done.22.refs_16_ = bf16[3,240,384]{2,1,0:T(8,128)(2,1)} collective-permute-done((bf16[3,240,384]{2,1,0:T(8,128)(2,1)S(1)}, bf16[3,240,384]{2,1,0:T(8,128)(2,1)}, u32[]{:S(2)}, u32[]{:S(2)}) %collective-permute-start.22) | collective-permute-done | bytes 552992 | tf_op jit(solution)/shard_map/ppermute | solution.py:471
  112.9 44.1 %middle.1 = (bf16[1024,768]{1,0:T(8,128)(2,1)}, bf16[1024,768]{1,0:T(8,128)(2,1)}, bf16[1024,3072]{1,0:T(8,128)(2,1)}, bf16[1024,768]{1,0:T(8,128)(2,1)}, bf16[1...) custom-call(s32[4]{0:T(128)} %pad_add_fusion.at_r, ...), custom_call_target="tpu_custom_call" | custom-call | flops 30000001024 | bytes 40000000 | tf_op jit(solution)/shard_map/middle/pallas_call | solution.py:335
  157.0 15.7 %grad_down.1 = (bf16[2,2,4,240,384]{4,3,2,1,0:T(8,128)(2,1)}, bf16[2,2,4,240,384]{4,3,2,1,0:T(8,128)(2,1)}) custom-call(s32[4]{0:T(128)} %pad_add_fusion.at_r, bf16[1024,256]{1,0:T(8,128)(2,1)} %get-tuple-element.138.refs_0_.ctx_r, bf16[1024,256]{1,0:T(8,128)(2,1)} %get-tuple-element.143.refs_1_.ctx_r, bf16[1024,256]{1,0:T(8,128)(2,1)} %get-tuple-element.151.refs_2_.ctx_r, ...), custom_call_target="tpu_custom_call" | custom-call | flops 8999999488 | bytes 14000000 | tf_op jit(solution)/shard_map/grad_down/pallas_call | solution.py:395
  172.9 13.7 %grad_up.1 = (bf16[2,2,2,4,96,384]{5,4,3,2,1,0:T(8,128)(2,1)}, bf16[2,2,2,4,96,384]{5,4,3,2,1,0:T(8,128)(2,1)}) custom-call(s32[4]{0:T(128)} %pad_add_fusion.at_r, bf16[1024,768]{1,0:T(8,128)(2,1)} %get-tuple-element.178.low, bf16[1024,3072]{1,0:T(8,128)(2,1)} %get-tuple-element.179.gu), custom_call_target="tpu_custom_call" | custom-call | flops 8999999488 | bytes 14000000 | tf_op jit(solution)/shard_map/grad_up/pallas_call | solution.py:437
  193.6 13.6 %attend_back.3 = (bf16[2,2,4,96,384]{4,3,2,1,0:T(8,128)(2,1)}, bf16[2,2,4,96,384]{4,3,2,1,0:T(8,128)(2,1)}, f32[1024,768]{1,0:T(8,128)}, f32[1,768]{1,0:T(1,128)}) custom-call(s32[4]{0:T(128)} %pad_add_fusion.at_r, bf16[1024,256]{1,0:T(8,128)(2,1)} %get-tuple-element.168.q_r, bf16[1024,256]{1,0:T(8,128)(2,1)} %get-tuple-element.169.k_r, ...), custom_call_target="tpu_custom_call" | custom-call | flops 8000000000 | bytes 8000000 | tf_op jit(solution)/shard_map/attend_back/pallas_call | solution.py:219
  221.2 14.1 %attend_back.4 = (bf16[2,2,4,96,384]{4,3,2,1,0:T(8,128)(2,1)}, bf16[2,2,4,96,384]{4,3,2,1,0:T(8,128)(2,1)}, f32[1024,768]{1,0:T(8,128)}, f32[1,768]{1,0:T(1,128)}) custom-call(s32[4]{0:T(128)} %pad_add_fusion.at_r, bf16[1024,256]{1,0:T(8,128)(2,1)} %get-tuple-element.164.q_r, ...), custom_call_target="tpu_custom_call", output_to_operand_aliasing={{0}: (14, {}), {1}: (15, {})} | custom-call | flops 8000000000 | bytes 8000000 | tf_op jit(solution)/shard_map/attend_back/pallas_call | solution.py:219
  240.2 14.2 %attend_back.5 = (bf16[2,2,4,64,384]{4,3,2,1,0:T(8,128)(2,1)}, bf16[2,2,4,64,384]{4,3,2,1,0:T(8,128)(2,1)}, bf16[1024,768]{1,0:T(8,128)(2,1)}, f32[1,768]{1,0:T(1,128)}) custom-call(s32[4]{0:T(128)} %pad_add_fusion.at_r, bf16[1024,256]{1,0:T(8,128)(2,1)} %get-tuple-element.159.q_r, bf16[1024,256]{1,0:T(8,128)(2,1)} %get-tuple-element.160.k_r, ...), custom_call_target="tpu_custom_call" | custom-call | flops 8000000000 | bytes 8000000 | tf_op jit(solution)/shard_map/attend_back/pallas_call | solution.py:219
  255.2 3.0 collective-permute-start.46
  266.3 7.4 %collective-permute-done.45 = bf16[2,96,384]{2,1,0:T(8,128)(2,1)S(1)} collective-permute-done((bf16[2,96,384]{2,1,0:T(8,128)(2,1)S(1)}, bf16[2,96,384]{2,1,0:T(8,128)(2,1)S(1)}, u32[]{:S(2)}, u32[]{:S(2)}) %collective-permute-start.45) | collective-permute-done | bytes 147488 | tf_op jit(solution)/shard_map/ppermute | solution.py:471
  279.4 3.3 %collective-permute-done.52 = bf16[336,384]{1,0:T(8,128)(2,1)S(1)} collective-permute-done((bf16[336,384]{1,0:T(8,128)(2,1)S(1)}, bf16[336,384]{1,0:T(8,128)(2,1)S(1)}, u32[]{:S(2)}, u32[]{:S(2)}) %collective-permute-start.52) | collective-permute-done | bytes 258080 | tf_op jit(solution)/shard_map/ppermute | solution.py:471
  286.1 4.6 %collective-permute-done.53.refs_3_ = bf16[432,384]{1,0:T(8,128)(2,1)S(1)} collective-permute-done((bf16[432,384]{1,0:T(8,128)(2,1)S(1)}, bf16[432,384]{1,0:T(8,128)(2,1)S(1)}, u32[]{:S(2)}, u32[]{:S(2)}) %collective-permute-start.53) | collective-permute-done | bytes 331808 | tf_op jit(solution)/shard_map/ppermute | solution.py:471
  295.0 4.5 %collective-permute-done.48 = bf16[2,160,384]{2,1,0:T(8,128)(2,1)S(1)} collective-permute-done((bf16[2,160,384]{2,1,0:T(8,128)(2,1)S(1)}, bf16[2,160,384]{2,1,0:T(8,128)(2,1)S(1)}, u32[]{:S(2)}, u32[]{:S(2)}) %collective-permute-start.48) | collective-permute-done | bytes 245792 | tf_op jit(solution)/shard_map/ppermute | solution.py:471
  (283 shorter events, 105.1 us)
Async XLA Ops:
  7.7 15.4 %collective-permute-start.4 = (bf16[480,768]{1,0:T(8,128)(2,1)S(1)}, bf16[480,768]{1,0:T(8,128)(2,1)}, u32[]{:S(2)}, u32[]{:S(2)}) collective-permute-start(bf16[480,768]{1,0:T(8,128)(2,1)S(1)} %pad_maximum_fusion.2.refs_14_), channel_id=1, source_target_pairs={{0,1},{1,0},{2,3},{3,2},{4,5},{5,4},{6,7},{7,6},{8,9},{9,8},{10,11... | collective-permute-start | bytes 2211848 | tf_op jit(solution)/shard_map/ppermute | solution.py:471
  7.8 15.2 %collective-permute-start.2 = (bf16[104,2304]{1,0:T(8,128)(2,1)S(1)}, bf16[104,2304]{1,0:T(8,128)(2,1)S(1)}, u32[]{:S(2)}, u32[]{:S(2)}) collective-permute-start(bf16[104,2304]{1,0:T(8,128)(2,1)S(1)} %fusion.11.refs_0_), channel_id=1, source_target_pairs={{0,1},{1,0},{2,3},{3,2},{4,5},{5,4},{6,7},{7,6},{8,9},{9,8},{10,11... | collective-permute-start | bytes 1437704 | tf_op jit(solution)/shard_map/ppermute | solution.py:471
  49.1 19.4 %collective-permute-start.16 = (bf16[480,384]{1,0:T(8,128)(2,1)S(1)}, bf16[480,384]{1,0:T(8,128)(2,1)S(1)}, u32[]{:S(2)}, u32[]{:S(2)}) collective-permute-start(bf16[480,384]{1,0:T(8,128)(2,1)S(1)} %pad_maximum_fusion.9), channel_id=1, source_target_pairs={{0,4},{1,5},{2,6},{3,7},{4,0},{5,1},{6,2},{7,3},{8,12},{9,13},{10,... | collective-permute-start | bytes 1105928 | tf_op jit(solution)/shard_map/ppermute | solution.py:471
  51.3 16.1 %collective-permute-start.14 = (bf16[3,48,768]{2,1,0:T(8,128)(2,1)}, bf16[3,48,768]{2,1,0:T(8,128)(2,1)}, u32[]{:S(2)}, u32[]{:S(2)}) collective-permute-start(bf16[3,48,768]{2,1,0:T(8,128)(2,1)} %get-tuple-element.301), channel_id=1, source_target_pairs={{0,8},{1,9},{2,10},{3,11},{4,12},{5,13},{6,14},{7,15},{8,0},{9,1},... | collective-permute-start | bytes 663560 | tf_op jit(solution)/shard_map/ppermute | solution.py:471
  51.9 15.6 %collective-permute-start.15 = (bf16[3,48,768]{2,1,0:T(8,128)(2,1)}, bf16[3,48,768]{2,1,0:T(8,128)(2,1)}, u32[]{:S(2)}, u32[]{:S(2)}) collective-permute-start(bf16[3,48,768]{2,1,0:T(8,128)(2,1)} %get-tuple-element.300), channel_id=1, source_target_pairs={{0,16},{1,17},{2,18},{3,19},{4,20},{5,21},{6,22},{7,23},{8,24},{9,... | collective-permute-start | bytes 663560 | tf_op jit(solution)/shard_map/ppermute | solution.py:471
  69.6 23.2 %collective-permute-start.18 = (bf16[2,3,48,768]{3,2,1,0:T(8,128)(2,1)S(1)}, bf16[2,3,48,768]{3,2,1,0:T(8,128)(2,1)S(1)}, u32[]{:S(2)}, u32[]{:S(2)}) collective-permute-start(bf16[2,3,48,768]{3,2,1,0:T(8,128)(2,1)S(1)} %pad_maximum_fusion.8.refs_8_), channel_id=1, source_target_pairs={{0,8},{1,9},{2,10},{3,11},{4,12},{5,13},{6,14},{7,15},{8,0},{9,1},... | collective-permute-start | bytes 1327112 | tf_op jit(solution)/shard_map/ppermute | solution.py:471
  71.2 21.6 %collective-permute-start.17 = (bf16[2,3,48,768]{3,2,1,0:T(8,128)(2,1)S(1)}, bf16[2,3,48,768]{3,2,1,0:T(8,128)(2,1)S(1)}, u32[]{:S(2)}, u32[]{:S(2)}) collective-permute-start(bf16[2,3,48,768]{3,2,1,0:T(8,128)(2,1)S(1)} %pad_maximum_fusion.7.refs_7_), channel_id=1, source_target_pairs={{0,16},{1,17},{2,18},{3,19},{4,20},{5,21},{6,22},{7,23},{8,24},{9,... | collective-permute-start | bytes 1327112 | tf_op jit(solution)/shard_map/ppermute | solution.py:471
  72.4 20.5 %collective-permute-start.19 = (bf16[2,3,48,768]{3,2,1,0:T(8,128)(2,1)S(1)}, bf16[2,3,48,768]{3,2,1,0:T(8,128)(2,1)S(1)}, u32[]{:S(2)}, u32[]{:S(2)}) collective-permute-start(bf16[2,3,48,768]{3,2,1,0:T(8,128)(2,1)S(1)} %pad_maximum_fusion.7.refs_7_), channel_id=1, source_target_pairs={{0,1},{1,0},{2,3},{3,2},{4,5},{5,4},{6,7},{7,6},{8,9},{9,8},{10,11... | collective-permute-start | bytes 1327112 | tf_op jit(solution)/shard_map/ppermute | solution.py:471
  74.0 18.8 %collective-permute-start.21 = (bf16[480,384]{1,0:T(8,128)(2,1)S(1)}, bf16[480,384]{1,0:T(8,128)(2,1)S(1)}, u32[]{:S(2)}, u32[]{:S(2)}) collective-permute-start(bf16[480,384]{1,0:T(8,128)(2,1)S(1)} %copy-done.19), channel_id=1, source_target_pairs={{0,6},{1,7},{2,0},{3,1},{4,2},{5,3},{6,4},{7,5},{8,14},{9,15},{10,... | collective-permute-start | bytes 1105928 | tf_op jit(solution)/shard_map/ppermute | solution.py:471
  93.0 16.1 %collective-permute-start.26 = (bf16[3,480,384]{2,1,0:T(8,128)(2,1)S(1)}, bf16[3,480,384]{2,1,0:T(8,128)(2,1)}, u32[]{:S(2)}, u32[]{:S(2)}) collective-permute-start(bf16[3,480,384]{2,1,0:T(8,128)(2,1)S(1)} %pad_maximum_fusion.refs_15_), channel_id=1, source_target_pairs={{0,1},{1,0},{2,3},{3,2},{4,5},{5,4},{6,7},{7,6},{8,9},{9,8},{10,11... | collective-permute-start | bytes 3317768 | tf_op jit(solution)/shard_map/ppermute | solution.py:471
  93.6 15.5 %collective-permute-start.25 = (bf16[2,2,3,48,768]{4,3,2,1,0:T(8,128)(2,1)S(1)}, bf16[2,2,3,48,768]{4,3,2,1,0:T(8,128)(2,1)}, u32[]{:S(2)}, u32[]{:S(2)}) collective-permute-start(bf16[2,2,3,48,768]{4,3,2,1,0:T(8,128)(2,1)S(1)} %pad_maximum_fusion.1.refs_9_), channel_id=1, source_target_pairs={{0,1},{1,0},{2,3},{3,2},{4,5},{5,4},{6,7},{7,6},{8,9},{9,8},{10,11... | collective-permute-start | bytes 2654216 | tf_op jit(solution)/shard_map/ppermute | solution.py:471
  172.7 16.1 %collective-permute-start.29 = (bf16[2,2,4,240,384]{4,3,2,1,0:T(8,128)(2,1)}, bf16[2,2,4,240,384]{4,3,2,1,0:T(8,128)(2,1)}, u32[]{:S(2)}, u32[]{:S(2)}) collective-permute-start(bf16[2,2,4,240,384]{4,3,2,1,0:T(8,128)(2,1)} %get-tuple-element.175), channel_id=1, source_target_pairs={{0,1},{1,0},{2,3},{3,2},{4,5},{5,4},{6,7},{7,6},{8,9},{9,8},{10,11... | collective-permute-start | bytes 8847368 | tf_op jit(solution)/shard_map/ppermute | solution.py:471
  186.5 20.7 %collective-permute-start.32 = (bf16[2,2,2,4,96,384]{5,4,3,2,1,0:T(8,128)(2,1)}, bf16[2,2,2,4,96,384]{5,4,3,2,1,0:T(8,128)(2,1)}, u32[]{:S(2)}, u32[]{:S(2)}) collective-permute-start(bf16[2,2,2,4,96,384]{5,4,3,2,1,0:T(8,128)(2,1)} %get-tuple-element.180), channel_id=1, source_target_pairs={{0,1},{1,0},{2,3},{3,2},{4,5},{5,4},{6,7},{7,6},{8,9},{9,8},{10,11... | collective-permute-start | bytes 7077896 | tf_op jit(solution)/shard_map/ppermute | solution.py:471
  191.7 20.6 %collective-permute-start.30 = (bf16[4,240,384]{2,1,0:T(8,128)(2,1)}, bf16[4,240,384]{2,1,0:T(8,128)(2,1)}, u32[]{:S(2)}, u32[]{:S(2)}) collective-permute-start(bf16[4,240,384]{2,1,0:T(8,128)(2,1)} %get-tuple-element.251), channel_id=1, source_target_pairs={{0,8},{1,9},{2,10},{3,11},{4,12},{5,13},{6,14},{7,15},{8,0},{9,1},... | collective-permute-start | bytes 2211848 | tf_op jit(solution)/shard_map/ppermute | solution.py:471
  193.1 19.1 %collective-permute-start.31 = (bf16[4,240,384]{2,1,0:T(8,128)(2,1)}, bf16[4,240,384]{2,1,0:T(8,128)(2,1)}, u32[]{:S(2)}, u32[]{:S(2)}) collective-permute-start(bf16[4,240,384]{2,1,0:T(8,128)(2,1)} %get-tuple-element.250), channel_id=1, source_target_pairs={{0,16},{1,17},{2,18},{3,19},{4,20},{5,21},{6,22},{7,23},{8,24},{9,... | collective-permute-start | bytes 2211848 | tf_op jit(solution)/shard_map/ppermute | solution.py:471
  210.2 25.2 %collective-permute-start.33 = (bf16[2,4,96,384]{3,2,1,0:T(8,128)(2,1)}, bf16[2,4,96,384]{3,2,1,0:T(8,128)(2,1)}, u32[]{:S(2)}, u32[]{:S(2)}) collective-permute-start(bf16[2,4,96,384]{3,2,1,0:T(8,128)(2,1)} %get-tuple-element.259), channel_id=1, source_target_pairs={{0,8},{1,9},{2,10},{3,11},{4,12},{5,13},{6,14},{7,15},{8,0},{9,1},... | collective-permute-start | bytes 1769480 | tf_op jit(solution)/shard_map/ppermute | solution.py:471
  211.1 24.3 %collective-permute-start.34 = (bf16[2,4,96,384]{3,2,1,0:T(8,128)(2,1)}, bf16[2,4,96,384]{3,2,1,0:T(8,128)(2,1)}, u32[]{:S(2)}, u32[]{:S(2)}) collective-permute-start(bf16[2,4,96,384]{3,2,1,0:T(8,128)(2,1)} %get-tuple-element.258), channel_id=1, source_target_pairs={{0,16},{1,17},{2,18},{3,19},{4,20},{5,21},{6,22},{7,23},{8,24},{9,... | collective-permute-start | bytes 1769480 | tf_op jit(solution)/shard_map/ppermute | solution.py:471
  216.4 38.6 %collective-permute-start.43 = (bf16[2,240,384]{2,1,0:T(8,128)(2,1)}, bf16[2,240,384]{2,1,0:T(8,128)(2,1)S(1)}, u32[]{:S(2)}, u32[]{:S(2)}) collective-permute-start(bf16[2,240,384]{2,1,0:T(8,128)(2,1)} %pad_maximum_fusion.12), channel_id=1, source_target_pairs={{0,6},{1,7},{2,0},{3,1},{4,2},{5,3},{6,4},{7,5},{8,14},{9,15},{10,... | collective-permute-start | bytes 1105928 | tf_op jit(solution)/shard_map/ppermute | solution.py:471
  219.1 36.0 %collective-permute-start.42 = (bf16[2,240,384]{2,1,0:T(8,128)(2,1)}, bf16[2,240,384]{2,1,0:T(8,128)(2,1)}, u32[]{:S(2)}, u32[]{:S(2)}) collective-permute-start(bf16[2,240,384]{2,1,0:T(8,128)(2,1)} %pad_maximum_fusion.11), channel_id=1, source_target_pairs={{0,4},{1,5},{2,6},{3,7},{4,0},{5,1},{6,2},{7,3},{8,12},{9,13},{10,... | collective-permute-start | bytes 1105928 | tf_op jit(solution)/shard_map/ppermute | solution.py:471
  220.4 34.6 %collective-permute-start.41 = (bf16[2,240,384]{2,1,0:T(8,128)(2,1)}, bf16[2,240,384]{2,1,0:T(8,128)(2,1)}, u32[]{:S(2)}, u32[]{:S(2)}) collective-permute-start(bf16[2,240,384]{2,1,0:T(8,128)(2,1)} %pad_maximum_fusion.10), channel_id=1, source_target_pairs={{0,2},{1,3},{2,4},{3,5},{4,6},{5,7},{6,0},{7,1},{8,10},{9,11},{10,... | collective-permute-start | bytes 1105928 | tf_op jit(solution)/shard_map/ppermute | solution.py:471
  238.1 16.3 %collective-permute-start.35 = (bf16[4,96,384]{2,1,0:T(8,128)(2,1)}, bf16[4,96,384]{2,1,0:T(8,128)(2,1)S(1)}, u32[]{:S(2)}, u32[]{:S(2)}) collective-permute-start(bf16[4,96,384]{2,1,0:T(8,128)(2,1)} %get-tuple-element.256), channel_id=1, source_target_pairs={{0,16},{1,17},{2,18},{3,19},{4,20},{5,21},{6,22},{7,23},{8,24},{9,... | collective-permute-start | bytes 884744 | tf_op jit(solution)/shard_map/ppermute | solution.py:471
  276.4 18.6 %collective-permute-start.49 = (bf16[2,160,384]{2,1,0:T(8,128)(2,1)S(1)}, bf16[2,160,384]{2,1,0:T(8,128)(2,1)S(1)}, u32[]{:S(2)}, u32[]{:S(2)}) collective-permute-start(bf16[2,160,384]{2,1,0:T(8,128)(2,1)S(1)} %pad_maximum_fusion.18), channel_id=1, source_target_pairs={{0,6},{1,7},{2,0},{3,1},{4,2},{5,3},{6,4},{7,5},{8,14},{9,15},{10,... | collective-permute-start | bytes 737288 | tf_op jit(solution)/shard_map/ppermute | solution.py:471
  278.8 20.7 %collective-permute-start.48 = (bf16[2,160,384]{2,1,0:T(8,128)(2,1)S(1)}, bf16[2,160,384]{2,1,0:T(8,128)(2,1)S(1)}, u32[]{:S(2)}, u32[]{:S(2)}) collective-permute-start(bf16[2,160,384]{2,1,0:T(8,128)(2,1)S(1)} %pad_maximum_fusion.17), channel_id=1, source_target_pairs={{0,4},{1,5},{2,6},{3,7},{4,0},{5,1},{6,2},{7,3},{8,12},{9,13},{10,... | collective-permute-start | bytes 737288 | tf_op jit(solution)/shard_map/ppermute | solution.py:471
  284.1 15.4 %collective-permute-start.47 = (bf16[2,160,384]{2,1,0:T(8,128)(2,1)S(1)}, bf16[2,160,384]{2,1,0:T(8,128)(2,1)S(1)}, u32[]{:S(2)}, u32[]{:S(2)}) collective-permute-start(bf16[2,160,384]{2,1,0:T(8,128)(2,1)S(1)} %pad_maximum_fusion.16), channel_id=1, source_target_pairs={{0,2},{1,3},{2,4},{3,5},{4,6},{5,7},{6,0},{7,1},{8,10},{9,11},{10,... | collective-permute-start | bytes 737288 | tf_op jit(solution)/shard_map/ppermute | solution.py:471
  (73 other events, 627.0 us)

commit v5 on v4

--- a/solution.py
+++ b/solution.py
@@ -49,10 +49,9 @@
     length, width = q.shape
     lane = lax.broadcasted_iota(jnp.int32, (length, width), 1) // HD
     slot = lax.broadcasted_iota(jnp.int32, (length, 128), 1)
-    acc = None
-    scale = jnp.zeros((length, width), f32)
-    stat = jnp.zeros((length, 128), f32)
-    for h in range(width // HD):
+
+    def head(h, state):
+        acc, scale, stat = state
         mine = lane == h
         qa = jnp.where(mine, q, aq[...])
         ka = jnp.where(mine, k, ak[...])
@@ -61,10 +60,11 @@
         m = jnp.max(t, axis=1, keepdims=True)
         p = jnp.exp2(t - m)
         total = jnp.sum(p, axis=1, keepdims=True)
-        part = nn(p.astype(bf16), va)
-        acc = part if acc is None else acc + part
-        scale = jnp.where(mine, 1.0 / total, scale)
-        stat = jnp.where(slot == h, m + jnp.log2(total), stat)
+        acc = acc + nn(p.astype(bf16), va)
+        return acc, jnp.where(mine, 1.0 / total, scale), jnp.where(slot == h, m + jnp.log2(total), stat)
+
+    zero = jnp.zeros((length, width), f32)
+    acc, scale, stat = lax.fori_loop(0, width // HD, head, (zero, zero, jnp.zeros((length, 128), f32)))
     ctx_o[...] = (acc * scale).astype(bf16)
     lse_o[0] = stat.T[:8]
 
@@ -106,13 +106,13 @@
     b = pl.program_id(0)
     last = b == pl.num_programs(0) - 1
     if mode == "plain":
-        dw_o, dx_o, db_o, dw_s = rest
+        dw_o, dx_o, db_o, dw_s, delta_s = rest
     elif mode == "first":
-        own_o, other_o, dx_o, db_o, dw_s = rest
+        own_o, other_o, dx_o, db_o, dw_s, delta_s = rest
     elif mode == "second":
-        _, _, own_o, other_o, dx_o, db_o, dw_s = rest
+        _, _, own_o, other_o, dx_o, db_o, dw_s, delta_s = rest
     else:
-        db0, db1, tbl, own_o, other_o, dx_o, db_o, dw_s = rest
+        db0, db1, tbl, own_o, other_o, dx_o, db_o, dw_s, delta_s = rest
     q, k, v, do = q_r[...], k_r[...], v_r[...], do_r[...]
     length, width = q.shape
     lane = lax.broadcasted_iota(jnp.int32, (length, width), 1) // HD
@@ -121,23 +121,24 @@
     prod = do.astype(f32) * ctx_r[...].astype(f32)
     hi = prod.astype(bf16)
     lo = (prod - hi.astype(f32)).astype(bf16)
-    delta = nt(sel, hi) + nt(sel, lo)
-    dq = dk = dv = None
+    delta_s[...] = nt(sel, hi) + nt(sel, lo)
     zero = jnp.zeros_like(q)
-    for h in range(width // HD):
+
+    def head(h, state):
+        dq, dk, dv = state
         mine = lane == h
         qa = jnp.where(mine, q, aq[...])
         ka = jnp.where(mine, k, ak[...])
         va = jnp.where(mine, v, zero)
-        p = jnp.exp2(nt(ka, qa) * SCALE - lse_r[0, h : h + 1, :])
+        p = jnp.exp2(nt(ka, qa) * SCALE - lse_r[0, pl.ds(h, 1), :])
         dp = nt(va, do)
-        ds = (p * (dp - delta[h : h + 1, :])).astype(bf16)
-        dv_h = nn(p.astype(bf16), jnp.where(mine, do, zero))
-        dk_h = nn(ds, jnp.where(mine, q, zero))
-        dq_h = tn(ds, jnp.where(mine, k, zero))
-        dv = dv_h if dv is None else dv + dv_h
-        dk = dk_h if dk is None else dk + dk_h
-        dq = dq_h if dq is None else dq + dq_h
+        ds = (p * (dp - delta_s[pl.ds(h, 1), :])).astype(bf16)
+        dv = dv + nn(p.astype(bf16), jnp.where(mine, do, zero))
+        dk = dk + nn(ds, jnp.where(mine, q, zero))
+        dq = dq + tn(ds, jnp.where(mine, k, zero))
+        return dq, dk, dv
+
+    dq, dk, dv = lax.fori_loop(0, width // HD, head, (jnp.zeros((length, width), f32),) * 3)
     dq = (dq * 0.125).astype(bf16)
     dk = (dk * 0.125).astype(bf16)
     dv = dv.astype(bf16)
@@ -222,7 +223,7 @@
         in_specs=in_specs,
         out_specs=out_specs,
         out_shape=out_shape,
-        scratch_shapes=[pltpu.VMEM((width, 3 * GW), f32)],
+        scratch_shapes=[pltpu.VMEM((width, 3 * GW), f32), pltpu.VMEM((8, length), f32)],
         input_output_aliases=aliases,
         compiler_params=params(),
         cost_estimate=cost(8_000_000_000, 8_000_000),
@@ -275,15 +276,17 @@
     normed = n1 * g1 + s1
     low = normed.astype(bf16)
     low_o[...] = low
-    acc = normed + bd
-    for c in range(chunks):
-        cols = slice(c * step, (c + 1) * step)
+
+    def forward(c, acc):
+        cols = pl.ds(pl.multiple_of(c * step, 128), step)
         hp = nn(low, wu[:, cols]) + bu[:, cols].astype(f32)
         cdf, pdf = phi(hp)
         slope[:, cols] = cdf + hp * pdf
         hid = (hp * cdf).astype(bf16)
         hid_o[:, cols] = hid
-        acc = acc + nn(hid, wd[cols, :])
+        return acc + nn(hid, wd[cols, :])
+
+    acc = lax.fori_loop(0, chunks, forward, normed + bd)
     centre = acc - mean(acc)
     r2 = lax.rsqrt(mean(centre * centre) + 1e-05)
     n2 = centre * r2
@@ -305,12 +308,14 @@
         def _():
             ref[at] += v
 
-    for c in range(chunks):
-        cols = slice(c * step, (c + 1) * step)
+    def backward(c, acc):
+        cols = pl.ds(pl.multiple_of(c * step, 128), step)
         gu = (nt(gd, wd[cols, :]) * slope[:, cols]).astype(bf16)
         gu_o[:, cols] = gu
         put(bup_o, (slice(0, 1), cols), total(gu.astype(f32)))
-        acc = acc + nt(gu, wu[:, cols])
+        return acc + nt(gu, wu[:, cols])
+
+    acc = lax.fori_loop(0, chunks, backward, acc)
     e = acc * g1
     gp1 = r1 * (e - mean(e) - n1 * mean(e * n1))
     gb = gp1.astype(bf16)

time: 323 us -> 356 us (1.10); the launches traced: 317 us -> 357 us
  Pallas kernels: 148 us -> 196 us
  waiting for transfers between devices: 71.4 us -> 60.1 us
    pallas_call x3, Pallas kernels: 23.7 us -> 36.7 us  [attend(): pl.pallas_call(attend_kernel, grid=(seqs,), in_specs=[seq, col(0), col(1)...]
    pallas_call x1, Pallas kernels: 44.1 us -> 57 us  [middle(): pl.pallas_call(functools.partial(middle_kernel, len(ctx), split), grid=(r...]
    pallas_call x1, Pallas kernels: 13.7 us -> 25.8 us  [grad_up(): pl.pallas_call(grad_up_kernel, grid=(8,), in_specs=[SMEM, pl.BlockSpec((r...]
    ppermute x58, waiting for transfers between devices: 71.4 us -> 60.1 us  [send(): return lax.ppermute(a, AXES, where)]
    pallas_call x3, Pallas kernels: 41.9 us -> 52.1 us  [attend_back(): pl.pallas_call(functools.partial(attend_back_kernel, mode), grid=(seqs,),...]
  transfers between devices with their start and end apart: 58 -> 58, of which waited for: 22 -> 19; matrix products, arithmetic and copies ran while one was open for 10% -> 9% of each run, Pallas kernels for 27% -> 34%
where the time goes in v5:
time: 356 us; the launch traced here: 357 us
  Pallas kernels  196 us (55%)
  waiting for transfers between devices  60.1 us (17%)
  starting transfers between devices  56.6 us (16%)
  other arithmetic  27.9 us (8%)
  local copies, waits for them, and re-layouts  12.8 us (4%)
    ppermute x58, waiting for transfers between devices, send(): return lax.ppermute(a, AXES, where)  60.1 us
    pallas_call x1, Pallas kernels, middle(): pl.pallas_call(functools.partial(middle_kernel, len(ctx), split), grid=(r...  57 us
    ppermute x58, starting transfers between devices, send(): return lax.ppermute(a, AXES, where)  56.6 us
    pallas_call x3, Pallas kernels, attend_back(): pl.pallas_call(functools.partial(attend_back_kernel, mode), grid=(seqs,),...  52.1 us
    pallas_call x3, Pallas kernels, attend(): pl.pallas_call(attend_kernel, grid=(seqs,), in_specs=[seq, col(0), col(1)...  36.7 us
    pallas_call x1, Pallas kernels, grad_up(): pl.pallas_call(grad_up_kernel, grid=(8,), in_specs=[SMEM, pl.BlockSpec((r...  25.8 us
    pallas_call x1, Pallas kernels, grad_down(): pl.pallas_call(functools.partial(grad_down_kernel, len(ctx)), grid_spec=p...  15.7 us
    convert_element_type x18, other arithmetic, total(): return out.astype(bf16)  14.3 us
  transfers between devices with their start and end apart: 58, of which 19 were waited for; matrix products, arithmetic and copies ran while one was open for 9% of the time, Pallas kernels for 34%

profile of v5, /device:TPU:0, one launch (start us, length us, event | category | flops | bytes accessed | tf_op | source)
XLA Modules:
  0.0 356.7 jit_solution(7517642640361109975)
XLA Ops:
  3.3 3.1 collective-permute-start
  10.0 4.3 %collective-permute-done = bf16[104,1152]{1,0:T(8,128)(2,1)S(1)} collective-permute-done((bf16[104,1152]{1,0:T(8,128)(2,1)S(1)}, bf16[104,1152]{1,0:T(8,128)(2,1)S(1)}, u32[]{:S(2)}, u32[]{:S(2)}) %collective-permute-start) | collective-permute-done | bytes 239648 | tf_op jit(solution)/shard_map/ppermute | solution.py:476
  15.9 7.2 %collective-permute-done.1 = bf16[104,1152]{1,0:T(8,128)(2,1)S(1)} collective-permute-done((bf16[104,1152]{1,0:T(8,128)(2,1)S(1)}, bf16[104,1152]{1,0:T(8,128)(2,1)S(1)}, u32[]{:S(2)}, u32[]{:S(2)}) %collective-permute-start.1) | collective-permute-done | bytes 239648 | tf_op jit(solution)/shard_map/ppermute | solution.py:476
  24.3 6.8 %collective-permute-done.5 = bf16[104,1152]{1,0:T(8,128)(2,1)S(1)} collective-permute-done((bf16[104,1152]{1,0:T(8,128)(2,1)S(1)}, bf16[104,1152]{1,0:T(8,128)(2,1)S(1)}, u32[]{:S(2)}, u32[]{:S(2)}) %collective-permute-start.5) | collective-permute-done | bytes 239648 | tf_op jit(solution)/shard_map/ppermute | solution.py:476
  35.4 3.7 %collective-permute-start.8 = (bf16[96,768]{1,0:T(8,128)(2,1)}, bf16[96,768]{1,0:T(8,128)(2,1)S(1)}, u32[]{:S(2)}, u32[]{:S(2)}) collective-permute-start(bf16[96,768]{1,0:T(8,128)(2,1)} %constant_dynamic-slice_fusion.2), channel_id=1, source_target_pairs={{0,6},{1,7},{2,0},{3,1},{4,2},{5,3},{6,4},{7,5},{8,14},{9,15},{10,... | collective-permute-start | bytes 442376 | tf_op jit(solution)/shard_map/ppermute | solution.py:476
  39.8 3.3 collective-permute-done.6
  43.1 3.4 collective-permute-done.7
  55.4 4.0 %assemble.1.wq.wk.wv = bf16[768,2304]{1,0:T(8,128)(2,1)} custom-call(s32[4]{0:T(128)} %pad_add_fusion.at_r, bf16[104,2304]{1,0:T(8,128)(2,1)} %copy-done.4, bf16[3,104,1152]{2,1,0:T(8,128)(2,1)} %copy-done, bf16[3,48,1152]{2,1,0:T(8,128)(2,1)} %copy-done.23, bf16[3,48,1152]{2,1,0:T(8,128)(2,1)} %copy-done.22, bf16[104,2304]{1,0:T(8,128)(2,1)} %copy-done.13, ...), custom_call_target="tpu_custom_call" | custom-call | bytes 7077888 | tf_op jit(solution)/shard_map/assemble/pallas_call | solution.py:542
  59.5 12.2 %attend.3 = (bf16[1024,256]{1,0:T(8,128)(2,1)}, bf16[1024,256]{1,0:T(8,128)(2,1)}, bf16[1024,256]{1,0:T(8,128)(2,1)}, bf16[1024,256]{1,0:T(8,128)(2,1)}, f32[2,8,512]{2,1,0:T(8,128)}) custom-call(bf16[1024,768]{1,0:T(8,128)(2,1)} %tok.10, bf16[768,2304]{1,0:T(8,128)(2,1)} %assemble.1.wq.wk.wv, bf16[768,2304]{1,0:T(8,128)(2,1)} %assemble.1.wq.wk.wv, ...), custom_call_target="tpu_custom_call" | custom-call | flops 4000000000 | bytes 5000000 | tf_op jit(solution)/shard_map/attend/pallas_call | solution.py:80
  80.7 12.2 %attend.4 = (bf16[1024,256]{1,0:T(8,128)(2,1)}, bf16[1024,256]{1,0:T(8,128)(2,1)}, bf16[1024,256]{1,0:T(8,128)(2,1)}, bf16[1024,256]{1,0:T(8,128)(2,1)}, f32[2,8,512]{2,1,0:T(8,128)}) custom-call(bf16[1024,768]{1,0:T(8,128)(2,1)} %tok.10, bf16[768,2304]{1,0:T(8,128)(2,1)} %assemble.1.wq.wk.wv, bf16[768,2304]{1,0:T(8,128)(2,1)} %assemble.1.wq.wk.wv, ...), custom_call_target="tpu_custom_call" | custom-call | flops 4000000000 | bytes 5000000 | tf_op jit(solution)/shard_map/attend/pallas_call | solution.py:80
  92.9 4.2 %collective-permute-done.21 = bf16[480,384]{1,0:T(8,128)(2,1)S(1)} collective-permute-done((bf16[480,384]{1,0:T(8,128)(2,1)S(1)}, bf16[480,384]{1,0:T(8,128)(2,1)S(1)}, u32[]{:S(2)}, u32[]{:S(2)}) %collective-permute-start.21) | collective-permute-done | bytes 368672 | tf_op jit(solution)/shard_map/ppermute | solution.py:476
  99.8 12.2 %attend.5 = (bf16[1024,256]{1,0:T(8,128)(2,1)}, bf16[1024,256]{1,0:T(8,128)(2,1)}, bf16[1024,256]{1,0:T(8,128)(2,1)}, bf16[1024,256]{1,0:T(8,128)(2,1)}, f32[2,8,512]{2,1,0:T(8,128)}) custom-call(bf16[1024,768]{1,0:T(8,128)(2,1)} %tok.10, bf16[768,2304]{1,0:T(8,128)(2,1)} %assemble.1.wq.wk.wv, bf16[768,2304]{1,0:T(8,128)(2,1)} %assemble.1.wq.wk.wv, ...), custom_call_target="tpu_custom_call" | custom-call | flops 4000000000 | bytes 5000000 | tf_op jit(solution)/shard_map/attend/pallas_call | solution.py:80
  117.2 57.0 %middle.1 = (bf16[1024,768]{1,0:T(8,128)(2,1)}, bf16[1024,768]{1,0:T(8,128)(2,1)}, bf16[1024,3072]{1,0:T(8,128)(2,1)}, bf16[1024,768]{1,0:T(8,128)(2,1)}, bf16[1...) custom-call(s32[4]{0:T(128)} %pad_add_fusion.at_r, ...), custom_call_target="tpu_custom_call" | custom-call | flops 30000001024 | bytes 40000000 | tf_op jit(solution)/shard_map/middle/pallas_call | solution.py:340
  174.3 15.7 %grad_down.1 = (bf16[2,2,4,240,384]{4,3,2,1,0:T(8,128)(2,1)}, bf16[2,2,4,240,384]{4,3,2,1,0:T(8,128)(2,1)}) custom-call(s32[4]{0:T(128)} %pad_add_fusion.at_r, bf16[1024,256]{1,0:T(8,128)(2,1)} %get-tuple-element.138.refs_0_.ctx_r, bf16[1024,256]{1,0:T(8,128)(2,1)} %get-tuple-element.143.refs_1_.ctx_r, bf16[1024,256]{1,0:T(8,128)(2,1)} %get-tuple-element.151.refs_2_.ctx_r, ...), custom_call_target="tpu_custom_call" | custom-call | flops 8999999488 | bytes 14000000 | tf_op jit(solution)/shard_map/grad_down/pallas_call | solution.py:400
  190.1 25.8 %grad_up.1 = (bf16[2,2,2,4,96,384]{5,4,3,2,1,0:T(8,128)(2,1)}, bf16[2,2,2,4,96,384]{5,4,3,2,1,0:T(8,128)(2,1)}) custom-call(s32[4]{0:T(128)} %pad_add_fusion.at_r, bf16[1024,768]{1,0:T(8,128)(2,1)} %get-tuple-element.178.low, bf16[1024,3072]{1,0:T(8,128)(2,1)} %get-tuple-element.179.gu), custom_call_target="tpu_custom_call" | custom-call | flops 8999999488 | bytes 14000000 | tf_op jit(solution)/shard_map/grad_up/pallas_call | solution.py:442
  222.9 17.1 %attend_back.3 = (bf16[2,2,4,96,384]{4,3,2,1,0:T(8,128)(2,1)}, bf16[2,2,4,96,384]{4,3,2,1,0:T(8,128)(2,1)}, f32[1024,768]{1,0:T(8,128)}, f32[1,768]{1,0:T(1,128)}) custom-call(s32[4]{0:T(128)} %pad_add_fusion.at_r, bf16[1024,256]{1,0:T(8,128)(2,1)} %get-tuple-element.168.q_r, bf16[1024,256]{1,0:T(8,128)(2,1)} %get-tuple-element.169.k_r, ...), custom_call_target="tpu_custom_call" | custom-call | flops 8000000000 | bytes 8000000 | tf_op jit(solution)/shard_map/attend_back/pallas_call | solution.py:220
  240.0 2.9 fusion.6
  253.5 17.4 %attend_back.4 = (bf16[2,2,4,96,384]{4,3,2,1,0:T(8,128)(2,1)}, bf16[2,2,4,96,384]{4,3,2,1,0:T(8,128)(2,1)}, f32[1024,768]{1,0:T(8,128)}, f32[1,768]{1,0:T(1,128)}) custom-call(s32[4]{0:T(128)} %pad_add_fusion.at_r, bf16[1024,256]{1,0:T(8,128)(2,1)} %get-tuple-element.164.q_r, ...), custom_call_target="tpu_custom_call", output_to_operand_aliasing={{0}: (14, {}), {1}: (15, {})} | custom-call | flops 8000000000 | bytes 8000000 | tf_op jit(solution)/shard_map/attend_back/pallas_call | solution.py:220
  275.7 17.6 %attend_back.5 = (bf16[2,2,4,64,384]{4,3,2,1,0:T(8,128)(2,1)}, bf16[2,2,4,64,384]{4,3,2,1,0:T(8,128)(2,1)}, bf16[1024,768]{1,0:T(8,128)(2,1)}, f32[1,768]{1,0:T(1,128)}) custom-call(s32[4]{0:T(128)} %pad_add_fusion.at_r, bf16[1024,256]{1,0:T(8,128)(2,1)} %get-tuple-element.159.q_r, bf16[1024,256]{1,0:T(8,128)(2,1)} %get-tuple-element.160.k_r, ...), custom_call_target="tpu_custom_call" | custom-call | flops 8000000000 | bytes 8000000 | tf_op jit(solution)/shard_map/attend_back/pallas_call | solution.py:220
  294.2 3.3 collective-permute-start.46
  305.3 7.4 %collective-permute-done.45 = bf16[2,96,384]{2,1,0:T(8,128)(2,1)S(1)} collective-permute-done((bf16[2,96,384]{2,1,0:T(8,128)(2,1)S(1)}, bf16[2,96,384]{2,1,0:T(8,128)(2,1)S(1)}, u32[]{:S(2)}, u32[]{:S(2)}) %collective-permute-start.45) | collective-permute-done | bytes 147488 | tf_op jit(solution)/shard_map/ppermute | solution.py:476
  330.2 2.9 finish_ffn.1
  333.1 5.9 %collective-permute-done.48 = bf16[2,160,384]{2,1,0:T(8,128)(2,1)S(1)} collective-permute-done((bf16[2,160,384]{2,1,0:T(8,128)(2,1)S(1)}, bf16[2,160,384]{2,1,0:T(8,128)(2,1)S(1)}, u32[]{:S(2)}, u32[]{:S(2)}) %collective-permute-start.48) | collective-permute-done | bytes 245792 | tf_op jit(solution)/shard_map/ppermute | solution.py:476
  348.2 2.9 collective-permute-done.55.refs_1_
  (283 shorter events, 102.2 us)
Async XLA Ops:
  7.7 15.4 %collective-permute-start.4 = (bf16[480,768]{1,0:T(8,128)(2,1)S(1)}, bf16[480,768]{1,0:T(8,128)(2,1)}, u32[]{:S(2)}, u32[]{:S(2)}) collective-permute-start(bf16[480,768]{1,0:T(8,128)(2,1)S(1)} %pad_maximum_fusion.2.refs_14_), channel_id=1, source_target_pairs={{0,1},{1,0},{2,3},{3,2},{4,5},{5,4},{6,7},{7,6},{8,9},{9,8},{10,11... | collective-permute-start | bytes 2211848 | tf_op jit(solution)/shard_map/ppermute | solution.py:476
  49.0 22.7 %collective-permute-start.16 = (bf16[480,384]{1,0:T(8,128)(2,1)S(1)}, bf16[480,384]{1,0:T(8,128)(2,1)S(1)}, u32[]{:S(2)}, u32[]{:S(2)}) collective-permute-start(bf16[480,384]{1,0:T(8,128)(2,1)S(1)} %pad_maximum_fusion.9), channel_id=1, source_target_pairs={{0,4},{1,5},{2,6},{3,7},{4,0},{5,1},{6,2},{7,3},{8,12},{9,13},{10,... | collective-permute-start | bytes 1105928 | tf_op jit(solution)/shard_map/ppermute | solution.py:476
  51.3 20.4 %collective-permute-start.14 = (bf16[3,48,768]{2,1,0:T(8,128)(2,1)}, bf16[3,48,768]{2,1,0:T(8,128)(2,1)}, u32[]{:S(2)}, u32[]{:S(2)}) collective-permute-start(bf16[3,48,768]{2,1,0:T(8,128)(2,1)} %get-tuple-element.301), channel_id=1, source_target_pairs={{0,8},{1,9},{2,10},{3,11},{4,12},{5,13},{6,14},{7,15},{8,0},{9,1},... | collective-permute-start | bytes 663560 | tf_op jit(solution)/shard_map/ppermute | solution.py:476
  51.8 19.9 %collective-permute-start.15 = (bf16[3,48,768]{2,1,0:T(8,128)(2,1)}, bf16[3,48,768]{2,1,0:T(8,128)(2,1)}, u32[]{:S(2)}, u32[]{:S(2)}) collective-permute-start(bf16[3,48,768]{2,1,0:T(8,128)(2,1)} %get-tuple-element.300), channel_id=1, source_target_pairs={{0,16},{1,17},{2,18},{3,19},{4,20},{5,21},{6,22},{7,23},{8,24},{9,... | collective-permute-start | bytes 663560 | tf_op jit(solution)/shard_map/ppermute | solution.py:476
  72.9 24.3 %collective-permute-start.18 = (bf16[2,3,48,768]{3,2,1,0:T(8,128)(2,1)S(1)}, bf16[2,3,48,768]{3,2,1,0:T(8,128)(2,1)S(1)}, u32[]{:S(2)}, u32[]{:S(2)}) collective-permute-start(bf16[2,3,48,768]{3,2,1,0:T(8,128)(2,1)S(1)} %pad_maximum_fusion.8.refs_8_), channel_id=1, source_target_pairs={{0,8},{1,9},{2,10},{3,11},{4,12},{5,13},{6,14},{7,15},{8,0},{9,1},... | collective-permute-start | bytes 1327112 | tf_op jit(solution)/shard_map/ppermute | solution.py:476
  75.1 22.1 %collective-permute-start.17 = (bf16[2,3,48,768]{3,2,1,0:T(8,128)(2,1)S(1)}, bf16[2,3,48,768]{3,2,1,0:T(8,128)(2,1)S(1)}, u32[]{:S(2)}, u32[]{:S(2)}) collective-permute-start(bf16[2,3,48,768]{3,2,1,0:T(8,128)(2,1)S(1)} %pad_maximum_fusion.7.refs_7_), channel_id=1, source_target_pairs={{0,16},{1,17},{2,18},{3,19},{4,20},{5,21},{6,22},{7,23},{8,24},{9,... | collective-permute-start | bytes 1327112 | tf_op jit(solution)/shard_map/ppermute | solution.py:476
  76.6 20.5 %collective-permute-start.19 = (bf16[2,3,48,768]{3,2,1,0:T(8,128)(2,1)S(1)}, bf16[2,3,48,768]{3,2,1,0:T(8,128)(2,1)S(1)}, u32[]{:S(2)}, u32[]{:S(2)}) collective-permute-start(bf16[2,3,48,768]{3,2,1,0:T(8,128)(2,1)S(1)} %pad_maximum_fusion.7.refs_7_), channel_id=1, source_target_pairs={{0,1},{1,0},{2,3},{3,2},{4,5},{5,4},{6,7},{7,6},{8,9},{9,8},{10,11... | collective-permute-start | bytes 1327112 | tf_op jit(solution)/shard_map/ppermute | solution.py:476
  76.6 16.3 %collective-permute-start.20 = (bf16[480,384]{1,0:T(8,128)(2,1)S(1)}, bf16[480,384]{1,0:T(8,128)(2,1)S(1)}, u32[]{:S(2)}, u32[]{:S(2)}) collective-permute-start(bf16[480,384]{1,0:T(8,128)(2,1)S(1)} %copy-done.19), channel_id=1, source_target_pairs={{0,2},{1,3},{2,4},{3,5},{4,6},{5,7},{6,0},{7,1},{8,10},{9,11},{10,... | collective-permute-start | bytes 1105928 | tf_op jit(solution)/shard_map/ppermute | solution.py:476
  78.3 18.9 %collective-permute-start.21 = (bf16[480,384]{1,0:T(8,128)(2,1)S(1)}, bf16[480,384]{1,0:T(8,128)(2,1)S(1)}, u32[]{:S(2)}, u32[]{:S(2)}) collective-permute-start(bf16[480,384]{1,0:T(8,128)(2,1)S(1)} %copy-done.19), channel_id=1, source_target_pairs={{0,6},{1,7},{2,0},{3,1},{4,2},{5,3},{6,4},{7,5},{8,14},{9,15},{10,... | collective-permute-start | bytes 1105928 | tf_op jit(solution)/shard_map/ppermute | solution.py:476
  97.4 16.1 %collective-permute-start.26 = (bf16[3,480,384]{2,1,0:T(8,128)(2,1)S(1)}, bf16[3,480,384]{2,1,0:T(8,128)(2,1)}, u32[]{:S(2)}, u32[]{:S(2)}) collective-permute-start(bf16[3,480,384]{2,1,0:T(8,128)(2,1)S(1)} %pad_maximum_fusion.refs_15_), channel_id=1, source_target_pairs={{0,1},{1,0},{2,3},{3,2},{4,5},{5,4},{6,7},{7,6},{8,9},{9,8},{10,11... | collective-permute-start | bytes 3317768 | tf_op jit(solution)/shard_map/ppermute | solution.py:476
  98.0 15.5 %collective-permute-start.25 = (bf16[2,2,3,48,768]{4,3,2,1,0:T(8,128)(2,1)S(1)}, bf16[2,2,3,48,768]{4,3,2,1,0:T(8,128)(2,1)}, u32[]{:S(2)}, u32[]{:S(2)}) collective-permute-start(bf16[2,2,3,48,768]{4,3,2,1,0:T(8,128)(2,1)S(1)} %pad_maximum_fusion.1.refs_9_), channel_id=1, source_target_pairs={{0,1},{1,0},{2,3},{3,2},{4,5},{5,4},{6,7},{7,6},{8,9},{9,8},{10,11... | collective-permute-start | bytes 2654216 | tf_op jit(solution)/shard_map/ppermute | solution.py:476
  190.0 28.1 %collective-permute-start.29 = (bf16[2,2,4,240,384]{4,3,2,1,0:T(8,128)(2,1)}, bf16[2,2,4,240,384]{4,3,2,1,0:T(8,128)(2,1)}, u32[]{:S(2)}, u32[]{:S(2)}) collective-permute-start(bf16[2,2,4,240,384]{4,3,2,1,0:T(8,128)(2,1)} %get-tuple-element.175), channel_id=1, source_target_pairs={{0,1},{1,0},{2,3},{3,2},{4,5},{5,4},{6,7},{7,6},{8,9},{9,8},{10,11... | collective-permute-start | bytes 8847368 | tf_op jit(solution)/shard_map/ppermute | solution.py:476
  216.0 24.0 %collective-permute-start.32 = (bf16[2,2,2,4,96,384]{5,4,3,2,1,0:T(8,128)(2,1)}, bf16[2,2,2,4,96,384]{5,4,3,2,1,0:T(8,128)(2,1)}, u32[]{:S(2)}, u32[]{:S(2)}) collective-permute-start(bf16[2,2,2,4,96,384]{5,4,3,2,1,0:T(8,128)(2,1)} %get-tuple-element.180), channel_id=1, source_target_pairs={{0,1},{1,0},{2,3},{3,2},{4,5},{5,4},{6,7},{7,6},{8,9},{9,8},{10,11... | collective-permute-start | bytes 7077896 | tf_op jit(solution)/shard_map/ppermute | solution.py:476
  220.9 24.0 %collective-permute-start.30 = (bf16[4,240,384]{2,1,0:T(8,128)(2,1)}, bf16[4,240,384]{2,1,0:T(8,128)(2,1)}, u32[]{:S(2)}, u32[]{:S(2)}) collective-permute-start(bf16[4,240,384]{2,1,0:T(8,128)(2,1)} %get-tuple-element.251), channel_id=1, source_target_pairs={{0,8},{1,9},{2,10},{3,11},{4,12},{5,13},{6,14},{7,15},{8,0},{9,1},... | collective-permute-start | bytes 2211848 | tf_op jit(solution)/shard_map/ppermute | solution.py:476
  222.4 22.5 %collective-permute-start.31 = (bf16[4,240,384]{2,1,0:T(8,128)(2,1)}, bf16[4,240,384]{2,1,0:T(8,128)(2,1)}, u32[]{:S(2)}, u32[]{:S(2)}) collective-permute-start(bf16[4,240,384]{2,1,0:T(8,128)(2,1)} %get-tuple-element.250), channel_id=1, source_target_pairs={{0,16},{1,17},{2,18},{3,19},{4,20},{5,21},{6,22},{7,23},{8,24},{9,... | collective-permute-start | bytes 2211848 | tf_op jit(solution)/shard_map/ppermute | solution.py:476
  242.9 28.0 %collective-permute-start.33 = (bf16[2,4,96,384]{3,2,1,0:T(8,128)(2,1)}, bf16[2,4,96,384]{3,2,1,0:T(8,128)(2,1)}, u32[]{:S(2)}, u32[]{:S(2)}) collective-permute-start(bf16[2,4,96,384]{3,2,1,0:T(8,128)(2,1)} %get-tuple-element.259), channel_id=1, source_target_pairs={{0,8},{1,9},{2,10},{3,11},{4,12},{5,13},{6,14},{7,15},{8,0},{9,1},... | collective-permute-start | bytes 1769480 | tf_op jit(solution)/shard_map/ppermute | solution.py:476
  243.9 27.1 %collective-permute-start.34 = (bf16[2,4,96,384]{3,2,1,0:T(8,128)(2,1)}, bf16[2,4,96,384]{3,2,1,0:T(8,128)(2,1)}, u32[]{:S(2)}, u32[]{:S(2)}) collective-permute-start(bf16[2,4,96,384]{3,2,1,0:T(8,128)(2,1)} %get-tuple-element.258), channel_id=1, source_target_pairs={{0,16},{1,17},{2,18},{3,19},{4,20},{5,21},{6,22},{7,23},{8,24},{9,... | collective-permute-start | bytes 1769480 | tf_op jit(solution)/shard_map/ppermute | solution.py:476
  249.2 44.8 %collective-permute-start.43 = (bf16[2,240,384]{2,1,0:T(8,128)(2,1)}, bf16[2,240,384]{2,1,0:T(8,128)(2,1)S(1)}, u32[]{:S(2)}, u32[]{:S(2)}) collective-permute-start(bf16[2,240,384]{2,1,0:T(8,128)(2,1)} %pad_maximum_fusion.12), channel_id=1, source_target_pairs={{0,6},{1,7},{2,0},{3,1},{4,2},{5,3},{6,4},{7,5},{8,14},{9,15},{10,... | collective-permute-start | bytes 1105928 | tf_op jit(solution)/shard_map/ppermute | solution.py:476
  251.8 42.2 %collective-permute-start.42 = (bf16[2,240,384]{2,1,0:T(8,128)(2,1)}, bf16[2,240,384]{2,1,0:T(8,128)(2,1)}, u32[]{:S(2)}, u32[]{:S(2)}) collective-permute-start(bf16[2,240,384]{2,1,0:T(8,128)(2,1)} %pad_maximum_fusion.11), channel_id=1, source_target_pairs={{0,4},{1,5},{2,6},{3,7},{4,0},{5,1},{6,2},{7,3},{8,12},{9,13},{10,... | collective-permute-start | bytes 1105928 | tf_op jit(solution)/shard_map/ppermute | solution.py:476
  252.9 41.1 %collective-permute-start.41 = (bf16[2,240,384]{2,1,0:T(8,128)(2,1)}, bf16[2,240,384]{2,1,0:T(8,128)(2,1)}, u32[]{:S(2)}, u32[]{:S(2)}) collective-permute-start(bf16[2,240,384]{2,1,0:T(8,128)(2,1)} %pad_maximum_fusion.10), channel_id=1, source_target_pairs={{0,2},{1,3},{2,4},{3,5},{4,6},{5,7},{6,0},{7,1},{8,10},{9,11},{10,... | collective-permute-start | bytes 1105928 | tf_op jit(solution)/shard_map/ppermute | solution.py:476
  273.7 19.6 %collective-permute-start.35 = (bf16[4,96,384]{2,1,0:T(8,128)(2,1)}, bf16[4,96,384]{2,1,0:T(8,128)(2,1)S(1)}, u32[]{:S(2)}, u32[]{:S(2)}) collective-permute-start(bf16[4,96,384]{2,1,0:T(8,128)(2,1)} %get-tuple-element.256), channel_id=1, source_target_pairs={{0,16},{1,17},{2,18},{3,19},{4,20},{5,21},{6,22},{7,23},{8,24},{9,... | collective-permute-start | bytes 884744 | tf_op jit(solution)/shard_map/ppermute | solution.py:476
  274.7 18.7 %collective-permute-start.36 = (bf16[4,96,384]{2,1,0:T(8,128)(2,1)S(1)}, bf16[4,96,384]{2,1,0:T(8,128)(2,1)S(1)}, u32[]{:S(2)}, u32[]{:S(2)}) collective-permute-start(bf16[4,96,384]{2,1,0:T(8,128)(2,1)S(1)} %get-tuple-element.253), channel_id=1, source_target_pairs={{0,8},{1,9},{2,10},{3,11},{4,12},{5,13},{6,14},{7,15},{8,0},{9,1},... | collective-permute-start | bytes 884744 | tf_op jit(solution)/shard_map/ppermute | solution.py:476
  315.4 17.7 %collective-permute-start.49 = (bf16[2,160,384]{2,1,0:T(8,128)(2,1)S(1)}, bf16[2,160,384]{2,1,0:T(8,128)(2,1)S(1)}, u32[]{:S(2)}, u32[]{:S(2)}) collective-permute-start(bf16[2,160,384]{2,1,0:T(8,128)(2,1)S(1)} %pad_maximum_fusion.18), channel_id=1, source_target_pairs={{0,6},{1,7},{2,0},{3,1},{4,2},{5,3},{6,4},{7,5},{8,14},{9,15},{10,... | collective-permute-start | bytes 737288 | tf_op jit(solution)/shard_map/ppermute | solution.py:476
  318.0 21.0 %collective-permute-start.48 = (bf16[2,160,384]{2,1,0:T(8,128)(2,1)S(1)}, bf16[2,160,384]{2,1,0:T(8,128)(2,1)S(1)}, u32[]{:S(2)}, u32[]{:S(2)}) collective-permute-start(bf16[2,160,384]{2,1,0:T(8,128)(2,1)S(1)} %pad_maximum_fusion.17), channel_id=1, source_target_pairs={{0,4},{1,5},{2,6},{3,7},{4,0},{5,1},{6,2},{7,3},{8,12},{9,13},{10,... | collective-permute-start | bytes 737288 | tf_op jit(solution)/shard_map/ppermute | solution.py:476
  (73 other events, 672.9 us)
